TPU v7x, 32 devices: a whole 2x2x4 slice. The times are simulated.
32 devices in a mesh: parts: 1, ctx: 32 (over z, y, x, core).
Axes of the slice: x: 2, y: 2, z: 4, core: 2. Of those that a mesh axis runs over, the one named last changes fastest.
Arguments:
- query_rows: bfloat16 [8192, 512], P(('parts', 'ctx')), may hold values from -6 to 6
- key_rows: bfloat16 [8192, 512], P(('parts', 'ctx')), may hold values from -6 to 6
- value_rows: bfloat16 [8192, 512], P(('parts', 'ctx')), may hold values from -6 to 6
- grad_out: bfloat16 [8192, 512], P(('parts', 'ctx')), may hold values from -6 to 6
- stripe_lists: int32 [64, 16], P(('parts', 'ctx')), may hold values from 0 to 31, all different within a row
Outputs:
- grad_query: float32 [8192, 512], P(('parts', 'ctx'))
- grad_key: float32 [8192, 512], P(('parts', 'ctx'))
- grad_value: float32 [8192, 512], P(('parts', 'ctx'))
Inputs may be any that keep to these rules, and one draw needn't show every extreme that they name: `stripe_lists`: the 16 shards listed for one query block are distinct.
All inputs are finite; a program needn't handle non-finite values.
Results may differ from a plain program's by a relative error of at most 0.012.
Values may be sent and summed in bfloat16 or wider, within the bound.
No kernel may reach another device: no remote copies, remote signals or barrier semaphores. Data moves between devices by JAX's collectives and lax.ppermute only.
A program may use at most 64 MiB of HBM per device.

v0:
```python
import math

import jax
import jax.numpy as jnp
from jax import lax
from jax.sharding import PartitionSpec as P

HEADS = 8
HEAD_DIM = 64
BLOCK = 128
WIN = 2
STRIPE = 16
NCOL = 16


def extended_2(x, sides, width):
    for axis, dim in sides:
        count, length = (lax.axis_size(axis), x.shape[dim])
        up = [(i, (i + 1) % count) for i in range(count - 1)]
        down = [(j, i) for i, j in up]
        last = lax.slice_in_dim(x, length - width, length, axis=dim)
        initial = lax.slice_in_dim(x, 0, width, axis=dim)
        before = lax.ppermute(last, axis, up)
        after = lax.ppermute(initial, axis, down)
        x = jnp.concatenate([before, x, after], axis=dim)
    return x


def shifted(value, axis, steps):
    count = lax.axis_size(axis)
    initial, last = (max(0, -steps), min(count, count - steps))
    return lax.ppermute(value, axis, [(source, source + steps) for source in range(initial, last)])


def block_gradients(query_block, key_block, value_block, grad_block, key_valid):
    score_scale = HEAD_DIM ** (-0.5)
    query_three = query_block.reshape(-1, HEADS, HEAD_DIM)
    key_three = key_block.reshape(-1, HEADS, HEAD_DIM)
    value_three = value_block.reshape(-1, HEADS, HEAD_DIM)
    grad_three = grad_block.reshape(-1, HEADS, HEAD_DIM)
    scores = (
        jnp.einsum("qhd,khd->hqk", query_three, key_three, preferred_element_type=jnp.float32)
        * score_scale
    )
    scores = jnp.where(key_valid[None, None, :], scores, -jnp.inf)
    maxima = jnp.max(scores, axis=-1, keepdims=True)
    raised = jnp.exp(scores - maxima)
    weights = raised / jnp.sum(raised, axis=-1, keepdims=True)
    weights_low = weights.astype(jnp.bfloat16)
    attended = jnp.einsum(
        "hqk,khd->qhd", weights_low, value_three, preferred_element_type=jnp.float32
    )
    row_dot = jnp.transpose(jnp.sum(grad_three.astype(jnp.float32) * attended, axis=-1))
    grad_weights = jnp.einsum(
        "qhd,khd->hqk", grad_three, value_three, preferred_element_type=jnp.float32
    )
    grad_scores = (weights * (grad_weights - row_dot[:, :, None]) * score_scale).astype(
        jnp.bfloat16
    )
    grad_query = jnp.einsum(
        "hqk,khd->qhd", grad_scores, key_three, preferred_element_type=jnp.float32
    )
    grad_key = jnp.einsum(
        "hqk,qhd->khd", grad_scores, query_three, preferred_element_type=jnp.float32
    )
    grad_value = jnp.einsum(
        "hqk,qhd->khd", weights_low, grad_three, preferred_element_type=jnp.float32
    )
    features = query_block.shape[1]
    return (
        grad_query.reshape(-1, features),
        jnp.concatenate([grad_key.reshape(-1, features), grad_value.reshape(-1, features)], axis=1),
    )


def body(query_rows, key_rows, value_rows, grad_out, stripe_lists):
    tokens, features = query_rows.shape
    halo_rows = WIN * BLOCK
    window_rows = (2 * WIN + 1) * BLOCK
    query_blocks = tokens // BLOCK
    device_count = lax.axis_size("ctx")
    device_index = lax.axis_index("ctx")
    total_blocks = query_blocks * device_count
    paired = jnp.concatenate([key_rows, value_rows], axis=1)
    extended = extended_2(paired, (("ctx", 0),), halo_rows)
    stripes = lax.all_gather(paired[tokens - STRIPE :], "ctx", axis=0, tiled=True).reshape(
        device_count, STRIPE, 2 * features
    )
    group_size = math.gcd(query_blocks, max(1, 512 // BLOCK))

    def group_step(carry, group_id):
        local_sums, stripe_table = carry
        first_block = group_id * group_size
        block_ids = first_block + jnp.arange(group_size, dtype=jnp.int32)
        query_group = query_rows.reshape(group_size, BLOCK, features)
        grad_group = grad_out.reshape(group_size, BLOCK, features)
        windows = jax.vmap(
            lambda start_block: lax.dynamic_slice_in_dim(
                extended, start_block * BLOCK, window_rows, 0
            )
        )(block_ids)
        far_rows = stripes[stripe_lists].reshape(group_size, NCOL * STRIPE, 2 * features)
        key_value = jnp.concatenate([windows, far_rows], axis=1)
        global_ids = device_index * query_blocks + block_ids
        window_ids = global_ids[:, None] - WIN + jnp.arange(2 * WIN + 1, dtype=jnp.int32)[None, :]
        block_valid = (window_ids >= 0) & (window_ids < total_blocks)
        key_valid = jnp.concatenate(
            [jnp.repeat(block_valid, BLOCK, axis=1), jnp.ones((group_size, NCOL * STRIPE), bool)],
            axis=1,
        )
        grad_query, grad_pairs = jax.vmap(block_gradients)(
            query_group,
            key_value[:, :, :features],
            key_value[:, :, features:],
            grad_group,
            key_valid,
        )
        for member in range(group_size):
            start_row = (first_block + member) * BLOCK
            current = lax.dynamic_slice_in_dim(local_sums, start_row, window_rows, 0)
            local_sums = lax.dynamic_update_slice_in_dim(
                local_sums, current + grad_pairs[member, :window_rows], start_row, 0
            )
            stripe_table = stripe_table.at[stripe_lists[member]].add(
                grad_pairs[member, window_rows:].reshape(NCOL, STRIPE, 2 * features)
            )
        return ((local_sums, stripe_table), grad_query)

    init = (
        jnp.zeros((tokens + 2 * halo_rows, 2 * features), jnp.float32),
        jnp.zeros((device_count, STRIPE, 2 * features), jnp.float32),
    )
    (local_sums, stripe_table), query_parts = lax.scan(
        group_step, init, jnp.arange(query_blocks // group_size, dtype=jnp.int32)
    )
    stripe_sum = lax.psum_scatter(
        stripe_table.reshape(device_count * STRIPE, 2 * features),
        "ctx",
        scatter_dimension=0,
        tiled=True,
    )
    from_after = shifted(local_sums[:halo_rows], "ctx", -1)
    from_before = shifted(local_sums[tokens + halo_rows :], "ctx", 1)
    owned = local_sums[halo_rows : halo_rows + tokens]
    owned = owned.at[:halo_rows].add(from_before)
    owned = owned.at[tokens - halo_rows :].add(from_after)
    owned = owned.at[tokens - STRIPE :].add(stripe_sum)
    return (query_parts.reshape(tokens, features), owned[:, :features], owned[:, features:])


def solution(mesh):
    return jax.shard_map(
        body,
        mesh=mesh,
        in_specs=(
            P(("parts", "ctx"), None),
            P(("parts", "ctx"), None),
            P(("parts", "ctx"), None),
            P(("parts", "ctx"), None),
            P(("parts", "ctx"), None),
        ),
        out_specs=(P(("parts", "ctx"), None), P(("parts", "ctx"), None), P(("parts", "ctx"), None)),
        check_vma=False,
    )
```

profile of v0, /device:TPU:0, one launch (start us, length us, event | category | flops | bytes accessed | tf_op | source)
XLA Modules:
  0.0 267.3 jit_solution(17050153589210675958)
XLA Ops:
  11.2 3.8 %collective-permute-start = (bf16[256,1024]{1,0:T(8,128)(2,1)S(1)}, bf16[256,1024]{1,0:T(8,128)(2,1)}, u32[]{:S(2)}, u32[]{:S(2)}) collective-permute-start(bf16[256,1024]{1,0:T(8,128)(2,1)S(1)} %constant_dynamic-update-slice_fusion), channel_id=1, source_target_pairs={{0,1},{1,2},{2,3},{3,4},{4,5},{5,6},{6,7},{7,8},{8,9},{9,10},{10,1... | collective-permute-start | bytes 1572872 | tf_op jit(solution)/shard_map/ppermute | solution.py:23
  20.4 3.0 %while.12 = (s32[]{:T(128)}, bf16[768,1024]{1,0:T(8,128)(2,1)S(1)}, s32[2,2]{1,0:T(2,128)S(1)}, bf16[2,640,1024]{2,1,0:T(8,128)(2,1)}, s32[]{:T(128)}) while((s32[]{:T(128)}, bf16[768,1024]{1,0:T(8,128)(2,1)S(1)}, s32[2,2]{1,0:T(2,128)S(1)}, bf16[2,640,1024]{2,1,0:T(8,128)(2,1)}, s32[]{:T(128)}) %tuple.47), condition=%wide.while_cond.3, body=%wide.while_body.3.sunk | while | flops 2 | bytes 2621537 | solution.py:98
  23.4 45.5 %all-gather.2.cloned.1.call-done = bf16[512,1024]{1,0:T(8,128)(2,1)} async-done(((bf16[16,1024]{1,0:T(8,128)(2,1)}), bf16[512,1024]{1,0:T(8,128)(2,1)}) %all-gather.2.cloned.1.call-update) | async-done | bytes 1048592 | tf_op jit(solution)/shard_map/all_gather | solution.py:86
  68.9 1.8 gather_fusion
  70.7 2.8 %pad_maximum_fusion = (bf16[2,896,512]{2,1,0:T(8,128)(2,1)S(1)}, bf16[2,896,512]{2,1,0:T(8,128)(2,1)}) fusion(bf16[2,256,1024]{2,1,0:T(8,128)(2,1)S(1)} %bitcast.96, bf16[2,640,1024]{2,1,0:T(8,128)(2,1)} %get-tuple-element.92), kind=kLoop, calls=%fused_computation.33 | loop fusion | flops 7340032 | bytes 7340032 | tf_op jit(solution)/shard_map/while/body/eval_jaxpr/concatenate | solution.py:103
  73.5 3.5 %copy.18 = bf16[2,896,512]{1,2,0:T(8,128)(2,1)} copy(bf16[2,896,512]{2,1,0:T(8,128)(2,1)} %get-tuple-element.109) | data formatting | bytes 3670016 | tf_op jit(solution)/shard_map/while/body/eval_jaxpr/slice | solution.py:113
  77.0 2.4 copy.21
  79.4 7.3 %fusion.30 = (f32[2,8,128]{2,1,0:T(8,128)S(1)}, f32[2,8,128,896]{2,3,1,0:T(8,128)}) fusion(pred[2,896]{1,0:T(4,128)(4,1)S(1)} %concatenate.34, bf16[2,896,8,64]{1,3,2,0:T(8,128)(2,1)} %bitcast.88, bf16[2,128,8,64]{1,3,2,0:T(8,128)(2,1)S(1)} %copy.20), kind=kOutput, calls=%fused_computation.63 | convolution fusion | flops 242221952 | bytes 9447168 | tf_op jit(solution)/shard_map/while/body/eval_jaxpr/vmap()/sub | solution.py:47
  86.7 4.1 %fusion.10 = bf16[2,8,128,896]{2,3,1,0:T(8,128)(2,1)S(1)} fusion(f32[2,8,128,896]{2,3,1,0:T(8,128)} %get-tuple-element.115, f32[2,8,128]{2,1,0:T(8,128)S(1)} %get-tuple-element.114), kind=kLoop, calls=%fused_computation.26 | loop fusion | flops 3670016 | bytes 11018240 | tf_op jit(solution)/shard_map/while/body/eval_jaxpr/vmap()/convert_element_type | solution.py:49
  90.9 3.5 %fusion.32 = f32[2,8,896,64]{2,3,1,0:T(8,128)} fusion(bf16[2,8,128,896]{2,3,1,0:T(8,128)(2,1)S(1)} %fusion.10, bf16[2,128,8,64]{1,3,2,0:T(8,128)(2,1)S(1)} %copy.23), kind=kOutput, calls=%fused_computation.65 | convolution fusion | flops 234881024 | bytes 7602176 | tf_op jit(solution)/shard_map/while/body/eval_jaxpr/vmap(hqk,qhd->khd)/dot_general | solution.py:66
  95.2 1.9 fusion.2
  97.1 3.4 %fusion.31 = f32[2,8,896,64]{2,3,1,0:T(8,128)} fusion(bf16[2,8,128,896]{2,3,1,0:T(8,128)(2,1)S(1)} %fusion.2, bf16[2,128,8,64]{1,3,2,0:T(8,128)(2,1)S(1)} %copy.20), kind=kOutput, calls=%fused_computation.64 | convolution fusion | flops 234881024 | bytes 7602176 | tf_op jit(solution)/shard_map/while/body/eval_jaxpr/vmap(hqk,qhd->khd)/dot_general | solution.py:63
  100.5 4.6 %copy.32 = f32[2,896,512]{2,1,0:T(8,128)} copy(f32[2,896,512]{1,2,0:T(8,128)} %bitcast.87) | data formatting | bytes 7340032 | tf_op jit(solution)/shard_map/while/body/eval_jaxpr/vmap()/reshape | solution.py:72
  105.1 4.6 %copy.33 = f32[2,896,512]{2,1,0:T(8,128)} copy(f32[2,896,512]{1,2,0:T(8,128)} %bitcast.86) | data formatting | bytes 7340032 | tf_op jit(solution)/shard_map/while/body/eval_jaxpr/vmap()/reshape | solution.py:72
  109.8 2.7 %pad_maximum_fusion.2 = (f32[1,256,1024]{2,1,0:T(8,128)S(1)}, f32[1,256,1024]{2,1,0:T(8,128)}) fusion(f32[2,896,512]{2,1,0:T(8,128)} %copy.33, f32[2,896,512]{2,1,0:T(8,128)} %copy.32), kind=kLoop, calls=%fused_computation.40 | loop fusion | flops 524288 | bytes 9437184 | tf_op jit(solution)/shard_map/while/body/eval_jaxpr/vmap()/concatenate | solution.py:72
  112.7 2.6 scatter_fusion
  115.4 1.8 scatter_fusion.1
  118.6 2.0 fusion.12
  127.0 4.0 %collective-permute-start.2 = (f32[256,1024]{1,0:T(8,128)}, f32[256,1024]{1,0:T(8,128)}, u32[]{:S(2)}, u32[]{:S(2)}) collective-permute-start(f32[256,1024]{1,0:T(8,128)} %slice.136), channel_id=1, source_target_pairs={{0,1},{1,2},{2,3},{3,4},{4,5},{5,6},{6,7},{7,8},{8,9},{9,10},{10,1... | collective-permute-start | bytes 3145736 | tf_op jit(solution)/shard_map/ppermute | solution.py:32
  133.2 2.3 reshape.266
  135.5 2.8 %fusion.20 = f32[256,1024]{1,0:T(8,128)} fusion(f32[256,1024]{1,0:T(8,128)} %collective-permute-done.3, f32[256,1024]{1,0:T(8,128)} %collective-permute-done.2, f32[640,1024]{1,0:T(8,128)S(1)} %get-tuple-element.105), kind=kLoop, calls=%fused_computation.42 | loop fusion | flops 524288 | bytes 4194304 | tf_op jit(solution)/shard_map/add | solution.py:146
  138.3 118.4 %reduce-scatter.2.cloned.1.call-done = f32[16,1024]{1,0:T(8,128)} async-done(((f32[512,1024]{1,0:T(8,128)}), f32[16,1024]{1,0:T(8,128)}) %reduce-scatter.2.cloned.1.call-update) | async-done | bytes 65552 | tf_op jit(solution)/shard_map/reduce_scatter | solution.py:136
  256.7 1.5 fusion.23
  258.2 2.2 fusion.29
  (63 shorter events, 23.3 us)
Async XLA Ops:
  7.2 12.1 %copy-start.7 = (s32[2,16]{1,0:T(2,128)S(1)}, s32[2,16]{1,0:T(2,128)}, u32[]{:S(2)}) copy-start(s32[2,16]{1,0:T(2,128)} %param.19) | copy-start | bytes 388
  7.2 61.7 %all-gather.2.cloned.1.call-start = ((), (), s32[]{:S(2)}) async-start(), calls=%async_computation.1 | async-start | bytes 1081344 | tf_op jit(solution)/shard_map/all_gather | solution.py:86
  9.8 246.9 %reduce-scatter.2.cloned.1.call-start = ((), (), s32[]{:S(2)}) async-start(), calls=%async_computation.2 | async-start | bytes 2162688 | tf_op jit(solution)/shard_map/reduce_scatter | solution.py:136
  9.9 9.4 %collective-permute-start.1 = (bf16[256,1024]{1,0:T(8,128)(2,1)S(1)}, bf16[256,1024]{1,0:T(8,128)(2,1)S(1)}, u32[]{:S(2)}, u32[]{:S(2)}) collective-permute-start(bf16[256,1024]{1,0:T(8,128)(2,1)S(1)} %constant_dynamic-update-slice_fusion), channel_id=1, source_target_pairs={{1,0},{2,1},{3,2},{4,3},{5,4},{6,5},{7,6},{8,7},{9,8},{10,9},{11,1... | collective-permute-start | bytes 1572872 | tf_op jit(solution)/shard_map/ppermute | solution.py:24
  11.2 8.1 %collective-permute-start = (bf16[256,1024]{1,0:T(8,128)(2,1)S(1)}, bf16[256,1024]{1,0:T(8,128)(2,1)}, u32[]{:S(2)}, u32[]{:S(2)}) collective-permute-start(bf16[256,1024]{1,0:T(8,128)(2,1)S(1)} %constant_dynamic-update-slice_fusion), channel_id=1, source_target_pairs={{0,1},{1,2},{2,3},{3,4},{4,5},{5,6},{6,7},{7,8},{8,9},{9,10},{10,1... | collective-permute-start | bytes 1572872 | tf_op jit(solution)/shard_map/ppermute | solution.py:23
  86.7 8.5 %slice-start = ((s8[7340032]{0:T(1024)(128)(4,1)}), s8[4194304]{0:T(1024)(128)(4,1)S(1)}, s32[]{:S(2)}) async-start(s8[7340032]{0:T(1024)(128)(4,1)} %bitcast.92), calls=%async_computation.3 | async-start | bytes 8388608
  90.8 3.5 %copy-start.6 = (bf16[2,896,512]{1,2,0:T(8,128)(2,1)S(1)}, bf16[2,896,512]{1,2,0:T(8,128)(2,1)}, u32[]{:S(2)}) copy-start(bf16[2,896,512]{1,2,0:T(8,128)(2,1)} %copy.21) | copy-start | bytes 5505028
  90.8 4.3 %slice-start.1 = ((s8[7340032]{0:T(1024)(128)(4,1)}), s8[3145728]{0:T(1024)(128)(4,1)S(1)}, s32[]{:S(2)}) async-start(s8[7340032]{0:T(1024)(128)(4,1)} %bitcast.92), calls=%async_computation.4 | async-start | bytes 6291456
  97.1 3.5 %copy-start.3 = (bf16[2,8,128,896]{2,3,1,0:T(8,128)(2,1)}, bf16[2,8,128,896]{2,3,1,0:T(8,128)(2,1)S(1)}, u32[]{:S(2)}) copy-start(bf16[2,8,128,896]{2,3,1,0:T(8,128)(2,1)S(1)} %fusion.2) | copy-start | bytes 11010052
  117.2 1.4 copy-start.2
  118.6 2.8 %copy-start.1 = (f32[2,896,512]{2,1,0:T(8,128)S(1)}, f32[2,896,512]{2,1,0:T(8,128)}, u32[]{:S(2)}) copy-start(f32[2,896,512]{2,1,0:T(8,128)} %copy.33) | copy-start | bytes 11010052
  120.6 2.2 copy-start
  122.9 8.1 %copy-start.5 = (bf16[2,896,512]{1,2,0:T(8,128)(2,1)S(1)}, bf16[2,896,512]{1,2,0:T(8,128)(2,1)}, u32[]{:S(2)}) copy-start(bf16[2,896,512]{1,2,0:T(8,128)(2,1)} %copy.18) | copy-start | bytes 5505028
  123.4 7.6 %copy-start.4 = (bf16[2,8,128,896]{2,3,1,0:T(8,128)(2,1)S(1)}, bf16[2,8,128,896]{2,3,1,0:T(8,128)(2,1)}, u32[]{:S(2)}) copy-start(bf16[2,8,128,896]{2,3,1,0:T(8,128)(2,1)} %copy-done.3) | copy-start | bytes 11010052
  124.5 11.0 %collective-permute-start.3 = (f32[256,1024]{1,0:T(8,128)}, f32[256,1024]{1,0:T(8,128)}, u32[]{:S(2)}, u32[]{:S(2)}) collective-permute-start(f32[256,1024]{1,0:T(8,128)} %slice.137), channel_id=1, source_target_pairs={{1,0},{2,1},{3,2},{4,3},{5,4},{6,5},{7,6},{8,7},{9,8},{10,9},{11,1... | collective-permute-start | bytes 3145736 | tf_op jit(solution)/shard_map/ppermute | solution.py:32
  127.0 8.6 %collective-permute-start.2 = (f32[256,1024]{1,0:T(8,128)}, f32[256,1024]{1,0:T(8,128)}, u32[]{:S(2)}, u32[]{:S(2)}) collective-permute-start(f32[256,1024]{1,0:T(8,128)} %slice.136), channel_id=1, source_target_pairs={{0,1},{1,2},{2,3},{3,4},{4,5},{5,6},{6,7},{7,8},{8,9},{9,10},{10,1... | collective-permute-start | bytes 3145736 | tf_op jit(solution)/shard_map/ppermute | solution.py:32
Sparse Core Ops, SparseCore 0:
  11.4 57.4 all-gather.1
  118.7 137.9 reduce-scatter.1
where the time goes:
time: 268 us; the launch traced here: 267 us
  waiting for transfers between devices  164 us (61%)
  local copies, waits for them, and re-layouts  37.7 us (14%)
  other arithmetic  22.8 us (9%)
  matrix products  17.8 us (7%)
  between operations  14.3 us (5%)
  starting transfers between devices  10.6 us (4%)
    reduce_scatter x1, waiting for transfers between devices, body(): lax.psum_scatter(stripe_table.reshape(device_count * STRIPE, 2 * features...  118 us
    all_gather x1, waiting for transfers between devices, body(): lax.all_gather(paired[tokens - STRIPE:], 'ctx', axis=0, tiled=True)  45.5 us
    unnamed x25, local copies, waits for them, and re-layouts  7.84 us
    sub x1, matrix products, block_gradients(): raised = jnp.exp(scores - maxima)  7.28 us
    ppermute x2, starting transfers between devices, shifted(): lax.ppermute(value, axis, [(source, source + steps) for source in range(i...  5.44 us
  transfers between devices with their start and end apart: 6, of which 2 were waited for; matrix products, arithmetic and copies ran while one was open for 8% of the time, Pallas kernels for 0%

commit v1 on v0

v1 whole, which is shorter than its diff:
```python
import functools

import jax
import jax.numpy as jnp
from jax import lax
from jax.experimental import pallas as pl
from jax.experimental.pallas import tpu as pltpu
from jax.sharding import PartitionSpec as P

HEAD_DIM = 64
BLOCK = 128
WIN = 2
STRIPE = 16
NCOL = 16
LANES = 128
ROWS = 2 * BLOCK
EXT = 3 * ROWS
FAR = NCOL * STRIPE
SPAN = (2 * WIN + 1) * BLOCK
SCALE = HEAD_DIM**-0.5
NT = (((1,), (1,)), ((), ()))


def attention_kernel(
    slots, flags, biases, query, grad, own, mate, across, table_a, table_b,
    grad_query, grad_own, grad_mate, grad_across, table_keep, table_send,
    ext_k, ext_v, table, far_k, far_v, q_two, g_two, probs, scores, far_probs, far_scores,
    ext_sum, table_sum,
):
    half = table_a.shape[0]
    mate_at = pl.multiple_of(flags[0], ROWS)
    across_at = pl.multiple_of(flags[1], ROWS)
    for which, ext in ((0, ext_k), (1, ext_v)):
        ext[ROWS : 2 * ROWS] = own[which]
        ext[pl.ds(mate_at, ROWS)] = mate[which]
        ext[pl.ds(across_at, ROWS)] = across[which]
    table[:half] = table_a[...]
    table[half:] = table_b[...]
    for i in range(2):
        for j in range(NCOL):
            slot = slots[i, j]
            far_k[i, j * STRIPE : (j + 1) * STRIPE] = table[slot, 0]
            far_v[i, j * STRIPE : (j + 1) * STRIPE] = table[slot, 1]
    first = lax.broadcasted_iota(jnp.int32, (ROWS, LANES), 1) < HEAD_DIM
    q = query[...] * jnp.bfloat16(SCALE)
    g = grad[...]
    zero = jnp.zeros_like(q)
    q_two[:ROWS] = jnp.where(first, q, zero)
    q_two[ROWS:] = jnp.where(first, zero, q)
    g_two[:ROWS] = jnp.where(first, g, zero)
    g_two[ROWS:] = jnp.where(first, zero, g)

    @pl.when(pl.program_id(0) == 0)
    def _():
        probs[...] = jnp.zeros_like(probs)
        scores[...] = jnp.zeros_like(scores)

    for h in range(2):
        qh = q_two[h * ROWS : (h + 1) * ROWS]
        gh = g_two[h * ROWS : (h + 1) * ROWS]
        s_win = lax.dot_general(ext_k[...], qh, NT, preferred_element_type=jnp.float32)
        d_win = lax.dot_general(ext_v[...], gh, NT, preferred_element_type=jnp.float32)
        for i in range(2):
            rows = slice(i * BLOCK, i * BLOCK + SPAN)
            cols = slice(i * BLOCK, (i + 1) * BLOCK)
            qi, gi = qh[cols], gh[cols]
            s_far = lax.dot_general(far_k[i], qi, NT, preferred_element_type=jnp.float32)
            d_far = lax.dot_general(far_v[i], gi, NT, preferred_element_type=jnp.float32)
            edge = ROWS - i * BLOCK
            s = s_win[rows, cols]
            s = jnp.concatenate(
                [s[:edge] + biases[0], s[edge : edge + ROWS], s[edge + ROWS :] + biases[1]], axis=0
            )
            d = d_win[rows, cols]
            top = jnp.maximum(
                jnp.max(s, axis=0, keepdims=True), jnp.max(s_far, axis=0, keepdims=True)
            )
            u = jnp.exp(s - top)
            u_far = jnp.exp(s_far - top)
            total = jnp.sum(u, axis=0, keepdims=True) + jnp.sum(u_far, axis=0, keepdims=True)
            inv = 1.0 / total
            dot = jnp.sum(u * d, axis=0, keepdims=True) + jnp.sum(u_far * d_far, axis=0, keepdims=True)
            dot = dot * inv
            p = u * inv
            p_far = u_far * inv
            wide = slice(h * ROWS + i * BLOCK, h * ROWS + (i + 1) * BLOCK)
            narrow = slice(h * BLOCK, (h + 1) * BLOCK)
            probs[rows, wide] = p.astype(jnp.bfloat16)
            scores[rows, wide] = (p * (d - dot)).astype(jnp.bfloat16)
            far_probs[i, :, narrow] = p_far.astype(jnp.bfloat16)
            far_scores[i, :, narrow] = (p_far * (d_far - dot)).astype(jnp.bfloat16)

    table_sum[...] = jnp.zeros_like(table_sum)
    for which, left, left_far, right in (
        (0, scores, far_scores, q_two),
        (1, probs, far_probs, g_two),
    ):
        ext_sum[which] = jnp.dot(left[...], right[...], preferred_element_type=jnp.float32)
        for i in range(2):
            cols = slice(i * BLOCK, (i + 1) * BLOCK)
            both = jnp.concatenate(
                [right[i * BLOCK : (i + 1) * BLOCK], right[ROWS + i * BLOCK : ROWS + (i + 1) * BLOCK]],
                axis=0,
            )
            far = jnp.dot(left_far[i], both, preferred_element_type=jnp.float32)
            for j in range(NCOL):
                slot = slots[i, j]
                table_sum[slot, which] += far[j * STRIPE : (j + 1) * STRIPE]
        grad_own[which] = ext_sum[which, ROWS : 2 * ROWS]
        grad_mate[which] = ext_sum[which, pl.ds(mate_at, ROWS)].astype(grad_mate.dtype)
        grad_across[which] = ext_sum[which, pl.ds(across_at, ROWS)].astype(grad_across.dtype)
    table_keep[...] = table_sum[:half]
    table_send[...] = table_sum[half:].astype(table_send.dtype)

    k_t = jnp.transpose(ext_k[...])
    f_t = [jnp.transpose(far_k[i]) for i in range(2)]
    parts = []
    for h in range(2):
        feats = slice(h * HEAD_DIM, (h + 1) * HEAD_DIM)
        near = jnp.dot(
            k_t[feats], scores[:, h * ROWS : (h + 1) * ROWS], preferred_element_type=jnp.float32
        )
        far = [
            jnp.dot(
                f_t[i][feats],
                far_scores[i, :, h * BLOCK : (h + 1) * BLOCK],
                preferred_element_type=jnp.float32,
            )
            for i in range(2)
        ]
        parts.append(near + jnp.concatenate(far, axis=1))
    grad_query[...] = jnp.transpose(jnp.concatenate(parts, axis=0)) * SCALE


def attention(slots, flags, biases, query, grad, own, mate, across, table_a, table_b):
    half = table_a.shape[0]
    width = query.shape[1]
    steps = width // LANES
    rows = pl.BlockSpec((ROWS, LANES), lambda p: (0, p))
    pair = pl.BlockSpec((2, ROWS, LANES), lambda p: (0, 0, p))
    tab = pl.BlockSpec((half, 2, STRIPE, LANES), lambda p: (0, 0, 0, p))
    smem = pl.BlockSpec(memory_space=pltpu.SMEM)
    bf16, f32 = jnp.bfloat16, jnp.float32
    return pl.pallas_call(
        attention_kernel,
        grid=(steps,),
        in_specs=[smem, smem, smem, rows, rows, pair, pair, pair, tab, tab],
        out_specs=[rows, pair, pair, pair, tab, tab],
        out_shape=[
            jax.ShapeDtypeStruct((ROWS, width), f32),
            jax.ShapeDtypeStruct((2, ROWS, width), f32),
            jax.ShapeDtypeStruct((2, ROWS, width), bf16),
            jax.ShapeDtypeStruct((2, ROWS, width), bf16),
            jax.ShapeDtypeStruct((half, 2, STRIPE, width), f32),
            jax.ShapeDtypeStruct((half, 2, STRIPE, width), bf16),
        ],
        scratch_shapes=[
            pltpu.VMEM((EXT, LANES), bf16),
            pltpu.VMEM((EXT, LANES), bf16),
            pltpu.VMEM((2 * half, 2, STRIPE, LANES), bf16),
            pltpu.VMEM((2, FAR, LANES), bf16),
            pltpu.VMEM((2, FAR, LANES), bf16),
            pltpu.VMEM((2 * ROWS, LANES), bf16),
            pltpu.VMEM((2 * ROWS, LANES), bf16),
            pltpu.VMEM((EXT, 2 * ROWS), bf16),
            pltpu.VMEM((EXT, 2 * ROWS), bf16),
            pltpu.VMEM((2, FAR, 2 * BLOCK), bf16),
            pltpu.VMEM((2, FAR, 2 * BLOCK), bf16),
            pltpu.VMEM((2, EXT, LANES), f32),
            pltpu.VMEM((2 * half, 2, STRIPE, LANES), f32),
        ],
        compiler_params=pltpu.CompilerParams(vmem_limit_bytes=48 << 20),
        cost_estimate=pl.CostEstimate(flops=3_000_000_000, bytes_accessed=8 << 20, transcendentals=1 << 21),
    )(slots, flags, biases, query, grad, own, mate, across, table_a, table_b)


def stage_bits(count):
    if count == 32:
        return [8, 16, 2, 4, 1]
    bits = [1 << k for k in range(count.bit_length() - 1)]
    return bits[1:] + bits[:1]


def swapped(x, count, bit):
    return lax.ppermute(x, "ctx", [(i, i ^ bit) for i in range(count)])


def crossed(x, count):
    up = [(i, i + 1) for i in range(1, count - 1, 2)]
    return lax.ppermute(x, "ctx", up + [(j, i) for i, j in up])


def body(query_rows, key_rows, value_rows, grad_out, stripe_lists):
    count = lax.axis_size("ctx")
    me = lax.axis_index("ctx")
    bits = stage_bits(count)
    own = jnp.stack([key_rows, value_rows])
    across = crossed(own, count)
    mate = swapped(own, count, 1)
    gathered = own[None, :, ROWS - STRIPE :]
    for bit in bits[:-1]:
        gathered = jnp.concatenate([gathered, swapped(gathered, count, bit)], axis=0)
    other = swapped(gathered, count, bits[-1])

    relative = stripe_lists ^ me
    slots = jnp.zeros_like(relative)
    for place, bit in enumerate(bits):
        slots = slots | jnp.where((relative & bit) != 0, 1 << place, 0)
    odd = me % 2
    flags = jnp.stack([jnp.where(odd, 0, 2 * ROWS), jnp.where(odd, 2 * ROWS, 0)]).astype(jnp.int32)
    biases = jnp.stack(
        [jnp.where(me == 0, -jnp.inf, 0.0), jnp.where(me == count - 1, -jnp.inf, 0.0)]
    ).astype(jnp.float32)
    grad_query, grad_own, grad_mate, grad_across, keep, send = attention(
        slots, flags, biases, query_rows, grad_out, own, mate, across, gathered, other
    )
    from_across = crossed(grad_across, count)
    from_mate = swapped(grad_mate, count, 1)
    for bit in bits[::-1]:
        total = keep + swapped(send, count, bit).astype(jnp.float32)
        half = total.shape[0] // 2
        keep, send = total[:half], total[half:].astype(jnp.bfloat16)
    tail = jnp.pad(total[0], ((0, 0), (ROWS - STRIPE, 0), (0, 0)))
    owned = grad_own + from_mate.astype(jnp.float32) + from_across.astype(jnp.float32) + tail
    return grad_query, owned[0], owned[1]


def solution(mesh):
    spec = P(("parts", "ctx"), None)
    return jax.shard_map(
        body,
        mesh=mesh,
        in_specs=(spec,) * 5,
        out_specs=(spec,) * 3,
        check_vma=False,
    )
```

time: 268 us -> 82.4 us (0.31)
  the two profiles are of different devices: /device:TPU:0 before, /device:TPU:13 now
where the time goes in v1:
time: 82.4 us; the launch traced here: 82.1 us
  waiting for transfers between devices  42.6 us (52%)
  starting transfers between devices  21.3 us (26%)
  Pallas kernels  12.7 us (15%)
  other arithmetic  2.8 us (3%)
  local copies, waits for them, and re-layouts  1.77 us (2%)
  between operations  0.83 us (1%)
    ppermute x12, waiting for transfers between devices, swapped(): return lax.ppermute(x, 'ctx', [(i, i ^ bit) for i in range(count)])  31.4 us
    ppermute x12, starting transfers between devices, swapped(): return lax.ppermute(x, 'ctx', [(i, i ^ bit) for i in range(count)])  14 us
    pallas_call x1, Pallas kernels, attention(): pl.pallas_call(attention_kernel, grid=(steps,), in_specs=[smem, smem, sme...  12.7 us
    ppermute x2, waiting for transfers between devices, crossed(): return lax.ppermute(x, 'ctx', up + [(j, i) for i, j in up])  11.3 us
    ppermute x2, starting transfers between devices, crossed(): return lax.ppermute(x, 'ctx', up + [(j, i) for i, j in up])  7.36 us
  transfers between devices with their start and end apart: 14, of which 9 were waited for; matrix products, arithmetic and copies ran while one was open for 0% of the time, Pallas kernels for 0%

profile of v1, /device:TPU:13, one launch (start us, length us, event | category | flops | bytes accessed | tf_op | source)
XLA Modules:
  0.0 82.1 jit_solution(3861501088340697851)
XLA Ops:
  0.6 0.8 constant_dynamic-update-slice_fusion.4
  1.6 2.6 %collective-permute-done.2 = bf16[1,2,16,512]{3,2,1,0:T(8,128)(2,1)S(1)} collective-permute-done((bf16[1,2,16,512]{3,2,1,0:T(8,128)(2,1)S(1)}, bf16[1,2,16,512]{3,2,1,0:T(8,128)(2,1)S(1)}, u32[]{:S(2)}, u32[]{:S(2)}) %collective-permute-start.2) | collective-permute-done | bytes 32800 | tf_op jit(solution)/shard_map/ppermute | solution.py:185
  4.3 2.4 %collective-permute-start.3 = (bf16[2,2,16,512]{3,2,1,0:T(8,128)(2,1)S(1)}, bf16[2,2,16,512]{3,2,1,0:T(8,128)(2,1)S(1)}, u32[]{:S(2)}, u32[]{:S(2)}) collective-permute-start(bf16[2,2,16,512]{3,2,1,0:T(8,128)(2,1)S(1)} %pad_maximum_fusion.3), channel_id=1, source_target_pairs={{0,16},{1,17},{2,18},{3,19},{4,20},{5,21},{6,22},{7,23},{8,24},{9,... | collective-permute-start | bytes 196616 | tf_op jit(solution)/shard_map/ppermute | solution.py:185
  6.6 1.8 %collective-permute-done.3 = bf16[2,2,16,512]{3,2,1,0:T(8,128)(2,1)S(1)} collective-permute-done((bf16[2,2,16,512]{3,2,1,0:T(8,128)(2,1)S(1)}, bf16[2,2,16,512]{3,2,1,0:T(8,128)(2,1)S(1)}, u32[]{:S(2)}, u32[]{:S(2)}) %collective-permute-start.3) | collective-permute-done | bytes 65568 | tf_op jit(solution)/shard_map/ppermute | solution.py:185
  8.4 1.3 %collective-permute-start.4 = (bf16[4,2,16,512]{3,2,1,0:T(8,128)(2,1)S(1)}, bf16[4,2,16,512]{3,2,1,0:T(8,128)(2,1)S(1)}, u32[]{:S(2)}, u32[]{:S(2)}) collective-permute-start(bf16[4,2,16,512]{3,2,1,0:T(8,128)(2,1)S(1)} %pad_maximum_fusion.2), channel_id=1, source_target_pairs={{0,2},{1,3},{2,0},{3,1},{4,6},{5,7},{6,4},{7,5},{8,10},{9,11},{10,... | collective-permute-start | bytes 393224 | tf_op jit(solution)/shard_map/ppermute | solution.py:185
  9.8 5.2 %collective-permute-start.1 = (bf16[2,256,512]{2,1,0:T(8,128)(2,1)S(1)}, bf16[2,256,512]{2,1,0:T(8,128)(2,1)S(1)}, u32[]{:S(2)}, u32[]{:S(2)}) collective-permute-start(bf16[2,256,512]{2,1,0:T(8,128)(2,1)S(1)} %pad_maximum_fusion.own), channel_id=1, source_target_pairs={{1,2},{3,4},{5,6},{7,8},{9,10},{11,12},{13,14},{15,16},{17,18},{19... | collective-permute-start | bytes 1572872 | tf_op jit(solution)/shard_map/ppermute | solution.py:190
  15.5 12.5 %collective-permute-done.5 = bf16[8,2,16,512]{3,2,1,0:T(8,128)(2,1)S(1)} collective-permute-done((bf16[8,2,16,512]{3,2,1,0:T(8,128)(2,1)S(1)}, bf16[8,2,16,512]{3,2,1,0:T(8,128)(2,1)S(1)}, u32[]{:S(2)}, u32[]{:S(2)}) %collective-permute-start.5) | collective-permute-done | bytes 262176 | tf_op jit(solution)/shard_map/ppermute | solution.py:185
  28.0 1.6 %collective-permute-start.6 = (bf16[16,2,16,512]{3,2,1,0:T(8,128)(2,1)S(1)}, bf16[16,2,16,512]{3,2,1,0:T(8,128)(2,1)S(1)}, u32[]{:S(2)}, u32[]{:S(2)}) collective-permute-start(bf16[16,2,16,512]{3,2,1,0:T(8,128)(2,1)S(1)} %constant_dynamic-update-slice_fusion.table_a), channel_id=1, source_target_pairs={{0,1},{1,0},{2,3},{3,2},{4,5},{5,4},{6,7},{7,6},{8,9},{9,8},{10,11... | collective-permute-start | bytes 1572872 | tf_op jit(solution)/shard_map/ppermute | solution.py:185
  29.8 0.6 copy-done.4
  30.4 0.8 collective-permute-done.6.table_b
  31.2 12.7 %shard_map.76 = (f32[256,512]{1,0:T(8,128)}, f32[2,256,512]{2,1,0:T(8,128)S(1)}, bf16[2,256,512]{2,1,0:T(8,128)(2,1)S(1)}, bf16[2,256,512]{2,1,0:T(8,128)(2,1)S(...) custom-call(s32[2,16]{1,0:T(2,128)S(1)} %fusion.6.slots, s32[2]{0:T(128)S(1)} %pad_add_fusion.1.flags, ...), custom_call_target="tpu_custom_call" | custom-call | flops 3000000000 | bytes 8388608 | tf_op jit(solution)/shard_map/pallas_call | solution.py:144
  43.9 0.4 collective-permute-start.9
  44.3 1.5 %collective-permute-done.9 = bf16[16,2,16,512]{3,2,1,0:T(8,128)(2,1)S(1)} collective-permute-done((bf16[16,2,16,512]{3,2,1,0:T(8,128)(2,1)S(1)}, bf16[16,2,16,512]{3,2,1,0:T(8,128)(2,1)S(1)}, u32[]{:S(2)}, u32[]{:S(2)}) %collective-permute-start.9) | collective-permute-done | bytes 524320 | tf_op jit(solution)/shard_map/ppermute | solution.py:185
  45.8 1.4 %convert_add_fusion = f32[16,2,16,512]{3,2,1,0:T(8,128)S(1)} fusion(f32[16,2,16,512]{3,2,1,0:T(8,128)} %get-tuple-element.13, bf16[16,2,16,512]{3,2,1,0:T(8,128)(2,1)S(1)} %collective-permute-done.9), kind=kLoop, calls=%fused_computation.1 | loop fusion | flops 524288 | bytes 2621440 | tf_op jit(solution)/shard_map/add | solution.py:220
  47.6 7.3 %collective-permute-done.10 = bf16[8,2,16,512]{3,2,1,0:T(8,128)(2,1)S(1)} collective-permute-done((bf16[8,2,16,512]{3,2,1,0:T(8,128)(2,1)S(1)}, bf16[8,2,16,512]{3,2,1,0:T(8,128)(2,1)S(1)}, u32[]{:S(2)}, u32[]{:S(2)}) %collective-permute-start.10) | collective-permute-done | bytes 262176 | tf_op jit(solution)/shard_map/ppermute | solution.py:185
  55.0 1.0 %collective-permute-start.11 = (bf16[4,2,16,512]{3,2,1,0:T(8,128)(2,1)S(1)}, bf16[4,2,16,512]{3,2,1,0:T(8,128)(2,1)S(1)}, u32[]{:S(2)}, u32[]{:S(2)}) collective-permute-start(bf16[4,2,16,512]{3,2,1,0:T(8,128)(2,1)S(1)} %slice.83), channel_id=1, source_target_pairs={{0,2},{1,3},{2,0},{3,1},{4,6},{5,7},{6,4},{7,5},{8,10},{9,11},{10,... | collective-permute-start | bytes 393224 | tf_op jit(solution)/shard_map/ppermute | solution.py:185
  56.0 2.8 %collective-permute-done.11 = bf16[4,2,16,512]{3,2,1,0:T(8,128)(2,1)S(1)} collective-permute-done((bf16[4,2,16,512]{3,2,1,0:T(8,128)(2,1)S(1)}, bf16[4,2,16,512]{3,2,1,0:T(8,128)(2,1)S(1)}, u32[]{:S(2)}, u32[]{:S(2)}) %collective-permute-start.11) | collective-permute-done | bytes 131104 | tf_op jit(solution)/shard_map/ppermute | solution.py:185
  58.9 3.0 %collective-permute-start.12 = (bf16[2,2,16,512]{3,2,1,0:T(8,128)(2,1)S(1)}, bf16[2,2,16,512]{3,2,1,0:T(8,128)(2,1)S(1)}, u32[]{:S(2)}, u32[]{:S(2)}) collective-permute-start(bf16[2,2,16,512]{3,2,1,0:T(8,128)(2,1)S(1)} %slice.84), channel_id=1, source_target_pairs={{0,16},{1,17},{2,18},{3,19},{4,20},{5,21},{6,22},{7,23},{8,24},{9,... | collective-permute-start | bytes 196616 | tf_op jit(solution)/shard_map/ppermute | solution.py:185
  61.9 2.6 %collective-permute-start.7 = (bf16[2,256,512]{2,1,0:T(8,128)(2,1)S(1)}, bf16[2,256,512]{2,1,0:T(8,128)(2,1)S(1)}, u32[]{:S(2)}, u32[]{:S(2)}) collective-permute-start(bf16[2,256,512]{2,1,0:T(8,128)(2,1)S(1)} %get-tuple-element.11), channel_id=1, source_target_pairs={{0,1},{1,0},{2,3},{3,2},{4,5},{5,4},{6,7},{7,6},{8,9},{9,8},{10,11... | collective-permute-start | bytes 1572872 | tf_op jit(solution)/shard_map/ppermute | solution.py:185
  64.5 2.1 %collective-permute-start.8 = (bf16[2,256,512]{2,1,0:T(8,128)(2,1)S(1)}, bf16[2,256,512]{2,1,0:T(8,128)(2,1)S(1)}, u32[]{:S(2)}, u32[]{:S(2)}) collective-permute-start(bf16[2,256,512]{2,1,0:T(8,128)(2,1)S(1)} %get-tuple-element.12), channel_id=1, source_target_pairs={{1,2},{3,4},{5,6},{7,8},{9,10},{11,12},{13,14},{15,16},{17,18},{19... | collective-permute-start | bytes 1572872 | tf_op jit(solution)/shard_map/ppermute | solution.py:190
  66.7 0.8 collective-permute-start.13
  67.5 2.0 %collective-permute-done.13 = bf16[1,2,16,512]{3,2,1,0:T(8,128)(2,1)S(1)} collective-permute-done((bf16[1,2,16,512]{3,2,1,0:T(8,128)(2,1)S(1)}, bf16[1,2,16,512]{3,2,1,0:T(8,128)(2,1)S(1)}, u32[]{:S(2)}, u32[]{:S(2)}) %collective-permute-start.13) | collective-permute-done | bytes 32800 | tf_op jit(solution)/shard_map/ppermute | solution.py:185
  69.6 11.3 %collective-permute-done.8 = bf16[2,256,512]{2,1,0:T(8,128)(2,1)S(1)} collective-permute-done((bf16[2,256,512]{2,1,0:T(8,128)(2,1)S(1)}, bf16[2,256,512]{2,1,0:T(8,128)(2,1)S(1)}, u32[]{:S(2)}, u32[]{:S(2)}) %collective-permute-start.8) | collective-permute-done | bytes 524320 | tf_op jit(solution)/shard_map/ppermute | solution.py:190
  81.1 1.0 %slice_bitcast_fusion = (f32[256,512]{1,0:T(8,128)}, f32[256,512]{1,0:T(8,128)}) fusion(f32[2,256,512]{2,1,0:T(8,128)S(1)} %pad_add_fusion), kind=kLoop, calls=%fused_computation.5 | loop fusion | bytes 2097152 | tf_op jit(solution)/shard_map/squeeze | solution.py:225
  (38 shorter events, 1.6 us)
Async XLA Ops:
  0.6 9.1 %copy-start.3 = (bf16[256,512]{1,0:T(8,128)(2,1)S(1)}, bf16[256,512]{1,0:T(8,128)(2,1)}, u32[]{:S(2)}) copy-start(bf16[256,512]{1,0:T(8,128)(2,1)} %param.6) | copy-start | bytes 786436
  1.4 8.3 %copy-start.2 = (bf16[256,512]{1,0:T(8,128)(2,1)S(1)}, bf16[256,512]{1,0:T(8,128)(2,1)}, u32[]{:S(2)}) copy-start(bf16[256,512]{1,0:T(8,128)(2,1)} %param.7) | copy-start | bytes 786436
  1.4 2.8 %collective-permute-start.2 = (bf16[1,2,16,512]{3,2,1,0:T(8,128)(2,1)S(1)}, bf16[1,2,16,512]{3,2,1,0:T(8,128)(2,1)S(1)}, u32[]{:S(2)}, u32[]{:S(2)}) collective-permute-start(bf16[1,2,16,512]{3,2,1,0:T(8,128)(2,1)S(1)} %get-tuple-element.16), channel_id=1, source_target_pairs={{0,8},{1,9},{2,10},{3,11},{4,12},{5,13},{6,14},{7,15},{8,0},{9,1},... | collective-permute-start | bytes 98312 | tf_op jit(solution)/shard_map/ppermute | solution.py:185
  4.3 4.2 %collective-permute-start.3 = (bf16[2,2,16,512]{3,2,1,0:T(8,128)(2,1)S(1)}, bf16[2,2,16,512]{3,2,1,0:T(8,128)(2,1)S(1)}, u32[]{:S(2)}, u32[]{:S(2)}) collective-permute-start(bf16[2,2,16,512]{3,2,1,0:T(8,128)(2,1)S(1)} %pad_maximum_fusion.3), channel_id=1, source_target_pairs={{0,16},{1,17},{2,18},{3,19},{4,20},{5,21},{6,22},{7,23},{8,24},{9,... | collective-permute-start | bytes 196616 | tf_op jit(solution)/shard_map/ppermute | solution.py:185
  8.4 6.6 %collective-permute-start.4 = (bf16[4,2,16,512]{3,2,1,0:T(8,128)(2,1)S(1)}, bf16[4,2,16,512]{3,2,1,0:T(8,128)(2,1)S(1)}, u32[]{:S(2)}, u32[]{:S(2)}) collective-permute-start(bf16[4,2,16,512]{3,2,1,0:T(8,128)(2,1)S(1)} %pad_maximum_fusion.2), channel_id=1, source_target_pairs={{0,2},{1,3},{2,0},{3,1},{4,6},{5,7},{6,4},{7,5},{8,10},{9,11},{10,... | collective-permute-start | bytes 393224 | tf_op jit(solution)/shard_map/ppermute | solution.py:185
  9.8 20.6 %collective-permute-start.1 = (bf16[2,256,512]{2,1,0:T(8,128)(2,1)S(1)}, bf16[2,256,512]{2,1,0:T(8,128)(2,1)S(1)}, u32[]{:S(2)}, u32[]{:S(2)}) collective-permute-start(bf16[2,256,512]{2,1,0:T(8,128)(2,1)S(1)} %pad_maximum_fusion.own), channel_id=1, source_target_pairs={{1,2},{3,4},{5,6},{7,8},{9,10},{11,12},{13,14},{15,16},{17,18},{19... | collective-permute-start | bytes 1572872 | tf_op jit(solution)/shard_map/ppermute | solution.py:190
  15.0 15.4 %collective-permute-start = (bf16[2,256,512]{2,1,0:T(8,128)(2,1)S(1)}, bf16[2,256,512]{2,1,0:T(8,128)(2,1)S(1)}, u32[]{:S(2)}, u32[]{:S(2)}) collective-permute-start(bf16[2,256,512]{2,1,0:T(8,128)(2,1)S(1)} %pad_maximum_fusion.own), channel_id=1, source_target_pairs={{0,1},{1,0},{2,3},{3,2},{4,5},{5,4},{6,7},{7,6},{8,9},{9,8},{10,11... | collective-permute-start | bytes 1572872 | tf_op jit(solution)/shard_map/ppermute | solution.py:185
  15.1 12.8 %collective-permute-start.5 = (bf16[8,2,16,512]{3,2,1,0:T(8,128)(2,1)S(1)}, bf16[8,2,16,512]{3,2,1,0:T(8,128)(2,1)S(1)}, u32[]{:S(2)}, u32[]{:S(2)}) collective-permute-start(bf16[8,2,16,512]{3,2,1,0:T(8,128)(2,1)S(1)} %pad_maximum_fusion.1), channel_id=1, source_target_pairs={{0,4},{1,5},{2,6},{3,7},{4,0},{5,1},{6,2},{7,3},{8,12},{9,13},{10,... | collective-permute-start | bytes 786440 | tf_op jit(solution)/shard_map/ppermute | solution.py:185
  15.5 15.7 %copy-start = (bf16[256,512]{1,0:T(8,128)(2,1)S(1)}, bf16[256,512]{1,0:T(8,128)(2,1)}, u32[]{:S(2)}) copy-start(bf16[256,512]{1,0:T(8,128)(2,1)} %query.1) | copy-start | bytes 786436
  15.5 15.7 %copy-start.1 = (bf16[256,512]{1,0:T(8,128)(2,1)S(1)}, bf16[256,512]{1,0:T(8,128)(2,1)}, u32[]{:S(2)}) copy-start(bf16[256,512]{1,0:T(8,128)(2,1)} %grad.1) | copy-start | bytes 786436
  28.0 3.2 %collective-permute-start.6 = (bf16[16,2,16,512]{3,2,1,0:T(8,128)(2,1)S(1)}, bf16[16,2,16,512]{3,2,1,0:T(8,128)(2,1)S(1)}, u32[]{:S(2)}, u32[]{:S(2)}) collective-permute-start(bf16[16,2,16,512]{3,2,1,0:T(8,128)(2,1)S(1)} %constant_dynamic-update-slice_fusion.table_a), channel_id=1, source_target_pairs={{0,1},{1,0},{2,3},{3,2},{4,5},{5,4},{6,7},{7,6},{8,9},{9,8},{10,11... | collective-permute-start | bytes 1572872 | tf_op jit(solution)/shard_map/ppermute | solution.py:185
  29.7 0.7 copy-start.4
  43.9 1.9 %collective-permute-start.9 = (bf16[16,2,16,512]{3,2,1,0:T(8,128)(2,1)S(1)}, bf16[16,2,16,512]{3,2,1,0:T(8,128)(2,1)S(1)}, u32[]{:S(2)}, u32[]{:S(2)}) collective-permute-start(bf16[16,2,16,512]{3,2,1,0:T(8,128)(2,1)S(1)} %get-tuple-element.14), channel_id=1, source_target_pairs={{0,1},{1,0},{2,3},{3,2},{4,5},{5,4},{6,7},{7,6},{8,9},{9,8},{10,11... | collective-permute-start | bytes 1572872 | tf_op jit(solution)/shard_map/ppermute | solution.py:185
  47.3 7.6 %collective-permute-start.10 = (bf16[8,2,16,512]{3,2,1,0:T(8,128)(2,1)S(1)}, bf16[8,2,16,512]{3,2,1,0:T(8,128)(2,1)S(1)}, u32[]{:S(2)}, u32[]{:S(2)}) collective-permute-start(bf16[8,2,16,512]{3,2,1,0:T(8,128)(2,1)S(1)} %slice.82), channel_id=1, source_target_pairs={{0,4},{1,5},{2,6},{3,7},{4,0},{5,1},{6,2},{7,3},{8,12},{9,13},{10,... | collective-permute-start | bytes 786440 | tf_op jit(solution)/shard_map/ppermute | solution.py:185
  55.0 3.9 %collective-permute-start.11 = (bf16[4,2,16,512]{3,2,1,0:T(8,128)(2,1)S(1)}, bf16[4,2,16,512]{3,2,1,0:T(8,128)(2,1)S(1)}, u32[]{:S(2)}, u32[]{:S(2)}) collective-permute-start(bf16[4,2,16,512]{3,2,1,0:T(8,128)(2,1)S(1)} %slice.83), channel_id=1, source_target_pairs={{0,2},{1,3},{2,0},{3,1},{4,6},{5,7},{6,4},{7,5},{8,10},{9,11},{10,... | collective-permute-start | bytes 393224 | tf_op jit(solution)/shard_map/ppermute | solution.py:185
  58.9 7.8 %collective-permute-start.12 = (bf16[2,2,16,512]{3,2,1,0:T(8,128)(2,1)S(1)}, bf16[2,2,16,512]{3,2,1,0:T(8,128)(2,1)S(1)}, u32[]{:S(2)}, u32[]{:S(2)}) collective-permute-start(bf16[2,2,16,512]{3,2,1,0:T(8,128)(2,1)S(1)} %slice.84), channel_id=1, source_target_pairs={{0,16},{1,17},{2,18},{3,19},{4,20},{5,21},{6,22},{7,23},{8,24},{9,... | collective-permute-start | bytes 196616 | tf_op jit(solution)/shard_map/ppermute | solution.py:185
  61.9 7.7 %collective-permute-start.7 = (bf16[2,256,512]{2,1,0:T(8,128)(2,1)S(1)}, bf16[2,256,512]{2,1,0:T(8,128)(2,1)S(1)}, u32[]{:S(2)}, u32[]{:S(2)}) collective-permute-start(bf16[2,256,512]{2,1,0:T(8,128)(2,1)S(1)} %get-tuple-element.11), channel_id=1, source_target_pairs={{0,1},{1,0},{2,3},{3,2},{4,5},{5,4},{6,7},{7,6},{8,9},{9,8},{10,11... | collective-permute-start | bytes 1572872 | tf_op jit(solution)/shard_map/ppermute | solution.py:185
  64.5 16.3 %collective-permute-start.8 = (bf16[2,256,512]{2,1,0:T(8,128)(2,1)S(1)}, bf16[2,256,512]{2,1,0:T(8,128)(2,1)S(1)}, u32[]{:S(2)}, u32[]{:S(2)}) collective-permute-start(bf16[2,256,512]{2,1,0:T(8,128)(2,1)S(1)} %get-tuple-element.12), channel_id=1, source_target_pairs={{1,2},{3,4},{5,6},{7,8},{9,10},{11,12},{13,14},{15,16},{17,18},{19... | collective-permute-start | bytes 1572872 | tf_op jit(solution)/shard_map/ppermute | solution.py:190
  66.7 2.8 %collective-permute-start.13 = (bf16[1,2,16,512]{3,2,1,0:T(8,128)(2,1)S(1)}, bf16[1,2,16,512]{3,2,1,0:T(8,128)(2,1)S(1)}, u32[]{:S(2)}, u32[]{:S(2)}) collective-permute-start(bf16[1,2,16,512]{3,2,1,0:T(8,128)(2,1)S(1)} %slice.85), channel_id=1, source_target_pairs={{0,8},{1,9},{2,10},{3,11},{4,12},{5,13},{6,14},{7,15},{8,0},{9,1},... | collective-permute-start | bytes 98312 | tf_op jit(solution)/shard_map/ppermute | solution.py:185

commit v2 on v1

v2 whole, which is shorter than its diff:
```python
import jax
import jax.numpy as jnp
from jax import lax
from jax.experimental import pallas as pl
from jax.experimental.pallas import tpu as pltpu
from jax.sharding import PartitionSpec as P

HEAD_DIM = 64
BLOCK = 128
WIN = 2
STRIPE = 16
NCOL = 16
LANES = 128
ROWS = WIN * BLOCK
EXT = 3 * ROWS
FAR = NCOL * STRIPE
SPAN = (2 * WIN + 1) * BLOCK
SCALE = HEAD_DIM**-0.5
NT = (((1,), (1,)), ((), ()))
BF16, F32 = jnp.bfloat16, jnp.float32


def tile(h, i):
    return slice((2 * h + i) * BLOCK, (2 * h + i + 1) * BLOCK)


def block_rows(i, flip):
    return pl.ds(pl.multiple_of((i ^ flip) * BLOCK, BLOCK), BLOCK)


def split_heads(ref, which, flip, two):
    first = lax.broadcasted_iota(jnp.int32, (BLOCK, LANES), 1) < HEAD_DIM
    for i in range(2):
        x = ref[which, block_rows(i, flip)]
        zero = jnp.zeros_like(x)
        two[tile(0, i)] = jnp.where(first, x, zero)
        two[tile(1, i)] = jnp.where(first, zero, x)


def fill_window(flip, mate, own, which, across, ext):
    for i in range(2):
        rows = block_rows(i, flip)
        ext[tile(0, i)] = mate[rows]
        ext[tile(1, i)] = own[which, rows]
        ext[tile(2, i)] = across[rows]


def column_max(x):
    return jnp.max(x, axis=0, keepdims=True)


def column_sum(x):
    return jnp.sum(x, axis=0, keepdims=True)


def near_rows(i):
    return slice(i * BLOCK, i * BLOCK + SPAN)


def window_kernel(
    flags, biases, pair, own, mate_k, across_k, mate_v, across_v,
    near_s, near_d, stats,
    ext_k, ext_v, q_two, g_two,
):
    flip = flags[0]
    fill_window(flip, mate_k, own, 0, across_k, ext_k)
    fill_window(flip, mate_v, own, 1, across_v, ext_v)
    split_heads(pair, 0, flip, q_two)
    split_heads(pair, 1, flip, g_two)
    for h in range(2):
        heads = slice(h * ROWS, (h + 1) * ROWS)
        s = lax.dot_general(ext_k[...], q_two[heads], NT, preferred_element_type=F32)
        near_s[0, : 2 * ROWS, heads] = s[: 2 * ROWS]
        near_s[0, 2 * ROWS :, heads] = s[2 * ROWS :] + biases[0]
        near_d[0, :, heads] = lax.dot_general(
            ext_v[...], g_two[heads], NT, preferred_element_type=F32
        )
    for h in range(2):
        for i in range(2):
            s = near_s[0, near_rows(i), tile(h, i)]
            d = near_d[0, near_rows(i), tile(h, i)]
            top = column_max(s)
            u = jnp.exp(s - top)
            stats[0, 0:1, tile(h, i)] = top
            stats[0, 1:2, tile(h, i)] = column_sum(u)
            stats[0, 2:3, tile(h, i)] = column_sum(u * d)


def stripe_kernel(
    flags, slots, pair, stats, table_a, table_b, coefs, far_query, table_keep, table_send,
    table, far_k, far_v, q_two, g_two, far_probs, far_scores, table_sum,
):
    flip = flags[0]
    half = table_a.shape[0]
    table[:half] = table_a[...]
    table[half:] = table_b[...]
    for i in range(2):
        for j in range(NCOL):
            slot = slots[i ^ flip, j]
            far_k[i, j * STRIPE : (j + 1) * STRIPE] = table[slot, 0]
            far_v[i, j * STRIPE : (j + 1) * STRIPE] = table[slot, 1]
    split_heads(pair, 0, flip, q_two)
    split_heads(pair, 1, flip, g_two)
    tiles = [(h, i) for h in range(2) for i in range(2)]
    s = jnp.concatenate(
        [
            lax.dot_general(far_k[i], q_two[tile(h, i)], NT, preferred_element_type=F32)
            for h, i in tiles
        ],
        axis=1,
    )
    d = jnp.concatenate(
        [
            lax.dot_general(far_v[i], g_two[tile(h, i)], NT, preferred_element_type=F32)
            for h, i in tiles
        ],
        axis=1,
    )
    near_top = stats[0, 0:1]
    top = jnp.maximum(near_top, column_max(s))
    shrink = jnp.exp(near_top - top)
    u = jnp.exp(s - top)
    total = stats[0, 1:2] * shrink + column_sum(u)
    inv = 1.0 / total
    dot = (stats[0, 2:3] * shrink + column_sum(u * d)) * inv
    coefs[0, 0:1] = top + jnp.log(total)
    coefs[0, 1:2] = dot
    p = u * inv
    far_probs[...] = p.astype(BF16)
    far_scores[...] = (p * (d - dot)).astype(BF16)
    table_sum[...] = jnp.zeros_like(table_sum)
    for which, left, right in ((0, far_scores, q_two), (1, far_probs, g_two)):
        for i in range(2):
            far = jnp.dot(
                jnp.concatenate([left[:, tile(0, i)], left[:, tile(1, i)]], axis=1),
                jnp.concatenate([right[tile(0, i)], right[tile(1, i)]], axis=0),
                preferred_element_type=F32,
            )
            for j in range(NCOL):
                slot = slots[i ^ flip, j]
                table_sum[slot, which] += far[j * STRIPE : (j + 1) * STRIPE]
    table_keep[...] = table_sum[:half]
    table_send[...] = table_sum[half:].astype(table_send.dtype)
    for i in range(2):
        k_t = jnp.transpose(far_k[i])
        for h in range(2):
            feats = slice(h * HEAD_DIM, (h + 1) * HEAD_DIM)
            far_query[0, feats, i * BLOCK : (i + 1) * BLOCK] = jnp.dot(
                k_t[feats], far_scores[:, tile(h, i)], preferred_element_type=F32
            )


def gradient_kernel(
    flags, pair, own, mate_k, across_k, near_s, near_d, coefs, far_query,
    grad_query, grad_key, grad_value, grad_mate, grad_across,
    ext_k, q_two, g_two, probs, scores,
):
    flip = flags[0]
    fill_window(flip, mate_k, own, 0, across_k, ext_k)
    split_heads(pair, 0, flip, q_two)
    split_heads(pair, 1, flip, g_two)

    for h in range(2):
        for i in range(2):
            idle = slice((1 - i) * SPAN, (1 - i) * SPAN + BLOCK)
            probs[idle, tile(h, i)] = jnp.zeros((BLOCK, BLOCK), BF16)
            scores[idle, tile(h, i)] = jnp.zeros((BLOCK, BLOCK), BF16)

    for h in range(2):
        for i in range(2):
            rows = near_rows(i)
            p = jnp.exp(near_s[0, rows, tile(h, i)] - coefs[0, 0:1, tile(h, i)])
            probs[rows, tile(h, i)] = p.astype(BF16)
            ds = p * (near_d[0, rows, tile(h, i)] - coefs[0, 1:2, tile(h, i)])
            scores[rows, tile(h, i)] = ds.astype(BF16)
    for which, left, right, grad_own in (
        (0, scores, q_two, grad_key),
        (1, probs, g_two, grad_value),
    ):
        total = jnp.dot(left[...], right[...], preferred_element_type=F32)
        for i in range(2):
            rows = block_rows(i, flip)
            grad_mate[which, rows] = total[tile(0, i)].astype(grad_mate.dtype)
            grad_own[rows] = total[tile(1, i)]
            grad_across[which, rows] = total[tile(2, i)].astype(grad_across.dtype)
    k_t = jnp.transpose(ext_k[...])
    near = [
        jnp.dot(
            k_t[h * HEAD_DIM : (h + 1) * HEAD_DIM],
            scores[:, h * ROWS : (h + 1) * ROWS],
            preferred_element_type=F32,
        )
        for h in range(2)
    ]
    out = jnp.transpose(jnp.concatenate(near, axis=0) + far_query[0]) * SCALE
    for i in range(2):
        grad_query[block_rows(i, flip)] = out[i * BLOCK : (i + 1) * BLOCK]


SMEM_SPEC = pl.BlockSpec(memory_space=pltpu.SMEM)
VMEM_SPEC = pl.BlockSpec(memory_space=pltpu.VMEM)
TWO = pltpu.VMEM((2 * ROWS, LANES), BF16)
EXTENT = pltpu.VMEM((EXT, LANES), BF16)
FULL, ROW, PAIR, TABLE, STEP = "full", "row", "pair", "table", "step"


def view(ref, kind, p):
    lanes = pl.ds(p * LANES, LANES)
    if kind == ROW:
        return ref.at[:, lanes]
    if kind == PAIR:
        return ref.at[:, :, lanes]
    if kind == TABLE:
        return ref.at[:, :, :, lanes]
    if kind == STEP:
        return ref.at[pl.ds(p, 1)]
    return ref


def call(kernel, steps, in_kinds, out_kinds, out_shape, scratch, flops, moved, args):
    kinds = in_kinds + out_kinds

    def whole(*refs):
        for p in range(steps):
            views = [view(ref, kind, p) for ref, kind in zip(refs, kinds)]
            kernel(*views, *refs[len(kinds) :])

    return pl.pallas_call(
        whole,
        in_specs=[SMEM_SPEC if kind == FULL else VMEM_SPEC for kind in in_kinds],
        out_specs=[VMEM_SPEC] * len(out_kinds),
        out_shape=[jax.ShapeDtypeStruct(shape, dtype) for shape, dtype in out_shape],
        scratch_shapes=scratch,
        compiler_params=pltpu.CompilerParams(vmem_limit_bytes=24 << 20),
        cost_estimate=pl.CostEstimate(flops=flops, bytes_accessed=moved, transcendentals=1 << 20),
    )(*args)


def window_part(flags, biases, pair, own, mate_k, across_k, mate_v, across_v):
    steps = pair.shape[2] // LANES
    near = ((steps, EXT, 2 * ROWS), F32)
    return call(
        window_kernel,
        steps,
        [FULL, FULL, PAIR, PAIR, ROW, ROW, ROW, ROW],
        [STEP, STEP, STEP],
        [near, near, ((steps, 8, 2 * ROWS), F32)],
        [EXTENT, EXTENT, TWO, TWO],
        1 << 34,
        12 << 20,
        (flags, biases, pair, own, mate_k, across_k, mate_v, across_v),
    )


def stripe_part(flags, slots, pair, stats, table_a, table_b):
    half = table_a.shape[0]
    width = pair.shape[2]
    steps = width // LANES
    return call(
        stripe_kernel,
        steps,
        [FULL, FULL, PAIR, STEP, TABLE, TABLE],
        [STEP, STEP, TABLE, TABLE],
        [
            ((steps, 8, 2 * ROWS), F32),
            ((steps, LANES, ROWS), F32),
            ((half, 2, STRIPE, width), F32),
            ((half, 2, STRIPE, width), BF16),
        ],
        [
            pltpu.VMEM((2 * half, 2, STRIPE, LANES), BF16),
            pltpu.VMEM((2, FAR, LANES), BF16),
            pltpu.VMEM((2, FAR, LANES), BF16),
            TWO,
            TWO,
            pltpu.VMEM((FAR, 4 * BLOCK), BF16),
            pltpu.VMEM((FAR, 4 * BLOCK), BF16),
            pltpu.VMEM((2 * half, 2, STRIPE, LANES), F32),
        ],
        1 << 30,
        4 << 20,
        (flags, slots, pair, stats, table_a, table_b),
    )


def gradient_part(flags, pair, own, mate_k, across_k, near_s, near_d, coefs, far_query):
    width = pair.shape[2]
    steps = width // LANES
    return call(
        gradient_kernel,
        steps,
        [FULL, PAIR, PAIR, ROW, ROW, STEP, STEP, STEP, STEP],
        [ROW, ROW, ROW, PAIR, PAIR],
        [((ROWS, width), F32)] * 3 + [((2, ROWS, width), BF16)] * 2,
        [
            EXTENT,
            TWO,
            TWO,
            pltpu.VMEM((EXT, 2 * ROWS), BF16),
            pltpu.VMEM((EXT, 2 * ROWS), BF16),
        ],
        1 << 34,
        14 << 20,
        (flags, pair, own, mate_k, across_k, near_s, near_d, coefs, far_query),
    )


def stage_bits(count):
    if count == 32:
        return [8, 16, 4, 2, 1]
    bits = [1 << k for k in range(count.bit_length() - 1)]
    return bits[1:] + bits[:1]


def swapped(x, count, bit):
    return lax.ppermute(x, "ctx", [(i, i ^ bit) for i in range(count)])


def crossed(x, count):
    up = [(i, i + 1) for i in range(1, count - 1, 2)]
    return lax.ppermute(x, "ctx", up + [(j, i) for i, j in up])


def body(query_rows, key_rows, value_rows, grad_out, stripe_lists):
    count = lax.axis_size("ctx")
    me = lax.axis_index("ctx")
    bits = stage_bits(count)
    x_bit, y_bit = bits[-2], bits[-3]
    relative = stripe_lists ^ me
    slots = jnp.zeros_like(relative)
    for place, bit in enumerate(bits):
        slots = slots | jnp.where((relative & bit) != 0, 1 << place, 0)
    flags = (1 - (me & 1)).reshape(1)
    alone = (me == 0) | (me == count - 1)
    biases = jnp.where(alone, -jnp.inf, 0.0).astype(F32).reshape(1)

    pair = jnp.stack([query_rows * BF16(SCALE), grad_out])
    own = jnp.stack([key_rows, value_rows])
    across_k = crossed(key_rows, count)
    across_v = crossed(value_rows, count)
    mate_k = swapped(key_rows, count, 1)
    mate_v = swapped(value_rows, count, 1)
    gathered = jnp.stack([key_rows[ROWS - STRIPE :], value_rows[ROWS - STRIPE :]])[None]
    for bit in bits[:-1]:
        if bit == y_bit:
            gathered, across_k = lax.optimization_barrier((gathered, across_k))
        if bit == x_bit:
            gathered, across_v, mate_k, mate_v = lax.optimization_barrier(
                (gathered, across_v, mate_k, mate_v)
            )
            near_s, near_d, stats = window_part(
                flags, biases, pair, own, mate_k, across_k, mate_v, across_v
            )
        gathered = jnp.concatenate([gathered, swapped(gathered, count, bit)], axis=0)
    gathered, stats = lax.optimization_barrier((gathered, stats))
    other = swapped(gathered, count, bits[-1])
    coefs, far_query, keep, send = stripe_part(flags, slots, pair, stats, gathered, other)
    for bit in bits[::-1]:
        total = keep + swapped(send, count, bit).astype(F32)
        half = total.shape[0] // 2
        keep, send = total[:half], total[half:].astype(BF16)
        if bit == 1:
            keep, send, coefs = lax.optimization_barrier((keep, send, coefs))
            grad_query, grad_key, grad_value, grad_mate, grad_across = gradient_part(
                flags, pair, own, mate_k, across_k, near_s, near_d, coefs, far_query
            )
        if bit == x_bit:
            keep, send, grad_across, grad_mate = lax.optimization_barrier(
                (keep, send, grad_across, grad_mate)
            )
            from_mate = swapped(grad_mate, count, 1)
            from_across = crossed(grad_across, count)
        if bit == bits[1]:
            keep, send, from_across = lax.optimization_barrier((keep, send, from_across))
    outs = []
    for which, grad_own in enumerate((grad_key, grad_value)):
        tail = jnp.pad(total[0, which], ((ROWS - STRIPE, 0), (0, 0)))
        outs.append(
            grad_own + from_mate[which].astype(F32) + from_across[which].astype(F32) + tail
        )
    return grad_query, outs[0], outs[1]


def solution(mesh):
    spec = P(("parts", "ctx"), None)
    return jax.shard_map(
        body,
        mesh=mesh,
        in_specs=(spec,) * 5,
        out_specs=(spec,) * 3,
        check_vma=False,
    )
```

time: 82.4 us -> 71.6 us (0.87)
  the two profiles are of different devices: /device:TPU:13 before, /device:TPU:0 now
where the time goes in v2:
time: 71.6 us; the launch traced here: 71.3 us
  waiting for transfers between devices  36.1 us (50%)
  starting transfers between devices  16 us (22%)
  Pallas kernels  12.1 us (17%)
  other arithmetic  4.65 us (6%)
  local copies, waits for them, and re-layouts  1.59 us (2%)
  between operations  0.92 us (1%)
    ppermute x13, waiting for transfers between devices, swapped(): return lax.ppermute(x, 'ctx', [(i, i ^ bit) for i in range(count)])  36.1 us
    ppermute x13, starting transfers between devices, swapped(): return lax.ppermute(x, 'ctx', [(i, i ^ bit) for i in range(count)])  13.9 us
    pallas_call x3, Pallas kernels, call(): pl.pallas_call(whole, in_specs=[SMEM_SPEC if kind == FULL else VMEM_SPEC...  12.1 us
    ppermute x3, starting transfers between devices, crossed(): return lax.ppermute(x, 'ctx', up + [(j, i) for i, j in up])  2.04 us
    another operation x2, other arithmetic, body(): pair = jnp.stack([query_rows * BF16(SCALE), grad_out])  1.98 us
    another operation x2, local copies, waits for them, and re-layouts, body(): jnp.stack([key_rows[ROWS - STRIPE:], value_rows[ROWS - STRIPE:]])[None]  1.44 us
  transfers between devices with their start and end apart: 16, of which 9 were waited for; matrix products, arithmetic and copies ran while one was open for 4% of the time, Pallas kernels for 11%

profile of v2, /device:TPU:0, one launch (start us, length us, event | category | flops | bytes accessed | tf_op | source)
XLA Modules:
  0.0 71.3 jit_solution(14436857425882399012)
XLA Ops:
  0.6 0.7 %slice_bitcast_fusion.4 = bf16[1,16,512]{2,1,0:T(8,128)(2,1)S(1)} fusion(bf16[256,512]{1,0:T(8,128)(2,1)} %param.7), kind=kLoop, calls=%fused_computation.27 | loop fusion | bytes 32768 | tf_op jit(solution)/shard_map/stack | solution.py:343
  1.4 0.7 %slice_bitcast_fusion.5 = bf16[1,16,512]{2,1,0:T(8,128)(2,1)S(1)} fusion(bf16[256,512]{1,0:T(8,128)(2,1)} %param.6), kind=kLoop, calls=%fused_computation.28 | loop fusion | bytes 32768 | tf_op jit(solution)/shard_map/stack | solution.py:343
  2.1 3.0 %collective-permute-start = (bf16[1,2,16,512]{3,2,1,0:T(8,128)(2,1)S(1)}, bf16[1,2,16,512]{3,2,1,0:T(8,128)(2,1)S(1)}, u32[]{:S(2)}, u32[]{:S(2)}) collective-permute-start(bf16[1,2,16,512]{3,2,1,0:T(8,128)(2,1)S(1)} %maximum_bitcast_fusion), channel_id=1, source_target_pairs={{0,8},{1,9},{2,10},{3,11},{4,12},{5,13},{6,14},{7,15},{8,0},{9,1},... | collective-permute-start | bytes 98312 | tf_op jit(solution)/shard_map/ppermute | solution.py:316
  5.8 0.7 collective-permute-start.4
  6.5 4.2 %collective-permute-start.5 = (bf16[256,512]{1,0:T(8,128)(2,1)}, bf16[256,512]{1,0:T(8,128)(2,1)S(1)}, u32[]{:S(2)}, u32[]{:S(2)}) collective-permute-start(bf16[256,512]{1,0:T(8,128)(2,1)} %param.6), channel_id=1, source_target_pairs={{0,1},{1,0},{2,3},{3,2},{4,5},{5,4},{6,7},{7,6},{8,9},{9,8},{10,11... | collective-permute-start | bytes 786440 | tf_op jit(solution)/shard_map/ppermute | solution.py:316
  10.7 5.0 %collective-permute-start.1 = (bf16[2,2,16,512]{3,2,1,0:T(8,128)(2,1)S(1)}, bf16[2,2,16,512]{3,2,1,0:T(8,128)(2,1)S(1)}, u32[]{:S(2)}, u32[]{:S(2)}) collective-permute-start(bf16[2,2,16,512]{3,2,1,0:T(8,128)(2,1)S(1)} %pad_maximum_fusion.5), channel_id=1, source_target_pairs={{0,16},{1,17},{2,18},{3,19},{4,20},{5,21},{6,22},{7,23},{8,24},{9,... | collective-permute-start | bytes 196616 | tf_op jit(solution)/shard_map/ppermute | solution.py:316
  15.7 1.0 %multiply_bitcast_fusion = bf16[1,256,512]{2,1,0:T(8,128)(2,1)S(1)} fusion(bf16[256,512]{1,0:T(8,128)(2,1)} %param.5), kind=kLoop, calls=%fused_computation.17 | loop fusion | flops 131072 | bytes 524288 | tf_op jit(solution)/shard_map/stack | solution.py:337
  16.7 5.6 %collective-permute-done.1 = bf16[2,2,16,512]{3,2,1,0:T(8,128)(2,1)S(1)} collective-permute-done((bf16[2,2,16,512]{3,2,1,0:T(8,128)(2,1)S(1)}, bf16[2,2,16,512]{3,2,1,0:T(8,128)(2,1)S(1)}, u32[]{:S(2)}, u32[]{:S(2)}) %collective-permute-start.1) | collective-permute-done | bytes 65568 | tf_op jit(solution)/shard_map/ppermute | solution.py:316
  22.4 1.0 %pad_maximum_fusion.refs_2_.refs_1_ = bf16[2,256,512]{2,1,0:T(8,128)(2,1)S(1)} fusion(bf16[1,256,512]{2,1,0:T(8,128)(2,1)} %bitcast.35, bf16[1,256,512]{2,1,0:T(8,128)(2,1)S(1)} %multiply_bitcast_fusion), kind=kLoop, calls=%fused_computation.2 | loop fusion | flops 262144 | bytes 1048576 | tf_op jit(solution)/shard_map/stack | solution.py:337
  23.4 1.1 %pad_maximum_fusion.1.refs_3_.refs_2_ = bf16[2,256,512]{2,1,0:T(8,128)(2,1)S(1)} fusion(bf16[1,256,512]{2,1,0:T(8,128)(2,1)} %bitcast.34, bf16[1,256,512]{2,1,0:T(8,128)(2,1)} %bitcast.33), kind=kLoop, calls=%fused_computation.3 | loop fusion | flops 262144 | bytes 1048576 | tf_op jit(solution)/shard_map/stack | solution.py:338
  24.5 2.9 %collective-permute-done.3 = bf16[4,2,16,512]{3,2,1,0:T(8,128)(2,1)S(1)} collective-permute-done((bf16[4,2,16,512]{3,2,1,0:T(8,128)(2,1)S(1)}, bf16[4,2,16,512]{3,2,1,0:T(8,128)(2,1)S(1)}, u32[]{:S(2)}, u32[]{:S(2)}) %collective-permute-start.3) | collective-permute-done | bytes 131104 | tf_op jit(solution)/shard_map/ppermute | solution.py:316
  27.5 3.1 %shard_map.76 = (f32[4,768,512]{2,1,0:T(8,128)S(1)}, f32[4,768,512]{2,1,0:T(8,128)S(1)}, f32[4,8,512]{2,1,0:T(8,128)S(1)}) custom-call(s32[1]{0:T(128)} %bitcast.refs_0_, f32[1]{0:T(128)} %bitcast.8.refs_1_, bf16[2,256,512]{2,1,0:T(8,128)(2,1)S(1)} %pad_maximum_fusion.refs_2_.refs_1_, bf16[2,256,512]{2,1,0:T(8,128)(2,1)S(1)} %pad_maximum_fusion.1.refs_3_.refs_2_, ...), custom_call_target="tpu_custom_call" | custom-call | flops 17179869184 | bytes 12582912 | tf_op jit(solution)/shard_map/pallas_call | solution.py:228
  30.6 3.3 %collective-permute-done.7 = bf16[8,2,16,512]{3,2,1,0:T(8,128)(2,1)S(1)} collective-permute-done((bf16[8,2,16,512]{3,2,1,0:T(8,128)(2,1)S(1)}, bf16[8,2,16,512]{3,2,1,0:T(8,128)(2,1)S(1)}, u32[]{:S(2)}, u32[]{:S(2)}) %collective-permute-start.7) | collective-permute-done | bytes 262176 | tf_op jit(solution)/shard_map/ppermute | solution.py:316
  34.0 1.9 %collective-permute-done.8.refs_5_ = bf16[16,2,16,512]{3,2,1,0:T(8,128)(2,1)S(1)} collective-permute-done((bf16[16,2,16,512]{3,2,1,0:T(8,128)(2,1)S(1)}, bf16[16,2,16,512]{3,2,1,0:T(8,128)(2,1)S(1)}, u32[]{:S(2)}, u32[]{:S(2)}) %collective-permute-start.8) | collective-permute-done | bytes 524320 | tf_op jit(solution)/shard_map/ppermute | solution.py:316
  35.9 4.4 %shard_map.77 = (f32[4,8,512]{2,1,0:T(8,128)S(1)}, f32[4,128,256]{2,1,0:T(8,128)S(1)}, f32[16,2,16,512]{3,2,1,0:T(8,128)S(1)}, bf16[16,2,16,512]{3,2,1,0:T(8,128)(2,1)S(1)}) custom-call(s32[1]{0:T(128)} %bitcast.refs_0_, s32[2,16]{1,0:T(2,128)S(1)} %fusion.5.refs_1_, bf16[2,256,512]{2,1,0:T(8,128)(2,1)S(1)} %pad_maximum_fusion.refs_2_.refs_1_, ...), custom_call_target="tpu_custom_call" | custom-call | flops 1073741824 | bytes 4194304 | tf_op jit(solution)/shard_map/pallas_call | solution.py:228
  40.5 1.8 %collective-permute-done.9 = bf16[16,2,16,512]{3,2,1,0:T(8,128)(2,1)S(1)} collective-permute-done((bf16[16,2,16,512]{3,2,1,0:T(8,128)(2,1)S(1)}, bf16[16,2,16,512]{3,2,1,0:T(8,128)(2,1)S(1)}, u32[]{:S(2)}, u32[]{:S(2)}) %collective-permute-start.9) | collective-permute-done | bytes 524320 | tf_op jit(solution)/shard_map/ppermute | solution.py:316
  42.6 4.6 %shard_map.78 = (f32[256,512]{1,0:T(8,128)}, f32[256,512]{1,0:T(8,128)S(1)}, f32[256,512]{1,0:T(8,128)S(1)}, bf16[2,256,512]{2,1,0:T(8,128)(2,1)S(1)}, bf16[2,256,512]{2,1,0:T(8,128)(2,1)S(1)}) custom-call(s32[1]{0:T(128)} %bitcast.refs_0_, bf16[2,256,512]{2,1,0:T(8,128)(2,1)S(1)} %pad_maximum_fusion.refs_2_.refs_1_, ...), custom_call_target="tpu_custom_call" | custom-call | flops 17179869184 | bytes 14680064 | tf_op jit(solution)/shard_map/pallas_call | solution.py:228
  47.2 3.7 %collective-permute-done.10 = bf16[8,2,16,512]{3,2,1,0:T(8,128)(2,1)S(1)} collective-permute-done((bf16[8,2,16,512]{3,2,1,0:T(8,128)(2,1)S(1)}, bf16[8,2,16,512]{3,2,1,0:T(8,128)(2,1)S(1)}, u32[]{:S(2)}, u32[]{:S(2)}) %collective-permute-start.10) | collective-permute-done | bytes 262176 | tf_op jit(solution)/shard_map/ppermute | solution.py:316
  51.2 0.7 collective-permute-start.14
  51.9 4.3 %collective-permute-done.12 = bf16[4,2,16,512]{3,2,1,0:T(8,128)(2,1)S(1)} collective-permute-done((bf16[4,2,16,512]{3,2,1,0:T(8,128)(2,1)S(1)}, bf16[4,2,16,512]{3,2,1,0:T(8,128)(2,1)S(1)}, u32[]{:S(2)}, u32[]{:S(2)}) %collective-permute-start.12) | collective-permute-done | bytes 131104 | tf_op jit(solution)/shard_map/ppermute | solution.py:316
  56.2 1.0 %collective-permute-start.13 = (bf16[2,2,16,512]{3,2,1,0:T(8,128)(2,1)S(1)}, bf16[2,2,16,512]{3,2,1,0:T(8,128)(2,1)S(1)}, u32[]{:S(2)}, u32[]{:S(2)}) collective-permute-start(bf16[2,2,16,512]{3,2,1,0:T(8,128)(2,1)S(1)} %slice.99), channel_id=1, source_target_pairs={{0,16},{1,17},{2,18},{3,19},{4,20},{5,21},{6,22},{7,23},{8,24},{9,... | collective-permute-start | bytes 196616 | tf_op jit(solution)/shard_map/ppermute | solution.py:316
  57.2 8.8 %collective-permute-done.13 = bf16[2,2,16,512]{3,2,1,0:T(8,128)(2,1)S(1)} collective-permute-done((bf16[2,2,16,512]{3,2,1,0:T(8,128)(2,1)S(1)}, bf16[2,2,16,512]{3,2,1,0:T(8,128)(2,1)S(1)}, u32[]{:S(2)}, u32[]{:S(2)}) %collective-permute-start.13) | collective-permute-done | bytes 65568 | tf_op jit(solution)/shard_map/ppermute | solution.py:316
  66.1 3.9 %collective-permute-done.15 = bf16[1,2,16,512]{3,2,1,0:T(8,128)(2,1)S(1)} collective-permute-done((bf16[1,2,16,512]{3,2,1,0:T(8,128)(2,1)S(1)}, bf16[1,2,16,512]{3,2,1,0:T(8,128)(2,1)S(1)}, u32[]{:S(2)}, u32[]{:S(2)}) %collective-permute-start.15) | collective-permute-done | bytes 32800 | tf_op jit(solution)/shard_map/ppermute | solution.py:316
  70.1 1.2 %fusion = (f32[256,512]{1,0:T(8,128)}, f32[256,512]{1,0:T(8,128)}) fusion(f32[256,512]{1,0:T(8,128)S(1)} %get-tuple-element.62, f32[16,512]{1,0:T(8,128)S(1)} %get-tuple-element.65, bf16[2,256,512]{2,1,0:T(8,128)(2,1)S(1)} %collective-permute-done.11, bf16[2,256,512]{2,1,0:T(8,128)(2,1)S(1)} %collective-permute-done.14, f32[16,512]{1,0:T(8,128)S(1)} %get-tuple-element.66, ...), kind=kLoop, calls=%fused_computation.6 | loop fusion | flops 1310720 | bytes 3211264 | tf_op jit(solution)/shard_map/add | solution.py:379
  (38 shorter events, 1.9 us)
Async XLA Ops:
  2.1 8.6 %collective-permute-start = (bf16[1,2,16,512]{3,2,1,0:T(8,128)(2,1)S(1)}, bf16[1,2,16,512]{3,2,1,0:T(8,128)(2,1)S(1)}, u32[]{:S(2)}, u32[]{:S(2)}) collective-permute-start(bf16[1,2,16,512]{3,2,1,0:T(8,128)(2,1)S(1)} %maximum_bitcast_fusion), channel_id=1, source_target_pairs={{0,8},{1,9},{2,10},{3,11},{4,12},{5,13},{6,14},{7,15},{8,0},{9,1},... | collective-permute-start | bytes 98312 | tf_op jit(solution)/shard_map/ppermute | solution.py:316
  5.1 17.2 %collective-permute-start.2 = (bf16[256,512]{1,0:T(8,128)(2,1)}, bf16[256,512]{1,0:T(8,128)(2,1)S(1)}, u32[]{:S(2)}, u32[]{:S(2)}) collective-permute-start(bf16[256,512]{1,0:T(8,128)(2,1)} %param.6), channel_id=1, source_target_pairs={{1,2},{3,4},{5,6},{7,8},{9,10},{11,12},{13,14},{15,16},{17,18},{19... | collective-permute-start | bytes 786440 | tf_op jit(solution)/shard_map/ppermute | solution.py:321
  5.8 21.6 %collective-permute-start.4 = (bf16[256,512]{1,0:T(8,128)(2,1)}, bf16[256,512]{1,0:T(8,128)(2,1)S(1)}, u32[]{:S(2)}, u32[]{:S(2)}) collective-permute-start(bf16[256,512]{1,0:T(8,128)(2,1)} %param.7), channel_id=1, source_target_pairs={{1,2},{3,4},{5,6},{7,8},{9,10},{11,12},{13,14},{15,16},{17,18},{19... | collective-permute-start | bytes 786440 | tf_op jit(solution)/shard_map/ppermute | solution.py:321
  6.5 20.9 %collective-permute-start.5 = (bf16[256,512]{1,0:T(8,128)(2,1)}, bf16[256,512]{1,0:T(8,128)(2,1)S(1)}, u32[]{:S(2)}, u32[]{:S(2)}) collective-permute-start(bf16[256,512]{1,0:T(8,128)(2,1)} %param.6), channel_id=1, source_target_pairs={{0,1},{1,0},{2,3},{3,2},{4,5},{5,4},{6,7},{7,6},{8,9},{9,8},{10,11... | collective-permute-start | bytes 786440 | tf_op jit(solution)/shard_map/ppermute | solution.py:316
  10.6 16.8 %collective-permute-start.6 = (bf16[256,512]{1,0:T(8,128)(2,1)}, bf16[256,512]{1,0:T(8,128)(2,1)S(1)}, u32[]{:S(2)}, u32[]{:S(2)}) collective-permute-start(bf16[256,512]{1,0:T(8,128)(2,1)} %param.7), channel_id=1, source_target_pairs={{0,1},{1,0},{2,3},{3,2},{4,5},{5,4},{6,7},{7,6},{8,9},{9,8},{10,11... | collective-permute-start | bytes 786440 | tf_op jit(solution)/shard_map/ppermute | solution.py:316
  10.7 11.6 %collective-permute-start.1 = (bf16[2,2,16,512]{3,2,1,0:T(8,128)(2,1)S(1)}, bf16[2,2,16,512]{3,2,1,0:T(8,128)(2,1)S(1)}, u32[]{:S(2)}, u32[]{:S(2)}) collective-permute-start(bf16[2,2,16,512]{3,2,1,0:T(8,128)(2,1)S(1)} %pad_maximum_fusion.5), channel_id=1, source_target_pairs={{0,16},{1,17},{2,18},{3,19},{4,20},{5,21},{6,22},{7,23},{8,24},{9,... | collective-permute-start | bytes 196616 | tf_op jit(solution)/shard_map/ppermute | solution.py:316
  22.3 5.0 %collective-permute-start.3 = (bf16[4,2,16,512]{3,2,1,0:T(8,128)(2,1)S(1)}, bf16[4,2,16,512]{3,2,1,0:T(8,128)(2,1)S(1)}, u32[]{:S(2)}, u32[]{:S(2)}) collective-permute-start(bf16[4,2,16,512]{3,2,1,0:T(8,128)(2,1)S(1)} %pad_maximum_fusion.4), channel_id=1, source_target_pairs={{0,4},{1,5},{2,6},{3,7},{4,0},{5,1},{6,2},{7,3},{8,12},{9,13},{10,... | collective-permute-start | bytes 393224 | tf_op jit(solution)/shard_map/ppermute | solution.py:316
  27.4 6.4 %collective-permute-start.7 = (bf16[8,2,16,512]{3,2,1,0:T(8,128)(2,1)S(1)}, bf16[8,2,16,512]{3,2,1,0:T(8,128)(2,1)S(1)}, u32[]{:S(2)}, u32[]{:S(2)}) collective-permute-start(bf16[8,2,16,512]{3,2,1,0:T(8,128)(2,1)S(1)} %pad_maximum_fusion.3), channel_id=1, source_target_pairs={{0,2},{1,3},{2,0},{3,1},{4,6},{5,7},{6,4},{7,5},{8,10},{9,11},{10,... | collective-permute-start | bytes 786440 | tf_op jit(solution)/shard_map/ppermute | solution.py:316
  27.5 6.5 %copy-start = (s32[2,16]{1,0:T(2,128)S(1)}, s32[2,16]{1,0:T(2,128)}, u32[]{:S(2)}) copy-start(s32[2,16]{1,0:T(2,128)} %param.9) | copy-start | bytes 388
  33.9 2.0 %collective-permute-start.8 = (bf16[16,2,16,512]{3,2,1,0:T(8,128)(2,1)S(1)}, bf16[16,2,16,512]{3,2,1,0:T(8,128)(2,1)S(1)}, u32[]{:S(2)}, u32[]{:S(2)}) collective-permute-start(bf16[16,2,16,512]{3,2,1,0:T(8,128)(2,1)S(1)} %pad_maximum_fusion.2.refs_4_), channel_id=1, source_target_pairs={{0,1},{1,0},{2,3},{3,2},{4,5},{5,4},{6,7},{7,6},{8,9},{9,8},{10,11... | collective-permute-start | bytes 1572872 | tf_op jit(solution)/shard_map/ppermute | solution.py:316
  40.3 2.0 %collective-permute-start.9 = (bf16[16,2,16,512]{3,2,1,0:T(8,128)(2,1)S(1)}, bf16[16,2,16,512]{3,2,1,0:T(8,128)(2,1)S(1)}, u32[]{:S(2)}, u32[]{:S(2)}) collective-permute-start(bf16[16,2,16,512]{3,2,1,0:T(8,128)(2,1)S(1)} %get-tuple-element.45), channel_id=1, source_target_pairs={{0,1},{1,0},{2,3},{3,2},{4,5},{5,4},{6,7},{7,6},{8,9},{9,8},{10,11... | collective-permute-start | bytes 1572872 | tf_op jit(solution)/shard_map/ppermute | solution.py:316
  42.5 8.4 %collective-permute-start.10 = (bf16[8,2,16,512]{3,2,1,0:T(8,128)(2,1)S(1)}, bf16[8,2,16,512]{3,2,1,0:T(8,128)(2,1)S(1)}, u32[]{:S(2)}, u32[]{:S(2)}) collective-permute-start(bf16[8,2,16,512]{3,2,1,0:T(8,128)(2,1)S(1)} %slice.97), channel_id=1, source_target_pairs={{0,2},{1,3},{2,0},{3,1},{4,6},{5,7},{6,4},{7,5},{8,10},{9,11},{10,... | collective-permute-start | bytes 786440 | tf_op jit(solution)/shard_map/ppermute | solution.py:316
  51.1 5.0 %collective-permute-start.12 = (bf16[4,2,16,512]{3,2,1,0:T(8,128)(2,1)S(1)}, bf16[4,2,16,512]{3,2,1,0:T(8,128)(2,1)S(1)}, u32[]{:S(2)}, u32[]{:S(2)}) collective-permute-start(bf16[4,2,16,512]{3,2,1,0:T(8,128)(2,1)S(1)} %slice.98), channel_id=1, source_target_pairs={{0,4},{1,5},{2,6},{3,7},{4,0},{5,1},{6,2},{7,3},{8,12},{9,13},{10,... | collective-permute-start | bytes 393224 | tf_op jit(solution)/shard_map/ppermute | solution.py:316
  51.2 14.9 %collective-permute-start.14 = (bf16[2,256,512]{2,1,0:T(8,128)(2,1)S(1)}, bf16[2,256,512]{2,1,0:T(8,128)(2,1)S(1)}, u32[]{:S(2)}, u32[]{:S(2)}) collective-permute-start(bf16[2,256,512]{2,1,0:T(8,128)(2,1)S(1)} %get-tuple-element.58), channel_id=1, source_target_pairs={{1,2},{3,4},{5,6},{7,8},{9,10},{11,12},{13,14},{15,16},{17,18},{19... | collective-permute-start | bytes 1572872 | tf_op jit(solution)/shard_map/ppermute | solution.py:321
  56.2 9.8 %collective-permute-start.13 = (bf16[2,2,16,512]{3,2,1,0:T(8,128)(2,1)S(1)}, bf16[2,2,16,512]{3,2,1,0:T(8,128)(2,1)S(1)}, u32[]{:S(2)}, u32[]{:S(2)}) collective-permute-start(bf16[2,2,16,512]{3,2,1,0:T(8,128)(2,1)S(1)} %slice.99), channel_id=1, source_target_pairs={{0,16},{1,17},{2,18},{3,19},{4,20},{5,21},{6,22},{7,23},{8,24},{9,... | collective-permute-start | bytes 196616 | tf_op jit(solution)/shard_map/ppermute | solution.py:316
  57.2 12.8 %collective-permute-start.11 = (bf16[2,256,512]{2,1,0:T(8,128)(2,1)S(1)}, bf16[2,256,512]{2,1,0:T(8,128)(2,1)S(1)}, u32[]{:S(2)}, u32[]{:S(2)}) collective-permute-start(bf16[2,256,512]{2,1,0:T(8,128)(2,1)S(1)} %get-tuple-element.55), channel_id=1, source_target_pairs={{0,1},{1,0},{2,3},{3,2},{4,5},{5,4},{6,7},{7,6},{8,9},{9,8},{10,11... | collective-permute-start | bytes 1572872 | tf_op jit(solution)/shard_map/ppermute | solution.py:316
  66.0 4.0 %collective-permute-start.15 = (bf16[1,2,16,512]{3,2,1,0:T(8,128)(2,1)S(1)}, bf16[1,2,16,512]{3,2,1,0:T(8,128)(2,1)S(1)}, u32[]{:S(2)}, u32[]{:S(2)}) collective-permute-start(bf16[1,2,16,512]{3,2,1,0:T(8,128)(2,1)S(1)} %slice.100), channel_id=1, source_target_pairs={{0,8},{1,9},{2,10},{3,11},{4,12},{5,13},{6,14},{7,15},{8,0},{9,1},... | collective-permute-start | bytes 98312 | tf_op jit(solution)/shard_map/ppermute | solution.py:316

commit v3 on v2

--- a/solution.py
+++ b/solution.py
@@ -18,6 +18,7 @@
 SCALE = HEAD_DIM**-0.5
 NT = (((1,), (1,)), ((), ()))
 BF16, F32 = jnp.bfloat16, jnp.float32
+SETS = 2
 
 
 def tile(h, i):
@@ -35,6 +36,23 @@
         zero = jnp.zeros_like(x)
         two[tile(0, i)] = jnp.where(first, x, zero)
         two[tile(1, i)] = jnp.where(first, zero, x)
+
+
+def both(i):
+    return slice(2 * i * BLOCK, 2 * (i + 1) * BLOCK)
+
+
+def stat(h, i):
+    return tile(i, h)
+
+
+def split_blocks(ref, which, flip, two):
+    first = lax.broadcasted_iota(jnp.int32, (BLOCK, LANES), 1) < HEAD_DIM
+    for i in range(2):
+        x = ref[which, block_rows(i, flip)]
+        zero = jnp.zeros_like(x)
+        two[stat(0, i)] = jnp.where(first, x, zero)
+        two[stat(1, i)] = jnp.where(first, zero, x)
 
 
 def fill_window(flip, mate, own, which, across, ext):
@@ -81,40 +99,40 @@
             d = near_d[0, near_rows(i), tile(h, i)]
             top = column_max(s)
             u = jnp.exp(s - top)
-            stats[0, 0:1, tile(h, i)] = top
-            stats[0, 1:2, tile(h, i)] = column_sum(u)
-            stats[0, 2:3, tile(h, i)] = column_sum(u * d)
+            stats[0, 0:1, stat(h, i)] = top
+            stats[0, 1:2, stat(h, i)] = column_sum(u)
+            stats[0, 2:3, stat(h, i)] = column_sum(u * d)
 
 
 def stripe_kernel(
-    flags, slots, pair, stats, table_a, table_b, coefs, far_query, table_keep, table_send,
-    table, far_k, far_v, q_two, g_two, far_probs, far_scores, table_sum,
+    flags, slots, pair, stats, table_a, table_b, table_c, table_d,
+    coefs, far_query, keep_a, keep_b, send_a, send_b,
+    far_k, far_v, q_two, g_two, far_probs, far_scores, table_sum,
 ):
     flip = flags[0]
-    half = table_a.shape[0]
-    table[:half] = table_a[...]
-    table[half:] = table_b[...]
+    part = table_a.shape[0]
     for i in range(2):
         for j in range(NCOL):
             slot = slots[i ^ flip, j]
-            far_k[i, j * STRIPE : (j + 1) * STRIPE] = table[slot, 0]
-            far_v[i, j * STRIPE : (j + 1) * STRIPE] = table[slot, 1]
-    split_heads(pair, 0, flip, q_two)
-    split_heads(pair, 1, flip, g_two)
-    tiles = [(h, i) for h in range(2) for i in range(2)]
-    s = jnp.concatenate(
-        [
-            lax.dot_general(far_k[i], q_two[tile(h, i)], NT, preferred_element_type=F32)
-            for h, i in tiles
-        ],
-        axis=1,
-    )
-    d = jnp.concatenate(
-        [
-            lax.dot_general(far_v[i], g_two[tile(h, i)], NT, preferred_element_type=F32)
-            for h, i in tiles
-        ],
-        axis=1,
+            place = slot & (part - 1)
+            rows = slice(j * STRIPE, (j + 1) * STRIPE)
+            for which, far in ((0, far_k), (1, far_v)):
+                far[i, rows] = jnp.where(
+                    slot < 2 * part,
+                    jnp.where(slot < part, table_a[place, which], table_b[place, which]),
+                    jnp.where(slot < 3 * part, table_c[place, which], table_d[place, which]),
+                )
+    split_blocks(pair, 0, flip, q_two)
+    split_blocks(pair, 1, flip, g_two)
+    s, d = (
+        jnp.concatenate(
+            [
+                lax.dot_general(far[i], two[both(i)], NT, preferred_element_type=F32)
+                for i in range(2)
+            ],
+            axis=1,
+        )
+        for far, two in ((far_k, q_two), (far_v, g_two))
     )
     near_top = stats[0, 0:1]
     top = jnp.maximum(near_top, column_max(s))
@@ -131,23 +149,24 @@
     table_sum[...] = jnp.zeros_like(table_sum)
     for which, left, right in ((0, far_scores, q_two), (1, far_probs, g_two)):
         for i in range(2):
-            far = jnp.dot(
-                jnp.concatenate([left[:, tile(0, i)], left[:, tile(1, i)]], axis=1),
-                jnp.concatenate([right[tile(0, i)], right[tile(1, i)]], axis=0),
-                preferred_element_type=F32,
-            )
-            for j in range(NCOL):
-                slot = slots[i ^ flip, j]
-                table_sum[slot, which] += far[j * STRIPE : (j + 1) * STRIPE]
-    table_keep[...] = table_sum[:half]
-    table_send[...] = table_sum[half:].astype(table_send.dtype)
-    for i in range(2):
-        k_t = jnp.transpose(far_k[i])
-        for h in range(2):
-            feats = slice(h * HEAD_DIM, (h + 1) * HEAD_DIM)
-            far_query[0, feats, i * BLOCK : (i + 1) * BLOCK] = jnp.dot(
-                k_t[feats], far_scores[:, tile(h, i)], preferred_element_type=F32
-            )
+            far = jnp.dot(left[:, both(i)], right[both(i)], preferred_element_type=F32)
+            parts = [far[j * STRIPE : (j + 1) * STRIPE] for j in range(NCOL)]
+            places = [slots[i ^ flip, j] for j in range(NCOL)]
+            if i == 1:
+                parts = [x + table_sum[place, which] for x, place in zip(parts, places)]
+            for x, place in zip(parts, places):
+                table_sum[place, which] = x
+    keep_a[...] = table_sum[:part]
+    keep_b[...] = table_sum[part : 2 * part]
+    send_a[...] = table_sum[2 * part : 3 * part].astype(send_a.dtype)
+    send_b[...] = table_sum[3 * part :].astype(send_b.dtype)
+    for i in range(2):
+        out = jnp.dot(
+            jnp.transpose(far_k[i]), far_scores[:, both(i)], preferred_element_type=F32
+        )
+        rows = slice(i * BLOCK, (i + 1) * BLOCK)
+        far_query[0, :HEAD_DIM, rows] = out[:HEAD_DIM, :BLOCK]
+        far_query[0, HEAD_DIM:, rows] = out[HEAD_DIM:, BLOCK:]
 
 
 def gradient_kernel(
@@ -169,9 +188,9 @@
     for h in range(2):
         for i in range(2):
             rows = near_rows(i)
-            p = jnp.exp(near_s[0, rows, tile(h, i)] - coefs[0, 0:1, tile(h, i)])
+            p = jnp.exp(near_s[0, rows, tile(h, i)] - coefs[0, 0:1, stat(h, i)])
             probs[rows, tile(h, i)] = p.astype(BF16)
-            ds = p * (near_d[0, rows, tile(h, i)] - coefs[0, 1:2, tile(h, i)])
+            ds = p * (near_d[0, rows, tile(h, i)] - coefs[0, 1:2, stat(h, i)])
             scores[rows, tile(h, i)] = ds.astype(BF16)
     for which, left, right, grad_own in (
         (0, scores, q_two, grad_key),
@@ -223,14 +242,15 @@
     def whole(*refs):
         for p in range(steps):
             views = [view(ref, kind, p) for ref, kind in zip(refs, kinds)]
-            kernel(*views, *refs[len(kinds) :])
+            first = len(kinds) + p % SETS * len(scratch)
+            kernel(*views, *refs[first : first + len(scratch)])
 
     return pl.pallas_call(
         whole,
         in_specs=[SMEM_SPEC if kind == FULL else VMEM_SPEC for kind in in_kinds],
         out_specs=[VMEM_SPEC] * len(out_kinds),
         out_shape=[jax.ShapeDtypeStruct(shape, dtype) for shape, dtype in out_shape],
-        scratch_shapes=scratch,
+        scratch_shapes=scratch * SETS,
         compiler_params=pltpu.CompilerParams(vmem_limit_bytes=24 << 20),
         cost_estimate=pl.CostEstimate(flops=flops, bytes_accessed=moved, transcendentals=1 << 20),
     )(*args)
@@ -252,34 +272,30 @@
     )
 
 
-def stripe_part(flags, slots, pair, stats, table_a, table_b):
-    half = table_a.shape[0]
+def stripe_part(flags, slots, pair, stats, *tables):
+    part = tables[0].shape[0]
     width = pair.shape[2]
     steps = width // LANES
     return call(
         stripe_kernel,
         steps,
-        [FULL, FULL, PAIR, STEP, TABLE, TABLE],
-        [STEP, STEP, TABLE, TABLE],
+        [FULL, FULL, PAIR, STEP] + [TABLE] * 4,
+        [STEP, STEP] + [TABLE] * 4,
+        [((steps, 8, 2 * ROWS), F32), ((steps, LANES, ROWS), F32)]
+        + [((part, 2, STRIPE, width), F32)] * 2
+        + [((part, 2, STRIPE, width), BF16)] * 2,
         [
-            ((steps, 8, 2 * ROWS), F32),
-            ((steps, LANES, ROWS), F32),
-            ((half, 2, STRIPE, width), F32),
-            ((half, 2, STRIPE, width), BF16),
-        ],
-        [
-            pltpu.VMEM((2 * half, 2, STRIPE, LANES), BF16),
             pltpu.VMEM((2, FAR, LANES), BF16),
             pltpu.VMEM((2, FAR, LANES), BF16),
             TWO,
             TWO,
             pltpu.VMEM((FAR, 4 * BLOCK), BF16),
             pltpu.VMEM((FAR, 4 * BLOCK), BF16),
-            pltpu.VMEM((2 * half, 2, STRIPE, LANES), F32),
+            pltpu.VMEM((4 * part, 2, STRIPE, LANES), F32),
         ],
         1 << 30,
         4 << 20,
-        (flags, slots, pair, stats, table_a, table_b),
+        (flags, slots, pair, stats, *tables),
     )
 
 
@@ -306,10 +322,8 @@
 
 
 def stage_bits(count):
-    if count == 32:
-        return [8, 16, 4, 2, 1]
     bits = [1 << k for k in range(count.bit_length() - 1)]
-    return bits[1:] + bits[:1]
+    return bits[3:] + bits[2::-1]
 
 
 def swapped(x, count, bit):
@@ -325,7 +339,7 @@
     count = lax.axis_size("ctx")
     me = lax.axis_index("ctx")
     bits = stage_bits(count)
-    x_bit, y_bit = bits[-2], bits[-3]
+    *z_bits, y_bit, x_bit, core_bit = bits
     relative = stripe_lists ^ me
     slots = jnp.zeros_like(relative)
     for place, bit in enumerate(bits):
@@ -336,48 +350,48 @@
 
     pair = jnp.stack([query_rows * BF16(SCALE), grad_out])
     own = jnp.stack([key_rows, value_rows])
+    mate_k = swapped(key_rows, count, core_bit)
+    mate_v = swapped(value_rows, count, core_bit)
+    gathered = own[None, :, ROWS - STRIPE :]
     across_k = crossed(key_rows, count)
-    across_v = crossed(value_rows, count)
-    mate_k = swapped(key_rows, count, 1)
-    mate_v = swapped(value_rows, count, 1)
-    gathered = jnp.stack([key_rows[ROWS - STRIPE :], value_rows[ROWS - STRIPE :]])[None]
-    for bit in bits[:-1]:
+    for stage, bit in enumerate((*z_bits, y_bit)):
         if bit == y_bit:
             gathered, across_k = lax.optimization_barrier((gathered, across_k))
-        if bit == x_bit:
-            gathered, across_v, mate_k, mate_v = lax.optimization_barrier(
-                (gathered, across_v, mate_k, mate_v)
-            )
-            near_s, near_d, stats = window_part(
-                flags, biases, pair, own, mate_k, across_k, mate_v, across_v
-            )
         gathered = jnp.concatenate([gathered, swapped(gathered, count, bit)], axis=0)
-    gathered, stats = lax.optimization_barrier((gathered, stats))
-    other = swapped(gathered, count, bits[-1])
-    coefs, far_query, keep, send = stripe_part(flags, slots, pair, stats, gathered, other)
-    for bit in bits[::-1]:
-        total = keep + swapped(send, count, bit).astype(F32)
+        if stage == 0:
+            gathered, late = lax.optimization_barrier((gathered, value_rows))
+            across_v = crossed(late, count)
+    gathered, across_v = lax.optimization_barrier((gathered, across_v))
+    near_s, near_d, stats = window_part(
+        flags, biases, pair, own, mate_k, across_k, mate_v, across_v
+    )
+    beside = swapped(gathered, count, x_bit)
+    beside, stats = lax.optimization_barrier((beside, stats))
+    tables = [gathered, beside] + [swapped(x, count, core_bit) for x in (gathered, beside)]
+    coefs, far_query, keep_a, keep_b, send_a, send_b = stripe_part(
+        flags, slots, pair, stats, *tables
+    )
+    send = keep_b + swapped(send_b, count, core_bit).astype(F32)
+    keep = keep_a + swapped(send_a, count, core_bit).astype(F32)
+    send, coefs = lax.optimization_barrier((send.astype(BF16), coefs))
+    grad_query, grad_key, grad_value, grad_mate, grad_across = gradient_part(
+        flags, pair, own, mate_k, across_k, near_s, near_d, coefs, far_query
+    )
+    total = keep + swapped(send, count, x_bit).astype(F32)
+    total, grad_mate = lax.optimization_barrier((total, grad_mate))
+    from_mate = swapped(grad_mate, count, core_bit)
+    from_across = crossed(grad_across, count)
+    for bit in (y_bit, *z_bits[::-1]):
         half = total.shape[0] // 2
         keep, send = total[:half], total[half:].astype(BF16)
-        if bit == 1:
-            keep, send, coefs = lax.optimization_barrier((keep, send, coefs))
-            grad_query, grad_key, grad_value, grad_mate, grad_across = gradient_part(
-                flags, pair, own, mate_k, across_k, near_s, near_d, coefs, far_query
-            )
-        if bit == x_bit:
-            keep, send, grad_across, grad_mate = lax.optimization_barrier(
-                (keep, send, grad_across, grad_mate)
-            )
-            from_mate = swapped(grad_mate, count, 1)
-            from_across = crossed(grad_across, count)
-        if bit == bits[1]:
-            keep, send, from_across = lax.optimization_barrier((keep, send, from_across))
+        if bit == z_bits[0]:
+            keep, from_across = lax.optimization_barrier((keep, from_across))
+        total = keep + swapped(send, count, bit).astype(F32)
     outs = []
     for which, grad_own in enumerate((grad_key, grad_value)):
-        tail = jnp.pad(total[0, which], ((ROWS - STRIPE, 0), (0, 0)))
-        outs.append(
-            grad_own + from_mate[which].astype(F32) + from_across[which].astype(F32) + tail
-        )
+        base = grad_own + from_mate[which].astype(F32) + from_across[which].astype(F32)
+        base = lax.optimization_barrier(base)
+        outs.append(base.at[ROWS - STRIPE :].add(total[0, which]))
     return grad_query, outs[0], outs[1]
 
 

time: 71.6 us -> 68.3 us (0.954)
  waiting for transfers between devices: 36.1 us -> 28.4 us
  starting transfers between devices: 16 us -> 21.2 us
    ppermute x13 -> x15, waiting for transfers between devices: 36.1 us -> 28.4 us  [swapped(): return lax.ppermute(x, 'ctx', [(i, i ^ bit) for i in range(count)])]
    ppermute x13 -> x15, starting transfers between devices: 13.9 us -> 19.2 us  [swapped(): return lax.ppermute(x, 'ctx', [(i, i ^ bit) for i in range(count)])]
    another operation x2 -> x0, local copies, waits for them, and re-layouts: 1.44 us -> none  [body(): jnp.stack([key_rows[ROWS - STRIPE:], value_rows[ROWS - STRIPE:]])[None]]
    unnamed x2 -> x6, local copies, waits for them, and re-layouts: 0.01 us -> 0.96 us
    add x1, other arithmetic: 1.19 us -> 0.26 us  [body(): grad_own + from_mate[which].astype(F32) + from_across[which].astype(F32)]
    broadcast_in_dim x1, other arithmetic: 0.01 us -> 0.74 us  [body(): gathered = own[None, :, ROWS - STRIPE:]]
  transfers between devices with their start and end apart: 16 -> 18, of which waited for: 9 -> 9; matrix products, arithmetic and copies ran while one was open for 4% -> 5% of each run, Pallas kernels for 11% -> 11%
where the time goes in v3:
time: 68.3 us; the launch traced here: 67.9 us
  waiting for transfers between devices  28.4 us (42%)
  starting transfers between devices  21.2 us (31%)
  Pallas kernels  12.1 us (18%)
  other arithmetic  4.38 us (6%)
  local copies, waits for them, and re-layouts  1 us (1%)
  between operations  0.84 us (1%)
    ppermute x15, waiting for transfers between devices, swapped(): return lax.ppermute(x, 'ctx', [(i, i ^ bit) for i in range(count)])  28.4 us
    ppermute x15, starting transfers between devices, swapped(): return lax.ppermute(x, 'ctx', [(i, i ^ bit) for i in range(count)])  19.2 us
    pallas_call x3, Pallas kernels, call(): pl.pallas_call(whole, in_specs=[SMEM_SPEC if kind == FULL else VMEM_SPEC...  12.1 us
    ppermute x3, starting transfers between devices, crossed(): return lax.ppermute(x, 'ctx', up + [(j, i) for i, j in up])  2.02 us
    another operation x2, other arithmetic, body(): pair = jnp.stack([query_rows * BF16(SCALE), grad_out])  1.98 us
  transfers between devices with their start and end apart: 18, of which 9 were waited for; matrix products, arithmetic and copies ran while one was open for 5% of the time, Pallas kernels for 11%

profile of v3, /device:TPU:0, one launch (start us, length us, event | category | flops | bytes accessed | tf_op | source)
XLA Modules:
  0.0 67.9 jit_solution(7491384748684727801)
XLA Ops:
  0.6 0.7 %fusion.5 = bf16[1,2,16,512]{3,2,1,0:T(8,128)(2,1)S(1)} fusion(bf16[1,256,512]{2,1,0:T(8,128)(2,1)} %bitcast.39, bf16[1,256,512]{2,1,0:T(8,128)(2,1)} %bitcast.37), kind=kLoop, calls=%fused_computation.29 | loop fusion | flops 16384 | bytes 557056 | tf_op jit(solution)/shard_map/broadcast_in_dim | solution.py:355
  1.4 3.0 %collective-permute-start.1 = (bf16[1,2,16,512]{3,2,1,0:T(8,128)(2,1)S(1)}, bf16[1,2,16,512]{3,2,1,0:T(8,128)(2,1)S(1)}, u32[]{:S(2)}, u32[]{:S(2)}) collective-permute-start(bf16[1,2,16,512]{3,2,1,0:T(8,128)(2,1)S(1)} %fusion.5), channel_id=1, source_target_pairs={{0,8},{1,9},{2,10},{3,11},{4,12},{5,13},{6,14},{7,15},{8,0},{9,1},... | collective-permute-start | bytes 98312 | tf_op jit(solution)/shard_map/ppermute | solution.py:330
  5.1 2.9 %collective-permute-start = (bf16[256,512]{1,0:T(8,128)(2,1)}, bf16[256,512]{1,0:T(8,128)(2,1)S(1)}, u32[]{:S(2)}, u32[]{:S(2)}) collective-permute-start(bf16[256,512]{1,0:T(8,128)(2,1)} %param.10), channel_id=1, source_target_pairs={{0,1},{1,0},{2,3},{3,2},{4,5},{5,4},{6,7},{7,6},{8,9},{9,8},{10,11... | collective-permute-start | bytes 786440 | tf_op jit(solution)/shard_map/ppermute | solution.py:330
  8.1 2.7 %collective-permute-start.2 = (bf16[2,2,16,512]{3,2,1,0:T(8,128)(2,1)S(1)}, bf16[2,2,16,512]{3,2,1,0:T(8,128)(2,1)S(1)}, u32[]{:S(2)}, u32[]{:S(2)}) collective-permute-start(bf16[2,2,16,512]{3,2,1,0:T(8,128)(2,1)S(1)} %pad_maximum_fusion.4), channel_id=1, source_target_pairs={{0,16},{1,17},{2,18},{3,19},{4,20},{5,21},{6,22},{7,23},{8,24},{9,... | collective-permute-start | bytes 196616 | tf_op jit(solution)/shard_map/ppermute | solution.py:330
  10.7 1.0 %multiply_bitcast_fusion = bf16[1,256,512]{2,1,0:T(8,128)(2,1)S(1)} fusion(bf16[256,512]{1,0:T(8,128)(2,1)} %param.9), kind=kLoop, calls=%fused_computation.15 | loop fusion | flops 131072 | bytes 524288 | tf_op jit(solution)/shard_map/stack | solution.py:351
  12.4 3.6 %collective-permute-done.2 = bf16[2,2,16,512]{3,2,1,0:T(8,128)(2,1)S(1)} collective-permute-done((bf16[2,2,16,512]{3,2,1,0:T(8,128)(2,1)S(1)}, bf16[2,2,16,512]{3,2,1,0:T(8,128)(2,1)S(1)}, u32[]{:S(2)}, u32[]{:S(2)}) %collective-permute-start.2) | collective-permute-done | bytes 65568 | tf_op jit(solution)/shard_map/ppermute | solution.py:330
  16.6 1.1 %pad_maximum_fusion.refs_3_.refs_2_ = bf16[2,256,512]{2,1,0:T(8,128)(2,1)S(1)} fusion(bf16[1,256,512]{2,1,0:T(8,128)(2,1)} %bitcast.40, bf16[1,256,512]{2,1,0:T(8,128)(2,1)} %bitcast.38), kind=kLoop, calls=%fused_computation.1 | loop fusion | flops 262144 | bytes 1048576 | tf_op jit(solution)/shard_map/stack | solution.py:352
  17.7 1.0 %pad_maximum_fusion.1.refs_2_.refs_1_ = bf16[2,256,512]{2,1,0:T(8,128)(2,1)S(1)} fusion(bf16[1,256,512]{2,1,0:T(8,128)(2,1)} %bitcast.41, bf16[1,256,512]{2,1,0:T(8,128)(2,1)S(1)} %multiply_bitcast_fusion), kind=kLoop, calls=%fused_computation.3 | loop fusion | flops 262144 | bytes 1048576 | tf_op jit(solution)/shard_map/stack | solution.py:351
  18.7 3.5 %collective-permute-done.5 = bf16[4,2,16,512]{3,2,1,0:T(8,128)(2,1)S(1)} collective-permute-done((bf16[4,2,16,512]{3,2,1,0:T(8,128)(2,1)S(1)}, bf16[4,2,16,512]{3,2,1,0:T(8,128)(2,1)S(1)}, u32[]{:S(2)}, u32[]{:S(2)}) %collective-permute-start.5) | collective-permute-done | bytes 131104 | tf_op jit(solution)/shard_map/ppermute | solution.py:330
  22.2 3.0 %collective-permute-start.7 = (bf16[8,2,16,512]{3,2,1,0:T(8,128)(2,1)S(1)}, bf16[8,2,16,512]{3,2,1,0:T(8,128)(2,1)S(1)}, u32[]{:S(2)}, u32[]{:S(2)}) collective-permute-start(bf16[8,2,16,512]{3,2,1,0:T(8,128)(2,1)S(1)} %pad_maximum_fusion.2.refs_4_), channel_id=1, source_target_pairs={{0,2},{1,3},{2,0},{3,1},{4,6},{5,7},{6,4},{7,5},{8,10},{9,11},{10,... | collective-permute-start | bytes 786440 | tf_op jit(solution)/shard_map/ppermute | solution.py:330
  25.3 3.1 %shard_map.76 = (f32[4,768,512]{2,1,0:T(8,128)S(1)}, f32[4,768,512]{2,1,0:T(8,128)S(1)}, f32[4,8,512]{2,1,0:T(8,128)S(1)}) custom-call(s32[1]{0:T(128)} %bitcast.refs_0_, f32[1]{0:T(128)} %bitcast.6.refs_1_, bf16[2,256,512]{2,1,0:T(8,128)(2,1)S(1)} %pad_maximum_fusion.1.refs_2_.refs_1_, bf16[2,256,512]{2,1,0:T(8,128)(2,1)S(1)} %pad_maximum_fusion.refs_3_.refs_2_, ...), custom_call_target="tpu_custom_call" | custom-call | flops 17179869184 | bytes 12582912 | tf_op jit(solution)/shard_map/pallas_call | solution.py:248
  28.4 3.2 %collective-permute-done.7.refs_5_ = bf16[8,2,16,512]{3,2,1,0:T(8,128)(2,1)S(1)} collective-permute-done((bf16[8,2,16,512]{3,2,1,0:T(8,128)(2,1)S(1)}, bf16[8,2,16,512]{3,2,1,0:T(8,128)(2,1)S(1)}, u32[]{:S(2)}, u32[]{:S(2)}) %collective-permute-start.7) | collective-permute-done | bytes 262176 | tf_op jit(solution)/shard_map/ppermute | solution.py:330
  31.6 1.5 %collective-permute-done.9.refs_7_ = bf16[8,2,16,512]{3,2,1,0:T(8,128)(2,1)S(1)} collective-permute-done((bf16[8,2,16,512]{3,2,1,0:T(8,128)(2,1)S(1)}, bf16[8,2,16,512]{3,2,1,0:T(8,128)(2,1)S(1)}, u32[]{:S(2)}, u32[]{:S(2)}) %collective-permute-start.9) | collective-permute-done | bytes 262176 | tf_op jit(solution)/shard_map/ppermute | solution.py:330
  33.1 4.2 %shard_map.77 = (f32[4,8,512]{2,1,0:T(8,128)S(1)}, f32[4,128,256]{2,1,0:T(8,128)S(1)}, f32[8,2,16,512]{3,2,1,0:T(8,128)S(1)}, f32[8,2,16,512]{3,2,1,0:T(8,128)S(...) custom-call(s32[1]{0:T(128)} %bitcast.refs_0_, s32[2,16]{1,0:T(2,128)S(1)} %fusion.9.refs_1_, ...), custom_call_target="tpu_custom_call" | custom-call | flops 1073741824 | bytes 4194304 | tf_op jit(solution)/shard_map/pallas_call | solution.py:248
  37.9 1.0 %collective-permute-done.10 = bf16[8,2,16,512]{3,2,1,0:T(8,128)(2,1)S(1)} collective-permute-done((bf16[8,2,16,512]{3,2,1,0:T(8,128)(2,1)S(1)}, bf16[8,2,16,512]{3,2,1,0:T(8,128)(2,1)S(1)}, u32[]{:S(2)}, u32[]{:S(2)}) %collective-permute-start.10) | collective-permute-done | bytes 262176 | tf_op jit(solution)/shard_map/ppermute | solution.py:330
  39.0 1.8 %collective-permute-start.12 = (bf16[8,2,16,512]{3,2,1,0:T(8,128)(2,1)S(1)}, bf16[8,2,16,512]{3,2,1,0:T(8,128)(2,1)S(1)}, u32[]{:S(2)}, u32[]{:S(2)}) collective-permute-start(bf16[8,2,16,512]{3,2,1,0:T(8,128)(2,1)S(1)} %add_convert_fusion), channel_id=1, source_target_pairs={{0,2},{1,3},{2,0},{3,1},{4,6},{5,7},{6,4},{7,5},{8,10},{9,11},{10,... | collective-permute-start | bytes 786440 | tf_op jit(solution)/shard_map/ppermute | solution.py:330
  40.8 4.7 %shard_map.78 = (f32[256,512]{1,0:T(8,128)}, f32[256,512]{1,0:T(8,128)S(1)}, f32[256,512]{1,0:T(8,128)S(1)}, bf16[2,256,512]{2,1,0:T(8,128)(2,1)S(1)}, bf16[2,256,512]{2,1,0:T(8,128)(2,1)S(1)}) custom-call(s32[1]{0:T(128)} %bitcast.refs_0_, bf16[2,256,512]{2,1,0:T(8,128)(2,1)S(1)} %pad_maximum_fusion.1.refs_2_.refs_1_, ...), custom_call_target="tpu_custom_call" | custom-call | flops 17179869184 | bytes 14680064 | tf_op jit(solution)/shard_map/pallas_call | solution.py:248
  45.5 1.9 %collective-permute-done.12 = bf16[8,2,16,512]{3,2,1,0:T(8,128)(2,1)S(1)} collective-permute-done((bf16[8,2,16,512]{3,2,1,0:T(8,128)(2,1)S(1)}, bf16[8,2,16,512]{3,2,1,0:T(8,128)(2,1)S(1)}, u32[]{:S(2)}, u32[]{:S(2)}) %collective-permute-start.12) | collective-permute-done | bytes 262176 | tf_op jit(solution)/shard_map/ppermute | solution.py:330
  47.6 1.8 %collective-permute-start.14 = (bf16[4,2,16,512]{3,2,1,0:T(8,128)(2,1)S(1)}, bf16[4,2,16,512]{3,2,1,0:T(8,128)(2,1)S(1)}, u32[]{:S(2)}, u32[]{:S(2)}) collective-permute-start(bf16[4,2,16,512]{3,2,1,0:T(8,128)(2,1)S(1)} %slice.143), channel_id=1, source_target_pairs={{0,4},{1,5},{2,6},{3,7},{4,0},{5,1},{6,2},{7,3},{8,12},{9,13},{10,... | collective-permute-start | bytes 393224 | tf_op jit(solution)/shard_map/ppermute | solution.py:330
  50.0 2.6 %collective-permute-done.14 = bf16[4,2,16,512]{3,2,1,0:T(8,128)(2,1)S(1)} collective-permute-done((bf16[4,2,16,512]{3,2,1,0:T(8,128)(2,1)S(1)}, bf16[4,2,16,512]{3,2,1,0:T(8,128)(2,1)S(1)}, u32[]{:S(2)}, u32[]{:S(2)}) %collective-permute-start.14) | collective-permute-done | bytes 131104 | tf_op jit(solution)/shard_map/ppermute | solution.py:330
  52.7 2.1 %collective-permute-start.15 = (bf16[2,2,16,512]{3,2,1,0:T(8,128)(2,1)S(1)}, bf16[2,2,16,512]{3,2,1,0:T(8,128)(2,1)S(1)}, u32[]{:S(2)}, u32[]{:S(2)}) collective-permute-start(bf16[2,2,16,512]{3,2,1,0:T(8,128)(2,1)S(1)} %slice.144), channel_id=1, source_target_pairs={{0,16},{1,17},{2,18},{3,19},{4,20},{5,21},{6,22},{7,23},{8,24},{9,... | collective-permute-start | bytes 196616 | tf_op jit(solution)/shard_map/ppermute | solution.py:330
  54.8 7.8 %collective-permute-done.15 = bf16[2,2,16,512]{3,2,1,0:T(8,128)(2,1)S(1)} collective-permute-done((bf16[2,2,16,512]{3,2,1,0:T(8,128)(2,1)S(1)}, bf16[2,2,16,512]{3,2,1,0:T(8,128)(2,1)S(1)}, u32[]{:S(2)}, u32[]{:S(2)}) %collective-permute-start.15) | collective-permute-done | bytes 65568 | tf_op jit(solution)/shard_map/ppermute | solution.py:330
  63.3 3.4 %collective-permute-done.17 = bf16[1,2,16,512]{3,2,1,0:T(8,128)(2,1)S(1)} collective-permute-done((bf16[1,2,16,512]{3,2,1,0:T(8,128)(2,1)S(1)}, bf16[1,2,16,512]{3,2,1,0:T(8,128)(2,1)S(1)}, u32[]{:S(2)}, u32[]{:S(2)}) %collective-permute-start.17) | collective-permute-done | bytes 32800 | tf_op jit(solution)/shard_map/ppermute | solution.py:330
  67.0 0.8 %copy-done = f32[256,512]{1,0:T(8,128)} copy-done((f32[256,512]{1,0:T(8,128)}, f32[256,512]{1,0:T(8,128)S(1)}, u32[]{:S(2)}) %copy-start) | copy-done | bytes 524312
  (40 shorter events, 4.8 us)
Async XLA Ops:
  1.4 6.7 %collective-permute-start.1 = (bf16[1,2,16,512]{3,2,1,0:T(8,128)(2,1)S(1)}, bf16[1,2,16,512]{3,2,1,0:T(8,128)(2,1)S(1)}, u32[]{:S(2)}, u32[]{:S(2)}) collective-permute-start(bf16[1,2,16,512]{3,2,1,0:T(8,128)(2,1)S(1)} %fusion.5), channel_id=1, source_target_pairs={{0,8},{1,9},{2,10},{3,11},{4,12},{5,13},{6,14},{7,15},{8,0},{9,1},... | collective-permute-start | bytes 98312 | tf_op jit(solution)/shard_map/ppermute | solution.py:330
  4.4 11.6 %collective-permute-start.3 = (bf16[256,512]{1,0:T(8,128)(2,1)}, bf16[256,512]{1,0:T(8,128)(2,1)S(1)}, u32[]{:S(2)}, u32[]{:S(2)}) collective-permute-start(bf16[256,512]{1,0:T(8,128)(2,1)} %param.10), channel_id=1, source_target_pairs={{1,2},{3,4},{5,6},{7,8},{9,10},{11,12},{13,14},{15,16},{17,18},{19... | collective-permute-start | bytes 786440 | tf_op jit(solution)/shard_map/ppermute | solution.py:335
  5.1 20.2 %collective-permute-start = (bf16[256,512]{1,0:T(8,128)(2,1)}, bf16[256,512]{1,0:T(8,128)(2,1)S(1)}, u32[]{:S(2)}, u32[]{:S(2)}) collective-permute-start(bf16[256,512]{1,0:T(8,128)(2,1)} %param.10), channel_id=1, source_target_pairs={{0,1},{1,0},{2,3},{3,2},{4,5},{5,4},{6,7},{7,6},{8,9},{9,8},{10,11... | collective-permute-start | bytes 786440 | tf_op jit(solution)/shard_map/ppermute | solution.py:330
  8.0 17.3 %collective-permute-start.4 = (bf16[256,512]{1,0:T(8,128)(2,1)}, bf16[256,512]{1,0:T(8,128)(2,1)S(1)}, u32[]{:S(2)}, u32[]{:S(2)}) collective-permute-start(bf16[256,512]{1,0:T(8,128)(2,1)} %param.11), channel_id=1, source_target_pairs={{0,1},{1,0},{2,3},{3,2},{4,5},{5,4},{6,7},{7,6},{8,9},{9,8},{10,11... | collective-permute-start | bytes 786440 | tf_op jit(solution)/shard_map/ppermute | solution.py:330
  8.1 7.9 %collective-permute-start.2 = (bf16[2,2,16,512]{3,2,1,0:T(8,128)(2,1)S(1)}, bf16[2,2,16,512]{3,2,1,0:T(8,128)(2,1)S(1)}, u32[]{:S(2)}, u32[]{:S(2)}) collective-permute-start(bf16[2,2,16,512]{3,2,1,0:T(8,128)(2,1)S(1)} %pad_maximum_fusion.4), channel_id=1, source_target_pairs={{0,16},{1,17},{2,18},{3,19},{4,20},{5,21},{6,22},{7,23},{8,24},{9,... | collective-permute-start | bytes 196616 | tf_op jit(solution)/shard_map/ppermute | solution.py:330
  11.7 10.5 %collective-permute-start.6 = (bf16[256,512]{1,0:T(8,128)(2,1)}, bf16[256,512]{1,0:T(8,128)(2,1)S(1)}, u32[]{:S(2)}, u32[]{:S(2)}) collective-permute-start(bf16[256,512]{1,0:T(8,128)(2,1)} %param.11), channel_id=1, source_target_pairs={{1,2},{3,4},{5,6},{7,8},{9,10},{11,12},{13,14},{15,16},{17,18},{19... | collective-permute-start | bytes 786440 | tf_op jit(solution)/shard_map/ppermute | solution.py:335
  16.0 6.2 %collective-permute-start.5 = (bf16[4,2,16,512]{3,2,1,0:T(8,128)(2,1)S(1)}, bf16[4,2,16,512]{3,2,1,0:T(8,128)(2,1)S(1)}, u32[]{:S(2)}, u32[]{:S(2)}) collective-permute-start(bf16[4,2,16,512]{3,2,1,0:T(8,128)(2,1)S(1)} %pad_maximum_fusion.3), channel_id=1, source_target_pairs={{0,4},{1,5},{2,6},{3,7},{4,0},{5,1},{6,2},{7,3},{8,12},{9,13},{10,... | collective-permute-start | bytes 393224 | tf_op jit(solution)/shard_map/ppermute | solution.py:330
  22.2 9.3 %collective-permute-start.7 = (bf16[8,2,16,512]{3,2,1,0:T(8,128)(2,1)S(1)}, bf16[8,2,16,512]{3,2,1,0:T(8,128)(2,1)S(1)}, u32[]{:S(2)}, u32[]{:S(2)}) collective-permute-start(bf16[8,2,16,512]{3,2,1,0:T(8,128)(2,1)S(1)} %pad_maximum_fusion.2.refs_4_), channel_id=1, source_target_pairs={{0,2},{1,3},{2,0},{3,1},{4,6},{5,7},{6,4},{7,5},{8,10},{9,11},{10,... | collective-permute-start | bytes 786440 | tf_op jit(solution)/shard_map/ppermute | solution.py:330
  25.2 6.3 %collective-permute-start.8 = (bf16[8,2,16,512]{3,2,1,0:T(8,128)(2,1)S(1)}, bf16[8,2,16,512]{3,2,1,0:T(8,128)(2,1)S(1)}, u32[]{:S(2)}, u32[]{:S(2)}) collective-permute-start(bf16[8,2,16,512]{3,2,1,0:T(8,128)(2,1)S(1)} %pad_maximum_fusion.2.refs_4_), channel_id=1, source_target_pairs={{0,1},{1,0},{2,3},{3,2},{4,5},{5,4},{6,7},{7,6},{8,9},{9,8},{10,11... | collective-permute-start | bytes 786440 | tf_op jit(solution)/shard_map/ppermute | solution.py:330
  25.3 6.3 %copy-start.2 = (s32[2,16]{1,0:T(2,128)S(1)}, s32[2,16]{1,0:T(2,128)}, u32[]{:S(2)}) copy-start(s32[2,16]{1,0:T(2,128)} %param.13) | copy-start | bytes 388
  31.5 1.5 %collective-permute-start.9 = (bf16[8,2,16,512]{3,2,1,0:T(8,128)(2,1)S(1)}, bf16[8,2,16,512]{3,2,1,0:T(8,128)(2,1)S(1)}, u32[]{:S(2)}, u32[]{:S(2)}) collective-permute-start(bf16[8,2,16,512]{3,2,1,0:T(8,128)(2,1)S(1)} %collective-permute-done.7.refs_5_), channel_id=1, source_target_pairs={{0,1},{1,0},{2,3},{3,2},{4,5},{5,4},{6,7},{7,6},{8,9},{9,8},{10,11... | collective-permute-start | bytes 786440 | tf_op jit(solution)/shard_map/ppermute | solution.py:330
  37.3 1.6 %collective-permute-start.10 = (bf16[8,2,16,512]{3,2,1,0:T(8,128)(2,1)S(1)}, bf16[8,2,16,512]{3,2,1,0:T(8,128)(2,1)S(1)}, u32[]{:S(2)}, u32[]{:S(2)}) collective-permute-start(bf16[8,2,16,512]{3,2,1,0:T(8,128)(2,1)S(1)} %get-tuple-element.67), channel_id=1, source_target_pairs={{0,1},{1,0},{2,3},{3,2},{4,5},{5,4},{6,7},{7,6},{8,9},{9,8},{10,11... | collective-permute-start | bytes 786440 | tf_op jit(solution)/shard_map/ppermute | solution.py:330
  37.5 8.0 %collective-permute-start.11 = (bf16[8,2,16,512]{3,2,1,0:T(8,128)(2,1)S(1)}, bf16[8,2,16,512]{3,2,1,0:T(8,128)(2,1)S(1)}, u32[]{:S(2)}, u32[]{:S(2)}) collective-permute-start(bf16[8,2,16,512]{3,2,1,0:T(8,128)(2,1)S(1)} %get-tuple-element.74), channel_id=1, source_target_pairs={{0,1},{1,0},{2,3},{3,2},{4,5},{5,4},{6,7},{7,6},{8,9},{9,8},{10,11... | collective-permute-start | bytes 786440 | tf_op jit(solution)/shard_map/ppermute | solution.py:330
  39.0 8.4 %collective-permute-start.12 = (bf16[8,2,16,512]{3,2,1,0:T(8,128)(2,1)S(1)}, bf16[8,2,16,512]{3,2,1,0:T(8,128)(2,1)S(1)}, u32[]{:S(2)}, u32[]{:S(2)}) collective-permute-start(bf16[8,2,16,512]{3,2,1,0:T(8,128)(2,1)S(1)} %add_convert_fusion), channel_id=1, source_target_pairs={{0,2},{1,3},{2,0},{3,1},{4,6},{5,7},{6,4},{7,5},{8,10},{9,11},{10,... | collective-permute-start | bytes 786440 | tf_op jit(solution)/shard_map/ppermute | solution.py:330
  47.6 5.0 %collective-permute-start.14 = (bf16[4,2,16,512]{3,2,1,0:T(8,128)(2,1)S(1)}, bf16[4,2,16,512]{3,2,1,0:T(8,128)(2,1)S(1)}, u32[]{:S(2)}, u32[]{:S(2)}) collective-permute-start(bf16[4,2,16,512]{3,2,1,0:T(8,128)(2,1)S(1)} %slice.143), channel_id=1, source_target_pairs={{0,4},{1,5},{2,6},{3,7},{4,0},{5,1},{6,2},{7,3},{8,12},{9,13},{10,... | collective-permute-start | bytes 393224 | tf_op jit(solution)/shard_map/ppermute | solution.py:330
  49.3 13.9 %collective-permute-start.16 = (bf16[2,256,512]{2,1,0:T(8,128)(2,1)S(1)}, bf16[2,256,512]{2,1,0:T(8,128)(2,1)S(1)}, u32[]{:S(2)}, u32[]{:S(2)}) collective-permute-start(bf16[2,256,512]{2,1,0:T(8,128)(2,1)S(1)} %get-tuple-element.79), channel_id=1, source_target_pairs={{1,2},{3,4},{5,6},{7,8},{9,10},{11,12},{13,14},{15,16},{17,18},{19... | collective-permute-start | bytes 1572872 | tf_op jit(solution)/shard_map/ppermute | solution.py:335
  52.7 10.0 %collective-permute-start.15 = (bf16[2,2,16,512]{3,2,1,0:T(8,128)(2,1)S(1)}, bf16[2,2,16,512]{3,2,1,0:T(8,128)(2,1)S(1)}, u32[]{:S(2)}, u32[]{:S(2)}) collective-permute-start(bf16[2,2,16,512]{3,2,1,0:T(8,128)(2,1)S(1)} %slice.144), channel_id=1, source_target_pairs={{0,16},{1,17},{2,18},{3,19},{4,20},{5,21},{6,22},{7,23},{8,24},{9,... | collective-permute-start | bytes 196616 | tf_op jit(solution)/shard_map/ppermute | solution.py:330
  54.8 11.9 %collective-permute-start.13 = (bf16[2,256,512]{2,1,0:T(8,128)(2,1)S(1)}, bf16[2,256,512]{2,1,0:T(8,128)(2,1)S(1)}, u32[]{:S(2)}, u32[]{:S(2)}) collective-permute-start(bf16[2,256,512]{2,1,0:T(8,128)(2,1)S(1)} %get-tuple-element.77), channel_id=1, source_target_pairs={{0,1},{1,0},{2,3},{3,2},{4,5},{5,4},{6,7},{7,6},{8,9},{9,8},{10,11... | collective-permute-start | bytes 1572872 | tf_op jit(solution)/shard_map/ppermute | solution.py:330
  62.6 4.0 %collective-permute-start.17 = (bf16[1,2,16,512]{3,2,1,0:T(8,128)(2,1)S(1)}, bf16[1,2,16,512]{3,2,1,0:T(8,128)(2,1)S(1)}, u32[]{:S(2)}, u32[]{:S(2)}) collective-permute-start(bf16[1,2,16,512]{3,2,1,0:T(8,128)(2,1)S(1)} %slice.145), channel_id=1, source_target_pairs={{0,8},{1,9},{2,10},{3,11},{4,12},{5,13},{6,14},{7,15},{8,0},{9,1},... | collective-permute-start | bytes 98312 | tf_op jit(solution)/shard_map/ppermute | solution.py:330
  66.9 0.8 %copy-start = (f32[256,512]{1,0:T(8,128)}, f32[256,512]{1,0:T(8,128)S(1)}, u32[]{:S(2)}) copy-start(f32[256,512]{1,0:T(8,128)S(1)} %get-tuple-element.85) | copy-start | bytes 1572868
  67.0 1.0 %copy-start.1 = (f32[256,512]{1,0:T(8,128)}, f32[256,512]{1,0:T(8,128)S(1)}, u32[]{:S(2)}) copy-start(f32[256,512]{1,0:T(8,128)S(1)} %get-tuple-element.86) | copy-start | bytes 1572868

commit v4 on v3

--- a/solution.py
+++ b/solution.py
@@ -18,7 +18,6 @@
 SCALE = HEAD_DIM**-0.5
 NT = (((1,), (1,)), ((), ()))
 BF16, F32 = jnp.bfloat16, jnp.float32
-SETS = 2
 
 
 def tile(h, i):
@@ -75,7 +74,7 @@
     return slice(i * BLOCK, i * BLOCK + SPAN)
 
 
-def window_kernel(
+def window_products(
     flags, biases, pair, own, mate_k, across_k, mate_v, across_v,
     near_s, near_d, stats,
     ext_k, ext_v, q_two, g_two,
@@ -93,6 +92,13 @@
         near_d[0, :, heads] = lax.dot_general(
             ext_v[...], g_two[heads], NT, preferred_element_type=F32
         )
+
+
+def window_stats(
+    flags, biases, pair, own, mate_k, across_k, mate_v, across_v,
+    near_s, near_d, stats,
+    ext_k, ext_v, q_two, g_two,
+):
     for h in range(2):
         for i in range(2):
             s = near_s[0, near_rows(i), tile(h, i)]
@@ -104,10 +110,10 @@
             stats[0, 2:3, stat(h, i)] = column_sum(u * d)
 
 
-def stripe_kernel(
+def stripe_products(
     flags, slots, pair, stats, table_a, table_b, table_c, table_d,
     coefs, far_query, keep_a, keep_b, send_a, send_b,
-    far_k, far_v, q_two, g_two, far_probs, far_scores, table_sum,
+    far_k, far_v, q_two, g_two, far_s, far_d, far_probs, far_scores, table_sum,
 ):
     flip = flags[0]
     part = table_a.shape[0]
@@ -124,16 +130,19 @@
                 )
     split_blocks(pair, 0, flip, q_two)
     split_blocks(pair, 1, flip, g_two)
-    s, d = (
-        jnp.concatenate(
-            [
-                lax.dot_general(far[i], two[both(i)], NT, preferred_element_type=F32)
-                for i in range(2)
-            ],
-            axis=1,
-        )
-        for far, two in ((far_k, q_two), (far_v, g_two))
-    )
+    for far, two, out in ((far_k, q_two, far_s), (far_v, g_two, far_d)):
+        for i in range(2):
+            out[:, both(i)] = lax.dot_general(
+                far[i], two[both(i)], NT, preferred_element_type=F32
+            )
+
+
+def stripe_probs(
+    flags, slots, pair, stats, table_a, table_b, table_c, table_d,
+    coefs, far_query, keep_a, keep_b, send_a, send_b,
+    far_k, far_v, q_two, g_two, far_s, far_d, far_probs, far_scores, table_sum,
+):
+    s, d = far_s[...], far_d[...]
     near_top = stats[0, 0:1]
     top = jnp.maximum(near_top, column_max(s))
     shrink = jnp.exp(near_top - top)
@@ -146,6 +155,15 @@
     p = u * inv
     far_probs[...] = p.astype(BF16)
     far_scores[...] = (p * (d - dot)).astype(BF16)
+
+
+def stripe_gradients(
+    flags, slots, pair, stats, table_a, table_b, table_c, table_d,
+    coefs, far_query, keep_a, keep_b, send_a, send_b,
+    far_k, far_v, q_two, g_two, far_s, far_d, far_probs, far_scores, table_sum,
+):
+    flip = flags[0]
+    part = table_a.shape[0]
     table_sum[...] = jnp.zeros_like(table_sum)
     for which, left, right in ((0, far_scores, q_two), (1, far_probs, g_two)):
         for i in range(2):
@@ -169,9 +187,9 @@
         far_query[0, HEAD_DIM:, rows] = out[HEAD_DIM:, BLOCK:]
 
 
-def gradient_kernel(
+def window_probs(
     flags, pair, own, mate_k, across_k, near_s, near_d, coefs, far_query,
-    grad_query, grad_key, grad_value, grad_mate, grad_across,
+    grad_query, grad_key, grad_value, grad_mate, across_k_out, across_v_out,
     ext_k, q_two, g_two, probs, scores,
 ):
     flip = flags[0]
@@ -192,16 +210,24 @@
             probs[rows, tile(h, i)] = p.astype(BF16)
             ds = p * (near_d[0, rows, tile(h, i)] - coefs[0, 1:2, stat(h, i)])
             scores[rows, tile(h, i)] = ds.astype(BF16)
-    for which, left, right, grad_own in (
-        (0, scores, q_two, grad_key),
-        (1, probs, g_two, grad_value),
+
+
+def window_gradients(
+    flags, pair, own, mate_k, across_k, near_s, near_d, coefs, far_query,
+    grad_query, grad_key, grad_value, grad_mate, across_k_out, across_v_out,
+    ext_k, q_two, g_two, probs, scores,
+):
+    flip = flags[0]
+    for which, left, right, grad_own, grad_across in (
+        (1, probs, g_two, grad_value, across_v_out),
+        (0, scores, q_two, grad_key, across_k_out),
     ):
         total = jnp.dot(left[...], right[...], preferred_element_type=F32)
         for i in range(2):
             rows = block_rows(i, flip)
             grad_mate[which, rows] = total[tile(0, i)].astype(grad_mate.dtype)
             grad_own[rows] = total[tile(1, i)]
-            grad_across[which, rows] = total[tile(2, i)].astype(grad_across.dtype)
+            grad_across[rows] = total[tile(2, i)].astype(grad_across.dtype)
     k_t = jnp.transpose(ext_k[...])
     near = [
         jnp.dot(
@@ -236,22 +262,23 @@
     return ref
 
 
-def call(kernel, steps, in_kinds, out_kinds, out_shape, scratch, flops, moved, args):
+def call(phases, steps, in_kinds, out_kinds, out_shape, scratch, flops, moved, args):
     kinds = in_kinds + out_kinds
 
     def whole(*refs):
-        for p in range(steps):
-            views = [view(ref, kind, p) for ref, kind in zip(refs, kinds)]
-            first = len(kinds) + p % SETS * len(scratch)
-            kernel(*views, *refs[first : first + len(scratch)])
+        for phase in phases:
+            for p in range(steps):
+                views = [view(ref, kind, p) for ref, kind in zip(refs, kinds)]
+                first = len(kinds) + p * len(scratch)
+                phase(*views, *refs[first : first + len(scratch)])
 
     return pl.pallas_call(
         whole,
         in_specs=[SMEM_SPEC if kind == FULL else VMEM_SPEC for kind in in_kinds],
         out_specs=[VMEM_SPEC] * len(out_kinds),
         out_shape=[jax.ShapeDtypeStruct(shape, dtype) for shape, dtype in out_shape],
-        scratch_shapes=scratch * SETS,
-        compiler_params=pltpu.CompilerParams(vmem_limit_bytes=24 << 20),
+        scratch_shapes=scratch * steps,
+        compiler_params=pltpu.CompilerParams(vmem_limit_bytes=32 << 20),
         cost_estimate=pl.CostEstimate(flops=flops, bytes_accessed=moved, transcendentals=1 << 20),
     )(*args)
 
@@ -260,7 +287,7 @@
     steps = pair.shape[2] // LANES
     near = ((steps, EXT, 2 * ROWS), F32)
     return call(
-        window_kernel,
+        (window_products, window_stats),
         steps,
         [FULL, FULL, PAIR, PAIR, ROW, ROW, ROW, ROW],
         [STEP, STEP, STEP],
@@ -277,7 +304,7 @@
     width = pair.shape[2]
     steps = width // LANES
     return call(
-        stripe_kernel,
+        (stripe_products, stripe_probs, stripe_gradients),
         steps,
         [FULL, FULL, PAIR, STEP] + [TABLE] * 4,
         [STEP, STEP] + [TABLE] * 4,
@@ -289,6 +316,8 @@
             pltpu.VMEM((2, FAR, LANES), BF16),
             TWO,
             TWO,
+            pltpu.VMEM((FAR, 4 * BLOCK), F32),
+            pltpu.VMEM((FAR, 4 * BLOCK), F32),
             pltpu.VMEM((FAR, 4 * BLOCK), BF16),
             pltpu.VMEM((FAR, 4 * BLOCK), BF16),
             pltpu.VMEM((4 * part, 2, STRIPE, LANES), F32),
@@ -303,11 +332,11 @@
     width = pair.shape[2]
     steps = width // LANES
     return call(
-        gradient_kernel,
+        (window_probs, window_gradients),
         steps,
         [FULL, PAIR, PAIR, ROW, ROW, STEP, STEP, STEP, STEP],
-        [ROW, ROW, ROW, PAIR, PAIR],
-        [((ROWS, width), F32)] * 3 + [((2, ROWS, width), BF16)] * 2,
+        [ROW, ROW, ROW, PAIR, ROW, ROW],
+        [((ROWS, width), F32)] * 3 + [((2, ROWS, width), BF16)] + [((ROWS, width), BF16)] * 2,
         [
             EXTENT,
             TWO,
@@ -315,8 +344,8 @@
             pltpu.VMEM((EXT, 2 * ROWS), BF16),
             pltpu.VMEM((EXT, 2 * ROWS), BF16),
         ],
-        1 << 34,
-        14 << 20,
+        1 << 30,
+        1 << 20,
         (flags, pair, own, mate_k, across_k, near_s, near_d, coefs, far_query),
     )
 
@@ -374,22 +403,24 @@
     send = keep_b + swapped(send_b, count, core_bit).astype(F32)
     keep = keep_a + swapped(send_a, count, core_bit).astype(F32)
     send, coefs = lax.optimization_barrier((send.astype(BF16), coefs))
-    grad_query, grad_key, grad_value, grad_mate, grad_across = gradient_part(
+    grad_query, grad_key, grad_value, grad_mate, out_k, out_v = gradient_part(
         flags, pair, own, mate_k, across_k, near_s, near_d, coefs, far_query
     )
+    from_v, from_k = crossed(out_v, count), crossed(out_k, count)
     total = keep + swapped(send, count, x_bit).astype(F32)
     total, grad_mate = lax.optimization_barrier((total, grad_mate))
     from_mate = swapped(grad_mate, count, core_bit)
-    from_across = crossed(grad_across, count)
     for bit in (y_bit, *z_bits[::-1]):
         half = total.shape[0] // 2
         keep, send = total[:half], total[half:].astype(BF16)
+        if bit == z_bits[-1]:
+            keep, from_v = lax.optimization_barrier((keep, from_v))
         if bit == z_bits[0]:
-            keep, from_across = lax.optimization_barrier((keep, from_across))
+            keep, from_k = lax.optimization_barrier((keep, from_k))
         total = keep + swapped(send, count, bit).astype(F32)
     outs = []
     for which, grad_own in enumerate((grad_key, grad_value)):
-        base = grad_own + from_mate[which].astype(F32) + from_across[which].astype(F32)
+        base = grad_own + from_mate[which].astype(F32) + (from_k, from_v)[which].astype(F32)
         base = lax.optimization_barrier(base)
         outs.append(base.at[ROWS - STRIPE :].add(total[0, which]))
     return grad_query, outs[0], outs[1]

time: 68.3 us -> 66 us (0.966)
  waiting for transfers between devices: 28.4 us -> 26.6 us
  Pallas kernels: 12.1 us -> 11.1 us
    ppermute x15, waiting for transfers between devices: 28.4 us -> 26.6 us  [swapped(): return lax.ppermute(x, 'ctx', [(i, i ^ bit) for i in range(count)])]
    pallas_call x3, Pallas kernels: 12.1 us -> 11.1 us  [call(): pl.pallas_call(whole, in_specs=[SMEM_SPEC if kind == FULL else VMEM_SPEC...]
    ppermute x3 -> x4, starting transfers between devices: 2.02 us -> 2.67 us  [crossed(): return lax.ppermute(x, 'ctx', up + [(j, i) for i, j in up])]
  transfers between devices with their start and end apart: 18 -> 19, of which waited for: 9 -> 9; matrix products, arithmetic and copies ran while one was open for 5% -> 5% of each run, Pallas kernels for 11% -> 11%
where the time goes in v4:
time: 66 us; the launch traced here: 65.4 us
  waiting for transfers between devices  26.6 us (40%)
  starting transfers between devices  21.5 us (33%)
  Pallas kernels  11.1 us (17%)
  other arithmetic  4.33 us (7%)
  local copies, waits for them, and re-layouts  1.01 us (2%)
  between operations  0.86 us (1%)
    ppermute x15, waiting for transfers between devices, swapped(): return lax.ppermute(x, 'ctx', [(i, i ^ bit) for i in range(count)])  26.6 us
    ppermute x15, starting transfers between devices, swapped(): return lax.ppermute(x, 'ctx', [(i, i ^ bit) for i in range(count)])  18.8 us
    pallas_call x3, Pallas kernels, call(): pl.pallas_call(whole, in_specs=[SMEM_SPEC if kind == FULL else VMEM_SPEC...  11.1 us
    ppermute x4, starting transfers between devices, crossed(): return lax.ppermute(x, 'ctx', up + [(j, i) for i, j in up])  2.67 us
    another operation x2, other arithmetic, body(): pair = jnp.stack([query_rows * BF16(SCALE), grad_out])  1.98 us
  transfers between devices with their start and end apart: 19, of which 9 were waited for; matrix products, arithmetic and copies ran while one was open for 5% of the time, Pallas kernels for 11%

profile of v4, /device:TPU:0, one launch (start us, length us, event | category | flops | bytes accessed | tf_op | source)
XLA Modules:
  0.0 65.4 jit_solution(12473329295825977021)
XLA Ops:
  0.6 0.7 %fusion.7 = bf16[1,2,16,512]{3,2,1,0:T(8,128)(2,1)S(1)} fusion(bf16[1,256,512]{2,1,0:T(8,128)(2,1)} %bitcast.33, bf16[1,256,512]{2,1,0:T(8,128)(2,1)} %bitcast.31), kind=kLoop, calls=%fused_computation.29 | loop fusion | flops 16384 | bytes 557056 | tf_op jit(solution)/shard_map/broadcast_in_dim | solution.py:384
  1.4 3.0 %collective-permute-start.1 = (bf16[1,2,16,512]{3,2,1,0:T(8,128)(2,1)S(1)}, bf16[1,2,16,512]{3,2,1,0:T(8,128)(2,1)S(1)}, u32[]{:S(2)}, u32[]{:S(2)}) collective-permute-start(bf16[1,2,16,512]{3,2,1,0:T(8,128)(2,1)S(1)} %fusion.7), channel_id=1, source_target_pairs={{0,8},{1,9},{2,10},{3,11},{4,12},{5,13},{6,14},{7,15},{8,0},{9,1},... | collective-permute-start | bytes 98312 | tf_op jit(solution)/shard_map/ppermute | solution.py:359
  5.1 2.9 %collective-permute-start = (bf16[256,512]{1,0:T(8,128)(2,1)}, bf16[256,512]{1,0:T(8,128)(2,1)S(1)}, u32[]{:S(2)}, u32[]{:S(2)}) collective-permute-start(bf16[256,512]{1,0:T(8,128)(2,1)} %param.10), channel_id=1, source_target_pairs={{0,1},{1,0},{2,3},{3,2},{4,5},{5,4},{6,7},{7,6},{8,9},{9,8},{10,11... | collective-permute-start | bytes 786440 | tf_op jit(solution)/shard_map/ppermute | solution.py:359
  8.1 2.7 %collective-permute-start.2 = (bf16[2,2,16,512]{3,2,1,0:T(8,128)(2,1)S(1)}, bf16[2,2,16,512]{3,2,1,0:T(8,128)(2,1)S(1)}, u32[]{:S(2)}, u32[]{:S(2)}) collective-permute-start(bf16[2,2,16,512]{3,2,1,0:T(8,128)(2,1)S(1)} %pad_maximum_fusion.4), channel_id=1, source_target_pairs={{0,16},{1,17},{2,18},{3,19},{4,20},{5,21},{6,22},{7,23},{8,24},{9,... | collective-permute-start | bytes 196616 | tf_op jit(solution)/shard_map/ppermute | solution.py:359
  10.7 1.0 %multiply_bitcast_fusion = bf16[1,256,512]{2,1,0:T(8,128)(2,1)S(1)} fusion(bf16[256,512]{1,0:T(8,128)(2,1)} %param.9), kind=kLoop, calls=%fused_computation.15 | loop fusion | flops 131072 | bytes 524288 | tf_op jit(solution)/shard_map/stack | solution.py:380
  12.4 3.6 %collective-permute-done.2 = bf16[2,2,16,512]{3,2,1,0:T(8,128)(2,1)S(1)} collective-permute-done((bf16[2,2,16,512]{3,2,1,0:T(8,128)(2,1)S(1)}, bf16[2,2,16,512]{3,2,1,0:T(8,128)(2,1)S(1)}, u32[]{:S(2)}, u32[]{:S(2)}) %collective-permute-start.2) | collective-permute-done | bytes 65568 | tf_op jit(solution)/shard_map/ppermute | solution.py:359
  16.6 1.1 %pad_maximum_fusion.refs_3_.refs_2_ = bf16[2,256,512]{2,1,0:T(8,128)(2,1)S(1)} fusion(bf16[1,256,512]{2,1,0:T(8,128)(2,1)} %bitcast.34, bf16[1,256,512]{2,1,0:T(8,128)(2,1)} %bitcast.32), kind=kLoop, calls=%fused_computation.1 | loop fusion | flops 262144 | bytes 1048576 | tf_op jit(solution)/shard_map/stack | solution.py:381
  17.7 1.0 %pad_maximum_fusion.1.refs_2_.refs_1_ = bf16[2,256,512]{2,1,0:T(8,128)(2,1)S(1)} fusion(bf16[1,256,512]{2,1,0:T(8,128)(2,1)} %bitcast.35, bf16[1,256,512]{2,1,0:T(8,128)(2,1)S(1)} %multiply_bitcast_fusion), kind=kLoop, calls=%fused_computation.3 | loop fusion | flops 262144 | bytes 1048576 | tf_op jit(solution)/shard_map/stack | solution.py:380
  18.7 3.5 %collective-permute-done.5 = bf16[4,2,16,512]{3,2,1,0:T(8,128)(2,1)S(1)} collective-permute-done((bf16[4,2,16,512]{3,2,1,0:T(8,128)(2,1)S(1)}, bf16[4,2,16,512]{3,2,1,0:T(8,128)(2,1)S(1)}, u32[]{:S(2)}, u32[]{:S(2)}) %collective-permute-start.5) | collective-permute-done | bytes 131104 | tf_op jit(solution)/shard_map/ppermute | solution.py:359
  22.2 3.0 %collective-permute-start.7 = (bf16[8,2,16,512]{3,2,1,0:T(8,128)(2,1)S(1)}, bf16[8,2,16,512]{3,2,1,0:T(8,128)(2,1)S(1)}, u32[]{:S(2)}, u32[]{:S(2)}) collective-permute-start(bf16[8,2,16,512]{3,2,1,0:T(8,128)(2,1)S(1)} %pad_maximum_fusion.2.refs_4_), channel_id=1, source_target_pairs={{0,2},{1,3},{2,0},{3,1},{4,6},{5,7},{6,4},{7,5},{8,10},{9,11},{10,... | collective-permute-start | bytes 786440 | tf_op jit(solution)/shard_map/ppermute | solution.py:359
  25.3 3.1 %shard_map.76 = (f32[4,768,512]{2,1,0:T(8,128)S(1)}, f32[4,768,512]{2,1,0:T(8,128)S(1)}, f32[4,8,512]{2,1,0:T(8,128)S(1)}) custom-call(s32[1]{0:T(128)} %bitcast.refs_0_, f32[1]{0:T(128)} %bitcast.6.refs_1_, bf16[2,256,512]{2,1,0:T(8,128)(2,1)S(1)} %pad_maximum_fusion.1.refs_2_.refs_1_, bf16[2,256,512]{2,1,0:T(8,128)(2,1)S(1)} %pad_maximum_fusion.refs_3_.refs_2_, ...), custom_call_target="tpu_custom_call" | custom-call | flops 17179869184 | bytes 12582912 | tf_op jit(solution)/shard_map/pallas_call | solution.py:275
  28.3 3.2 %collective-permute-done.7.refs_5_ = bf16[8,2,16,512]{3,2,1,0:T(8,128)(2,1)S(1)} collective-permute-done((bf16[8,2,16,512]{3,2,1,0:T(8,128)(2,1)S(1)}, bf16[8,2,16,512]{3,2,1,0:T(8,128)(2,1)S(1)}, u32[]{:S(2)}, u32[]{:S(2)}) %collective-permute-start.7) | collective-permute-done | bytes 262176 | tf_op jit(solution)/shard_map/ppermute | solution.py:359
  31.6 1.5 %collective-permute-done.9.refs_7_ = bf16[8,2,16,512]{3,2,1,0:T(8,128)(2,1)S(1)} collective-permute-done((bf16[8,2,16,512]{3,2,1,0:T(8,128)(2,1)S(1)}, bf16[8,2,16,512]{3,2,1,0:T(8,128)(2,1)S(1)}, u32[]{:S(2)}, u32[]{:S(2)}) %collective-permute-start.9) | collective-permute-done | bytes 262176 | tf_op jit(solution)/shard_map/ppermute | solution.py:359
  33.1 4.1 %shard_map.77 = (f32[4,8,512]{2,1,0:T(8,128)S(1)}, f32[4,128,256]{2,1,0:T(8,128)S(1)}, f32[8,2,16,512]{3,2,1,0:T(8,128)S(1)}, f32[8,2,16,512]{3,2,1,0:T(8,128)S(...) custom-call(s32[1]{0:T(128)} %bitcast.refs_0_, s32[2,16]{1,0:T(2,128)S(1)} %fusion.11.refs_1_, ...), custom_call_target="tpu_custom_call" | custom-call | flops 1073741824 | bytes 4194304 | tf_op jit(solution)/shard_map/pallas_call | solution.py:275
  37.7 1.0 %collective-permute-done.10 = bf16[8,2,16,512]{3,2,1,0:T(8,128)(2,1)S(1)} collective-permute-done((bf16[8,2,16,512]{3,2,1,0:T(8,128)(2,1)S(1)}, bf16[8,2,16,512]{3,2,1,0:T(8,128)(2,1)S(1)}, u32[]{:S(2)}, u32[]{:S(2)}) %collective-permute-start.10) | collective-permute-done | bytes 262176 | tf_op jit(solution)/shard_map/ppermute | solution.py:359
  38.8 1.8 %collective-permute-start.12 = (bf16[8,2,16,512]{3,2,1,0:T(8,128)(2,1)S(1)}, bf16[8,2,16,512]{3,2,1,0:T(8,128)(2,1)S(1)}, u32[]{:S(2)}, u32[]{:S(2)}) collective-permute-start(bf16[8,2,16,512]{3,2,1,0:T(8,128)(2,1)S(1)} %add_convert_fusion), channel_id=1, source_target_pairs={{0,2},{1,3},{2,0},{3,1},{4,6},{5,7},{6,4},{7,5},{8,10},{9,11},{10,... | collective-permute-start | bytes 786440 | tf_op jit(solution)/shard_map/ppermute | solution.py:359
  40.6 4.0 %shard_map.78 = (f32[256,512]{1,0:T(8,128)}, f32[256,512]{1,0:T(8,128)S(1)}, f32[256,512]{1,0:T(8,128)S(1)}, bf16[2,256,512]{2,1,0:T(8,128)(2,1)S(1)}, bf16[256,...) custom-call(s32[1]{0:T(128)} %bitcast.refs_0_, bf16[2,256,512]{2,1,0:T(8,128)(2,1)S(1)} %pad_maximum_fusion.1.refs_2_.refs_1_, ...), custom_call_target="tpu_custom_call" | custom-call | flops 1073741824 | bytes 1048576 | tf_op jit(solution)/shard_map/pallas_call | solution.py:275
  44.6 2.7 %collective-permute-done.12 = bf16[8,2,16,512]{3,2,1,0:T(8,128)(2,1)S(1)} collective-permute-done((bf16[8,2,16,512]{3,2,1,0:T(8,128)(2,1)S(1)}, bf16[8,2,16,512]{3,2,1,0:T(8,128)(2,1)S(1)}, u32[]{:S(2)}, u32[]{:S(2)}) %collective-permute-start.12) | collective-permute-done | bytes 262176 | tf_op jit(solution)/shard_map/ppermute | solution.py:359
  47.4 1.8 %collective-permute-start.14 = (bf16[4,2,16,512]{3,2,1,0:T(8,128)(2,1)S(1)}, bf16[4,2,16,512]{3,2,1,0:T(8,128)(2,1)S(1)}, u32[]{:S(2)}, u32[]{:S(2)}) collective-permute-start(bf16[4,2,16,512]{3,2,1,0:T(8,128)(2,1)S(1)} %slice.132), channel_id=1, source_target_pairs={{0,4},{1,5},{2,6},{3,7},{4,0},{5,1},{6,2},{7,3},{8,12},{9,13},{10,... | collective-permute-start | bytes 393224 | tf_op jit(solution)/shard_map/ppermute | solution.py:359
  49.8 2.6 %collective-permute-done.14 = bf16[4,2,16,512]{3,2,1,0:T(8,128)(2,1)S(1)} collective-permute-done((bf16[4,2,16,512]{3,2,1,0:T(8,128)(2,1)S(1)}, bf16[4,2,16,512]{3,2,1,0:T(8,128)(2,1)S(1)}, u32[]{:S(2)}, u32[]{:S(2)}) %collective-permute-start.14) | collective-permute-done | bytes 131104 | tf_op jit(solution)/shard_map/ppermute | solution.py:359
  52.5 2.1 %collective-permute-start.16 = (bf16[2,2,16,512]{3,2,1,0:T(8,128)(2,1)S(1)}, bf16[2,2,16,512]{3,2,1,0:T(8,128)(2,1)S(1)}, u32[]{:S(2)}, u32[]{:S(2)}) collective-permute-start(bf16[2,2,16,512]{3,2,1,0:T(8,128)(2,1)S(1)} %slice.133), channel_id=1, source_target_pairs={{0,16},{1,17},{2,18},{3,19},{4,20},{5,21},{6,22},{7,23},{8,24},{9,... | collective-permute-start | bytes 196616 | tf_op jit(solution)/shard_map/ppermute | solution.py:359
  55.3 4.3 %collective-permute-done.16 = bf16[2,2,16,512]{3,2,1,0:T(8,128)(2,1)S(1)} collective-permute-done((bf16[2,2,16,512]{3,2,1,0:T(8,128)(2,1)S(1)}, bf16[2,2,16,512]{3,2,1,0:T(8,128)(2,1)S(1)}, u32[]{:S(2)}, u32[]{:S(2)}) %collective-permute-start.16) | collective-permute-done | bytes 65568 | tf_op jit(solution)/shard_map/ppermute | solution.py:359
  59.9 4.2 %collective-permute-done.18 = bf16[1,2,16,512]{3,2,1,0:T(8,128)(2,1)S(1)} collective-permute-done((bf16[1,2,16,512]{3,2,1,0:T(8,128)(2,1)S(1)}, bf16[1,2,16,512]{3,2,1,0:T(8,128)(2,1)S(1)}, u32[]{:S(2)}, u32[]{:S(2)}) %collective-permute-start.18) | collective-permute-done | bytes 32800 | tf_op jit(solution)/shard_map/ppermute | solution.py:359
  64.4 0.8 %copy-done = f32[256,512]{1,0:T(8,128)} copy-done((f32[256,512]{1,0:T(8,128)}, f32[256,512]{1,0:T(8,128)S(1)}, u32[]{:S(2)}) %copy-start) | copy-done | bytes 524312
  (43 shorter events, 5.0 us)
Async XLA Ops:
  1.4 6.7 %collective-permute-start.1 = (bf16[1,2,16,512]{3,2,1,0:T(8,128)(2,1)S(1)}, bf16[1,2,16,512]{3,2,1,0:T(8,128)(2,1)S(1)}, u32[]{:S(2)}, u32[]{:S(2)}) collective-permute-start(bf16[1,2,16,512]{3,2,1,0:T(8,128)(2,1)S(1)} %fusion.7), channel_id=1, source_target_pairs={{0,8},{1,9},{2,10},{3,11},{4,12},{5,13},{6,14},{7,15},{8,0},{9,1},... | collective-permute-start | bytes 98312 | tf_op jit(solution)/shard_map/ppermute | solution.py:359
  4.4 11.6 %collective-permute-start.3 = (bf16[256,512]{1,0:T(8,128)(2,1)}, bf16[256,512]{1,0:T(8,128)(2,1)S(1)}, u32[]{:S(2)}, u32[]{:S(2)}) collective-permute-start(bf16[256,512]{1,0:T(8,128)(2,1)} %param.10), channel_id=1, source_target_pairs={{1,2},{3,4},{5,6},{7,8},{9,10},{11,12},{13,14},{15,16},{17,18},{19... | collective-permute-start | bytes 786440 | tf_op jit(solution)/shard_map/ppermute | solution.py:364
  5.1 20.2 %collective-permute-start = (bf16[256,512]{1,0:T(8,128)(2,1)}, bf16[256,512]{1,0:T(8,128)(2,1)S(1)}, u32[]{:S(2)}, u32[]{:S(2)}) collective-permute-start(bf16[256,512]{1,0:T(8,128)(2,1)} %param.10), channel_id=1, source_target_pairs={{0,1},{1,0},{2,3},{3,2},{4,5},{5,4},{6,7},{7,6},{8,9},{9,8},{10,11... | collective-permute-start | bytes 786440 | tf_op jit(solution)/shard_map/ppermute | solution.py:359
  8.0 17.3 %collective-permute-start.4 = (bf16[256,512]{1,0:T(8,128)(2,1)}, bf16[256,512]{1,0:T(8,128)(2,1)S(1)}, u32[]{:S(2)}, u32[]{:S(2)}) collective-permute-start(bf16[256,512]{1,0:T(8,128)(2,1)} %param.11), channel_id=1, source_target_pairs={{0,1},{1,0},{2,3},{3,2},{4,5},{5,4},{6,7},{7,6},{8,9},{9,8},{10,11... | collective-permute-start | bytes 786440 | tf_op jit(solution)/shard_map/ppermute | solution.py:359
  8.1 7.9 %collective-permute-start.2 = (bf16[2,2,16,512]{3,2,1,0:T(8,128)(2,1)S(1)}, bf16[2,2,16,512]{3,2,1,0:T(8,128)(2,1)S(1)}, u32[]{:S(2)}, u32[]{:S(2)}) collective-permute-start(bf16[2,2,16,512]{3,2,1,0:T(8,128)(2,1)S(1)} %pad_maximum_fusion.4), channel_id=1, source_target_pairs={{0,16},{1,17},{2,18},{3,19},{4,20},{5,21},{6,22},{7,23},{8,24},{9,... | collective-permute-start | bytes 196616 | tf_op jit(solution)/shard_map/ppermute | solution.py:359
  11.7 10.5 %collective-permute-start.6 = (bf16[256,512]{1,0:T(8,128)(2,1)}, bf16[256,512]{1,0:T(8,128)(2,1)S(1)}, u32[]{:S(2)}, u32[]{:S(2)}) collective-permute-start(bf16[256,512]{1,0:T(8,128)(2,1)} %param.11), channel_id=1, source_target_pairs={{1,2},{3,4},{5,6},{7,8},{9,10},{11,12},{13,14},{15,16},{17,18},{19... | collective-permute-start | bytes 786440 | tf_op jit(solution)/shard_map/ppermute | solution.py:364
  16.0 6.2 %collective-permute-start.5 = (bf16[4,2,16,512]{3,2,1,0:T(8,128)(2,1)S(1)}, bf16[4,2,16,512]{3,2,1,0:T(8,128)(2,1)S(1)}, u32[]{:S(2)}, u32[]{:S(2)}) collective-permute-start(bf16[4,2,16,512]{3,2,1,0:T(8,128)(2,1)S(1)} %pad_maximum_fusion.3), channel_id=1, source_target_pairs={{0,4},{1,5},{2,6},{3,7},{4,0},{5,1},{6,2},{7,3},{8,12},{9,13},{10,... | collective-permute-start | bytes 393224 | tf_op jit(solution)/shard_map/ppermute | solution.py:359
  22.2 9.3 %collective-permute-start.7 = (bf16[8,2,16,512]{3,2,1,0:T(8,128)(2,1)S(1)}, bf16[8,2,16,512]{3,2,1,0:T(8,128)(2,1)S(1)}, u32[]{:S(2)}, u32[]{:S(2)}) collective-permute-start(bf16[8,2,16,512]{3,2,1,0:T(8,128)(2,1)S(1)} %pad_maximum_fusion.2.refs_4_), channel_id=1, source_target_pairs={{0,2},{1,3},{2,0},{3,1},{4,6},{5,7},{6,4},{7,5},{8,10},{9,11},{10,... | collective-permute-start | bytes 786440 | tf_op jit(solution)/shard_map/ppermute | solution.py:359
  25.2 6.3 %collective-permute-start.8 = (bf16[8,2,16,512]{3,2,1,0:T(8,128)(2,1)S(1)}, bf16[8,2,16,512]{3,2,1,0:T(8,128)(2,1)S(1)}, u32[]{:S(2)}, u32[]{:S(2)}) collective-permute-start(bf16[8,2,16,512]{3,2,1,0:T(8,128)(2,1)S(1)} %pad_maximum_fusion.2.refs_4_), channel_id=1, source_target_pairs={{0,1},{1,0},{2,3},{3,2},{4,5},{5,4},{6,7},{7,6},{8,9},{9,8},{10,11... | collective-permute-start | bytes 786440 | tf_op jit(solution)/shard_map/ppermute | solution.py:359
  25.3 6.3 %copy-start.2 = (s32[2,16]{1,0:T(2,128)S(1)}, s32[2,16]{1,0:T(2,128)}, u32[]{:S(2)}) copy-start(s32[2,16]{1,0:T(2,128)} %param.13) | copy-start | bytes 388
  31.5 1.5 %collective-permute-start.9 = (bf16[8,2,16,512]{3,2,1,0:T(8,128)(2,1)S(1)}, bf16[8,2,16,512]{3,2,1,0:T(8,128)(2,1)S(1)}, u32[]{:S(2)}, u32[]{:S(2)}) collective-permute-start(bf16[8,2,16,512]{3,2,1,0:T(8,128)(2,1)S(1)} %collective-permute-done.7.refs_5_), channel_id=1, source_target_pairs={{0,1},{1,0},{2,3},{3,2},{4,5},{5,4},{6,7},{7,6},{8,9},{9,8},{10,11... | collective-permute-start | bytes 786440 | tf_op jit(solution)/shard_map/ppermute | solution.py:359
  37.1 1.6 %collective-permute-start.10 = (bf16[8,2,16,512]{3,2,1,0:T(8,128)(2,1)S(1)}, bf16[8,2,16,512]{3,2,1,0:T(8,128)(2,1)S(1)}, u32[]{:S(2)}, u32[]{:S(2)}) collective-permute-start(bf16[8,2,16,512]{3,2,1,0:T(8,128)(2,1)S(1)} %get-tuple-element.70), channel_id=1, source_target_pairs={{0,1},{1,0},{2,3},{3,2},{4,5},{5,4},{6,7},{7,6},{8,9},{9,8},{10,11... | collective-permute-start | bytes 786440 | tf_op jit(solution)/shard_map/ppermute | solution.py:359
  37.3 7.2 %collective-permute-start.11 = (bf16[8,2,16,512]{3,2,1,0:T(8,128)(2,1)S(1)}, bf16[8,2,16,512]{3,2,1,0:T(8,128)(2,1)S(1)}, u32[]{:S(2)}, u32[]{:S(2)}) collective-permute-start(bf16[8,2,16,512]{3,2,1,0:T(8,128)(2,1)S(1)} %get-tuple-element.77), channel_id=1, source_target_pairs={{0,1},{1,0},{2,3},{3,2},{4,5},{5,4},{6,7},{7,6},{8,9},{9,8},{10,11... | collective-permute-start | bytes 786440 | tf_op jit(solution)/shard_map/ppermute | solution.py:359
  38.8 8.4 %collective-permute-start.12 = (bf16[8,2,16,512]{3,2,1,0:T(8,128)(2,1)S(1)}, bf16[8,2,16,512]{3,2,1,0:T(8,128)(2,1)S(1)}, u32[]{:S(2)}, u32[]{:S(2)}) collective-permute-start(bf16[8,2,16,512]{3,2,1,0:T(8,128)(2,1)S(1)} %add_convert_fusion), channel_id=1, source_target_pairs={{0,2},{1,3},{2,0},{3,1},{4,6},{5,7},{6,4},{7,5},{8,10},{9,11},{10,... | collective-permute-start | bytes 786440 | tf_op jit(solution)/shard_map/ppermute | solution.py:359
  47.4 5.0 %collective-permute-start.14 = (bf16[4,2,16,512]{3,2,1,0:T(8,128)(2,1)S(1)}, bf16[4,2,16,512]{3,2,1,0:T(8,128)(2,1)S(1)}, u32[]{:S(2)}, u32[]{:S(2)}) collective-permute-start(bf16[4,2,16,512]{3,2,1,0:T(8,128)(2,1)S(1)} %slice.132), channel_id=1, source_target_pairs={{0,4},{1,5},{2,6},{3,7},{4,0},{5,1},{6,2},{7,3},{8,12},{9,13},{10,... | collective-permute-start | bytes 393224 | tf_op jit(solution)/shard_map/ppermute | solution.py:359
  49.1 6.1 %collective-permute-start.15 = (bf16[256,512]{1,0:T(8,128)(2,1)S(1)}, bf16[256,512]{1,0:T(8,128)(2,1)S(1)}, u32[]{:S(2)}, u32[]{:S(2)}) collective-permute-start(bf16[256,512]{1,0:T(8,128)(2,1)S(1)} %get-tuple-element.82), channel_id=1, source_target_pairs={{1,2},{3,4},{5,6},{7,8},{9,10},{11,12},{13,14},{15,16},{17,18},{19... | collective-permute-start | bytes 786440 | tf_op jit(solution)/shard_map/ppermute | solution.py:364
  52.5 7.2 %collective-permute-start.16 = (bf16[2,2,16,512]{3,2,1,0:T(8,128)(2,1)S(1)}, bf16[2,2,16,512]{3,2,1,0:T(8,128)(2,1)S(1)}, u32[]{:S(2)}, u32[]{:S(2)}) collective-permute-start(bf16[2,2,16,512]{3,2,1,0:T(8,128)(2,1)S(1)} %slice.133), channel_id=1, source_target_pairs={{0,16},{1,17},{2,18},{3,19},{4,20},{5,21},{6,22},{7,23},{8,24},{9,... | collective-permute-start | bytes 196616 | tf_op jit(solution)/shard_map/ppermute | solution.py:359
  54.6 9.6 %collective-permute-start.13 = (bf16[2,256,512]{2,1,0:T(8,128)(2,1)S(1)}, bf16[2,256,512]{2,1,0:T(8,128)(2,1)S(1)}, u32[]{:S(2)}, u32[]{:S(2)}) collective-permute-start(bf16[2,256,512]{2,1,0:T(8,128)(2,1)S(1)} %get-tuple-element.80), channel_id=1, source_target_pairs={{0,1},{1,0},{2,3},{3,2},{4,5},{5,4},{6,7},{7,6},{8,9},{9,8},{10,11... | collective-permute-start | bytes 1572872 | tf_op jit(solution)/shard_map/ppermute | solution.py:359
  54.6 5.3 %collective-permute-start.17 = (bf16[256,512]{1,0:T(8,128)(2,1)S(1)}, bf16[256,512]{1,0:T(8,128)(2,1)S(1)}, u32[]{:S(2)}, u32[]{:S(2)}) collective-permute-start(bf16[256,512]{1,0:T(8,128)(2,1)S(1)} %get-tuple-element.84), channel_id=1, source_target_pairs={{1,2},{3,4},{5,6},{7,8},{9,10},{11,12},{13,14},{15,16},{17,18},{19... | collective-permute-start | bytes 786440 | tf_op jit(solution)/shard_map/ppermute | solution.py:364
  59.7 4.5 %collective-permute-start.18 = (bf16[1,2,16,512]{3,2,1,0:T(8,128)(2,1)S(1)}, bf16[1,2,16,512]{3,2,1,0:T(8,128)(2,1)S(1)}, u32[]{:S(2)}, u32[]{:S(2)}) collective-permute-start(bf16[1,2,16,512]{3,2,1,0:T(8,128)(2,1)S(1)} %slice.134), channel_id=1, source_target_pairs={{0,8},{1,9},{2,10},{3,11},{4,12},{5,13},{6,14},{7,15},{8,0},{9,1},... | collective-permute-start | bytes 98312 | tf_op jit(solution)/shard_map/ppermute | solution.py:359
  64.4 0.8 %copy-start = (f32[256,512]{1,0:T(8,128)}, f32[256,512]{1,0:T(8,128)S(1)}, u32[]{:S(2)}) copy-start(f32[256,512]{1,0:T(8,128)S(1)} %get-tuple-element.91) | copy-start | bytes 1572868
  64.4 1.0 %copy-start.1 = (f32[256,512]{1,0:T(8,128)}, f32[256,512]{1,0:T(8,128)S(1)}, u32[]{:S(2)}) copy-start(f32[256,512]{1,0:T(8,128)S(1)} %get-tuple-element.92) | copy-start | bytes 1572868

commit v5 on v4

--- a/solution.py
+++ b/solution.py
@@ -119,7 +119,7 @@
     part = table_a.shape[0]
     for i in range(2):
         for j in range(NCOL):
-            slot = slots[i ^ flip, j]
+            slot = slots[0, i ^ flip, j]
             place = slot & (part - 1)
             rows = slice(j * STRIPE, (j + 1) * STRIPE)
             for which, far in ((0, far_k), (1, far_v)):
@@ -169,7 +169,7 @@
         for i in range(2):
             far = jnp.dot(left[:, both(i)], right[both(i)], preferred_element_type=F32)
             parts = [far[j * STRIPE : (j + 1) * STRIPE] for j in range(NCOL)]
-            places = [slots[i ^ flip, j] for j in range(NCOL)]
+            places = [slots[1, i ^ flip, j] for j in range(NCOL)]
             if i == 1:
                 parts = [x + table_sum[place, which] for x, place in zip(parts, places)]
             for x, place in zip(parts, places):
@@ -370,9 +370,12 @@
     bits = stage_bits(count)
     *z_bits, y_bit, x_bit, core_bit = bits
     relative = stripe_lists ^ me
-    slots = jnp.zeros_like(relative)
-    for place, bit in enumerate(bits):
-        slots = slots | jnp.where((relative & bit) != 0, 1 << place, 0)
+    slots = jnp.stack(
+        [
+            sum(jnp.where((relative & bit) != 0, 1 << place, 0) for place, bit in enumerate(order))
+            for order in ((*z_bits, y_bit, x_bit, core_bit), (*z_bits, x_bit, y_bit, core_bit))
+        ]
+    )
     flags = (1 - (me & 1)).reshape(1)
     alone = (me == 0) | (me == count - 1)
     biases = jnp.where(alone, -jnp.inf, 0.0).astype(F32).reshape(1)
@@ -407,10 +410,10 @@
         flags, pair, own, mate_k, across_k, near_s, near_d, coefs, far_query
     )
     from_v, from_k = crossed(out_v, count), crossed(out_k, count)
-    total = keep + swapped(send, count, x_bit).astype(F32)
+    total = keep + swapped(send, count, y_bit).astype(F32)
     total, grad_mate = lax.optimization_barrier((total, grad_mate))
     from_mate = swapped(grad_mate, count, core_bit)
-    for bit in (y_bit, *z_bits[::-1]):
+    for bit in (x_bit, *z_bits[::-1]):
         half = total.shape[0] // 2
         keep, send = total[:half], total[half:].astype(BF16)
         if bit == z_bits[-1]:

time: 66 us -> 65.7 us (level)
  no operation moved by 1% of the time
where the time goes in v5:
time: 65.7 us; the launch traced here: 65.1 us
  waiting for transfers between devices  26.5 us (40%)
  starting transfers between devices  21.3 us (32%)
  Pallas kernels  11 us (17%)
  other arithmetic  4.33 us (7%)
  local copies, waits for them, and re-layouts  1.01 us (2%)
  between operations  0.89 us (1%)
    ppermute x15, waiting for transfers between devices, swapped(): return lax.ppermute(x, 'ctx', [(i, i ^ bit) for i in range(count)])  26.5 us
    ppermute x15, starting transfers between devices, swapped(): return lax.ppermute(x, 'ctx', [(i, i ^ bit) for i in range(count)])  18.6 us
    pallas_call x3, Pallas kernels, call(): pl.pallas_call(whole, in_specs=[SMEM_SPEC if kind == FULL else VMEM_SPEC...  11 us
    ppermute x4, starting transfers between devices, crossed(): return lax.ppermute(x, 'ctx', up + [(j, i) for i, j in up])  2.67 us
    another operation x2, other arithmetic, body(): pair = jnp.stack([query_rows * BF16(SCALE), grad_out])  1.98 us
  transfers between devices with their start and end apart: 19, of which 9 were waited for; matrix products, arithmetic and copies ran while one was open for 5% of the time, Pallas kernels for 11%

profile of v5, /device:TPU:0, one launch (start us, length us, event | category | flops | bytes accessed | tf_op | source)
XLA Modules:
  0.0 65.1 jit_solution(15821902594128459029)
XLA Ops:
  0.6 0.7 %fusion.7 = bf16[1,2,16,512]{3,2,1,0:T(8,128)(2,1)S(1)} fusion(bf16[1,256,512]{2,1,0:T(8,128)(2,1)} %bitcast.37, bf16[1,256,512]{2,1,0:T(8,128)(2,1)} %bitcast.35), kind=kLoop, calls=%fused_computation.29 | loop fusion | flops 16384 | bytes 557056 | tf_op jit(solution)/shard_map/broadcast_in_dim | solution.py:387
  1.4 3.0 %collective-permute-start.1 = (bf16[1,2,16,512]{3,2,1,0:T(8,128)(2,1)S(1)}, bf16[1,2,16,512]{3,2,1,0:T(8,128)(2,1)S(1)}, u32[]{:S(2)}, u32[]{:S(2)}) collective-permute-start(bf16[1,2,16,512]{3,2,1,0:T(8,128)(2,1)S(1)} %fusion.7), channel_id=1, source_target_pairs={{0,8},{1,9},{2,10},{3,11},{4,12},{5,13},{6,14},{7,15},{8,0},{9,1},... | collective-permute-start | bytes 98312 | tf_op jit(solution)/shard_map/ppermute | solution.py:359
  5.1 2.9 %collective-permute-start = (bf16[256,512]{1,0:T(8,128)(2,1)}, bf16[256,512]{1,0:T(8,128)(2,1)S(1)}, u32[]{:S(2)}, u32[]{:S(2)}) collective-permute-start(bf16[256,512]{1,0:T(8,128)(2,1)} %param.10), channel_id=1, source_target_pairs={{0,1},{1,0},{2,3},{3,2},{4,5},{5,4},{6,7},{7,6},{8,9},{9,8},{10,11... | collective-permute-start | bytes 786440 | tf_op jit(solution)/shard_map/ppermute | solution.py:359
  8.1 2.7 %collective-permute-start.2 = (bf16[2,2,16,512]{3,2,1,0:T(8,128)(2,1)S(1)}, bf16[2,2,16,512]{3,2,1,0:T(8,128)(2,1)S(1)}, u32[]{:S(2)}, u32[]{:S(2)}) collective-permute-start(bf16[2,2,16,512]{3,2,1,0:T(8,128)(2,1)S(1)} %pad_maximum_fusion.4), channel_id=1, source_target_pairs={{0,16},{1,17},{2,18},{3,19},{4,20},{5,21},{6,22},{7,23},{8,24},{9,... | collective-permute-start | bytes 196616 | tf_op jit(solution)/shard_map/ppermute | solution.py:359
  10.7 1.0 %multiply_bitcast_fusion = bf16[1,256,512]{2,1,0:T(8,128)(2,1)S(1)} fusion(bf16[256,512]{1,0:T(8,128)(2,1)} %param.9), kind=kLoop, calls=%fused_computation.15 | loop fusion | flops 131072 | bytes 524288 | tf_op jit(solution)/shard_map/stack | solution.py:383
  12.4 3.6 %collective-permute-done.2 = bf16[2,2,16,512]{3,2,1,0:T(8,128)(2,1)S(1)} collective-permute-done((bf16[2,2,16,512]{3,2,1,0:T(8,128)(2,1)S(1)}, bf16[2,2,16,512]{3,2,1,0:T(8,128)(2,1)S(1)}, u32[]{:S(2)}, u32[]{:S(2)}) %collective-permute-start.2) | collective-permute-done | bytes 65568 | tf_op jit(solution)/shard_map/ppermute | solution.py:359
  16.6 1.1 %pad_maximum_fusion.refs_3_.refs_2_ = bf16[2,256,512]{2,1,0:T(8,128)(2,1)S(1)} fusion(bf16[1,256,512]{2,1,0:T(8,128)(2,1)} %bitcast.38, bf16[1,256,512]{2,1,0:T(8,128)(2,1)} %bitcast.36), kind=kLoop, calls=%fused_computation.1 | loop fusion | flops 262144 | bytes 1048576 | tf_op jit(solution)/shard_map/stack | solution.py:384
  17.7 1.0 %pad_maximum_fusion.1.refs_2_.refs_1_ = bf16[2,256,512]{2,1,0:T(8,128)(2,1)S(1)} fusion(bf16[1,256,512]{2,1,0:T(8,128)(2,1)} %bitcast.39, bf16[1,256,512]{2,1,0:T(8,128)(2,1)S(1)} %multiply_bitcast_fusion), kind=kLoop, calls=%fused_computation.3 | loop fusion | flops 262144 | bytes 1048576 | tf_op jit(solution)/shard_map/stack | solution.py:383
  18.7 3.5 %collective-permute-done.5 = bf16[4,2,16,512]{3,2,1,0:T(8,128)(2,1)S(1)} collective-permute-done((bf16[4,2,16,512]{3,2,1,0:T(8,128)(2,1)S(1)}, bf16[4,2,16,512]{3,2,1,0:T(8,128)(2,1)S(1)}, u32[]{:S(2)}, u32[]{:S(2)}) %collective-permute-start.5) | collective-permute-done | bytes 131104 | tf_op jit(solution)/shard_map/ppermute | solution.py:359
  22.2 3.0 %collective-permute-start.7 = (bf16[8,2,16,512]{3,2,1,0:T(8,128)(2,1)S(1)}, bf16[8,2,16,512]{3,2,1,0:T(8,128)(2,1)S(1)}, u32[]{:S(2)}, u32[]{:S(2)}) collective-permute-start(bf16[8,2,16,512]{3,2,1,0:T(8,128)(2,1)S(1)} %pad_maximum_fusion.2.refs_4_), channel_id=1, source_target_pairs={{0,2},{1,3},{2,0},{3,1},{4,6},{5,7},{6,4},{7,5},{8,10},{9,11},{10,... | collective-permute-start | bytes 786440 | tf_op jit(solution)/shard_map/ppermute | solution.py:359
  25.3 3.1 %shard_map.76 = (f32[4,768,512]{2,1,0:T(8,128)S(1)}, f32[4,768,512]{2,1,0:T(8,128)S(1)}, f32[4,8,512]{2,1,0:T(8,128)S(1)}) custom-call(s32[1]{0:T(128)} %bitcast.refs_0_, f32[1]{0:T(128)} %bitcast.6.refs_1_, bf16[2,256,512]{2,1,0:T(8,128)(2,1)S(1)} %pad_maximum_fusion.1.refs_2_.refs_1_, bf16[2,256,512]{2,1,0:T(8,128)(2,1)S(1)} %pad_maximum_fusion.refs_3_.refs_2_, ...), custom_call_target="tpu_custom_call" | custom-call | flops 17179869184 | bytes 12582912 | tf_op jit(solution)/shard_map/pallas_call | solution.py:275
  28.3 3.2 %collective-permute-done.7.refs_5_ = bf16[8,2,16,512]{3,2,1,0:T(8,128)(2,1)S(1)} collective-permute-done((bf16[8,2,16,512]{3,2,1,0:T(8,128)(2,1)S(1)}, bf16[8,2,16,512]{3,2,1,0:T(8,128)(2,1)S(1)}, u32[]{:S(2)}, u32[]{:S(2)}) %collective-permute-start.7) | collective-permute-done | bytes 262176 | tf_op jit(solution)/shard_map/ppermute | solution.py:359
  31.6 1.5 %collective-permute-done.9.refs_7_ = bf16[8,2,16,512]{3,2,1,0:T(8,128)(2,1)S(1)} collective-permute-done((bf16[8,2,16,512]{3,2,1,0:T(8,128)(2,1)S(1)}, bf16[8,2,16,512]{3,2,1,0:T(8,128)(2,1)S(1)}, u32[]{:S(2)}, u32[]{:S(2)}) %collective-permute-start.9) | collective-permute-done | bytes 262176 | tf_op jit(solution)/shard_map/ppermute | solution.py:359
  33.1 4.0 %shard_map.77 = (f32[4,8,512]{2,1,0:T(8,128)S(1)}, f32[4,128,256]{2,1,0:T(8,128)S(1)}, f32[8,2,16,512]{3,2,1,0:T(8,128)S(1)}, f32[8,2,16,512]{3,2,1,0:T(8,128)S(...) custom-call(s32[1]{0:T(128)} %bitcast.refs_0_, s32[2,2,16]{2,1,0:T(2,128)S(1)} %pad_add_fusion.refs_1_, ...), custom_call_target="tpu_custom_call" | custom-call | flops 1073741824 | bytes 4194304 | tf_op jit(solution)/shard_map/pallas_call | solution.py:275
  37.6 1.0 %collective-permute-done.10 = bf16[8,2,16,512]{3,2,1,0:T(8,128)(2,1)S(1)} collective-permute-done((bf16[8,2,16,512]{3,2,1,0:T(8,128)(2,1)S(1)}, bf16[8,2,16,512]{3,2,1,0:T(8,128)(2,1)S(1)}, u32[]{:S(2)}, u32[]{:S(2)}) %collective-permute-start.10) | collective-permute-done | bytes 262176 | tf_op jit(solution)/shard_map/ppermute | solution.py:359
  38.7 1.8 %collective-permute-start.12 = (bf16[8,2,16,512]{3,2,1,0:T(8,128)(2,1)S(1)}, bf16[8,2,16,512]{3,2,1,0:T(8,128)(2,1)S(1)}, u32[]{:S(2)}, u32[]{:S(2)}) collective-permute-start(bf16[8,2,16,512]{3,2,1,0:T(8,128)(2,1)S(1)} %add_convert_fusion), channel_id=1, source_target_pairs={{0,4},{1,5},{2,6},{3,7},{4,0},{5,1},{6,2},{7,3},{8,12},{9,13},{10,... | collective-permute-start | bytes 786440 | tf_op jit(solution)/shard_map/ppermute | solution.py:359
  40.5 4.0 %shard_map.78 = (f32[256,512]{1,0:T(8,128)}, f32[256,512]{1,0:T(8,128)S(1)}, f32[256,512]{1,0:T(8,128)S(1)}, bf16[2,256,512]{2,1,0:T(8,128)(2,1)S(1)}, bf16[256,...) custom-call(s32[1]{0:T(128)} %bitcast.refs_0_, bf16[2,256,512]{2,1,0:T(8,128)(2,1)S(1)} %pad_maximum_fusion.1.refs_2_.refs_1_, ...), custom_call_target="tpu_custom_call" | custom-call | flops 1073741824 | bytes 1048576 | tf_op jit(solution)/shard_map/pallas_call | solution.py:275
  44.5 2.7 %collective-permute-done.12 = bf16[8,2,16,512]{3,2,1,0:T(8,128)(2,1)S(1)} collective-permute-done((bf16[8,2,16,512]{3,2,1,0:T(8,128)(2,1)S(1)}, bf16[8,2,16,512]{3,2,1,0:T(8,128)(2,1)S(1)}, u32[]{:S(2)}, u32[]{:S(2)}) %collective-permute-start.12) | collective-permute-done | bytes 262176 | tf_op jit(solution)/shard_map/ppermute | solution.py:359
  47.3 1.8 %collective-permute-start.14 = (bf16[4,2,16,512]{3,2,1,0:T(8,128)(2,1)S(1)}, bf16[4,2,16,512]{3,2,1,0:T(8,128)(2,1)S(1)}, u32[]{:S(2)}, u32[]{:S(2)}) collective-permute-start(bf16[4,2,16,512]{3,2,1,0:T(8,128)(2,1)S(1)} %slice.132), channel_id=1, source_target_pairs={{0,2},{1,3},{2,0},{3,1},{4,6},{5,7},{6,4},{7,5},{8,10},{9,11},{10,... | collective-permute-start | bytes 393224 | tf_op jit(solution)/shard_map/ppermute | solution.py:359
  49.8 2.6 %collective-permute-done.14 = bf16[4,2,16,512]{3,2,1,0:T(8,128)(2,1)S(1)} collective-permute-done((bf16[4,2,16,512]{3,2,1,0:T(8,128)(2,1)S(1)}, bf16[4,2,16,512]{3,2,1,0:T(8,128)(2,1)S(1)}, u32[]{:S(2)}, u32[]{:S(2)}) %collective-permute-start.14) | collective-permute-done | bytes 131104 | tf_op jit(solution)/shard_map/ppermute | solution.py:359
  52.4 2.1 %collective-permute-start.16 = (bf16[2,2,16,512]{3,2,1,0:T(8,128)(2,1)S(1)}, bf16[2,2,16,512]{3,2,1,0:T(8,128)(2,1)S(1)}, u32[]{:S(2)}, u32[]{:S(2)}) collective-permute-start(bf16[2,2,16,512]{3,2,1,0:T(8,128)(2,1)S(1)} %slice.133), channel_id=1, source_target_pairs={{0,16},{1,17},{2,18},{3,19},{4,20},{5,21},{6,22},{7,23},{8,24},{9,... | collective-permute-start | bytes 196616 | tf_op jit(solution)/shard_map/ppermute | solution.py:359
  55.2 4.3 %collective-permute-done.16 = bf16[2,2,16,512]{3,2,1,0:T(8,128)(2,1)S(1)} collective-permute-done((bf16[2,2,16,512]{3,2,1,0:T(8,128)(2,1)S(1)}, bf16[2,2,16,512]{3,2,1,0:T(8,128)(2,1)S(1)}, u32[]{:S(2)}, u32[]{:S(2)}) %collective-permute-start.16) | collective-permute-done | bytes 65568 | tf_op jit(solution)/shard_map/ppermute | solution.py:359
  59.7 4.1 %collective-permute-done.18 = bf16[1,2,16,512]{3,2,1,0:T(8,128)(2,1)S(1)} collective-permute-done((bf16[1,2,16,512]{3,2,1,0:T(8,128)(2,1)S(1)}, bf16[1,2,16,512]{3,2,1,0:T(8,128)(2,1)S(1)}, u32[]{:S(2)}, u32[]{:S(2)}) %collective-permute-start.18) | collective-permute-done | bytes 32800 | tf_op jit(solution)/shard_map/ppermute | solution.py:359
  64.1 0.8 %copy-done = f32[256,512]{1,0:T(8,128)} copy-done((f32[256,512]{1,0:T(8,128)}, f32[256,512]{1,0:T(8,128)S(1)}, u32[]{:S(2)}) %copy-start) | copy-done | bytes 524312
  (44 shorter events, 4.9 us)
Async XLA Ops:
  1.4 6.7 %collective-permute-start.1 = (bf16[1,2,16,512]{3,2,1,0:T(8,128)(2,1)S(1)}, bf16[1,2,16,512]{3,2,1,0:T(8,128)(2,1)S(1)}, u32[]{:S(2)}, u32[]{:S(2)}) collective-permute-start(bf16[1,2,16,512]{3,2,1,0:T(8,128)(2,1)S(1)} %fusion.7), channel_id=1, source_target_pairs={{0,8},{1,9},{2,10},{3,11},{4,12},{5,13},{6,14},{7,15},{8,0},{9,1},... | collective-permute-start | bytes 98312 | tf_op jit(solution)/shard_map/ppermute | solution.py:359
  4.4 11.6 %collective-permute-start.3 = (bf16[256,512]{1,0:T(8,128)(2,1)}, bf16[256,512]{1,0:T(8,128)(2,1)S(1)}, u32[]{:S(2)}, u32[]{:S(2)}) collective-permute-start(bf16[256,512]{1,0:T(8,128)(2,1)} %param.10), channel_id=1, source_target_pairs={{1,2},{3,4},{5,6},{7,8},{9,10},{11,12},{13,14},{15,16},{17,18},{19... | collective-permute-start | bytes 786440 | tf_op jit(solution)/shard_map/ppermute | solution.py:364
  5.1 20.2 %collective-permute-start = (bf16[256,512]{1,0:T(8,128)(2,1)}, bf16[256,512]{1,0:T(8,128)(2,1)S(1)}, u32[]{:S(2)}, u32[]{:S(2)}) collective-permute-start(bf16[256,512]{1,0:T(8,128)(2,1)} %param.10), channel_id=1, source_target_pairs={{0,1},{1,0},{2,3},{3,2},{4,5},{5,4},{6,7},{7,6},{8,9},{9,8},{10,11... | collective-permute-start | bytes 786440 | tf_op jit(solution)/shard_map/ppermute | solution.py:359
  8.0 17.3 %collective-permute-start.4 = (bf16[256,512]{1,0:T(8,128)(2,1)}, bf16[256,512]{1,0:T(8,128)(2,1)S(1)}, u32[]{:S(2)}, u32[]{:S(2)}) collective-permute-start(bf16[256,512]{1,0:T(8,128)(2,1)} %param.11), channel_id=1, source_target_pairs={{0,1},{1,0},{2,3},{3,2},{4,5},{5,4},{6,7},{7,6},{8,9},{9,8},{10,11... | collective-permute-start | bytes 786440 | tf_op jit(solution)/shard_map/ppermute | solution.py:359
  8.1 7.9 %collective-permute-start.2 = (bf16[2,2,16,512]{3,2,1,0:T(8,128)(2,1)S(1)}, bf16[2,2,16,512]{3,2,1,0:T(8,128)(2,1)S(1)}, u32[]{:S(2)}, u32[]{:S(2)}) collective-permute-start(bf16[2,2,16,512]{3,2,1,0:T(8,128)(2,1)S(1)} %pad_maximum_fusion.4), channel_id=1, source_target_pairs={{0,16},{1,17},{2,18},{3,19},{4,20},{5,21},{6,22},{7,23},{8,24},{9,... | collective-permute-start | bytes 196616 | tf_op jit(solution)/shard_map/ppermute | solution.py:359
  11.7 10.5 %collective-permute-start.6 = (bf16[256,512]{1,0:T(8,128)(2,1)}, bf16[256,512]{1,0:T(8,128)(2,1)S(1)}, u32[]{:S(2)}, u32[]{:S(2)}) collective-permute-start(bf16[256,512]{1,0:T(8,128)(2,1)} %param.11), channel_id=1, source_target_pairs={{1,2},{3,4},{5,6},{7,8},{9,10},{11,12},{13,14},{15,16},{17,18},{19... | collective-permute-start | bytes 786440 | tf_op jit(solution)/shard_map/ppermute | solution.py:364
  16.0 6.2 %collective-permute-start.5 = (bf16[4,2,16,512]{3,2,1,0:T(8,128)(2,1)S(1)}, bf16[4,2,16,512]{3,2,1,0:T(8,128)(2,1)S(1)}, u32[]{:S(2)}, u32[]{:S(2)}) collective-permute-start(bf16[4,2,16,512]{3,2,1,0:T(8,128)(2,1)S(1)} %pad_maximum_fusion.3), channel_id=1, source_target_pairs={{0,4},{1,5},{2,6},{3,7},{4,0},{5,1},{6,2},{7,3},{8,12},{9,13},{10,... | collective-permute-start | bytes 393224 | tf_op jit(solution)/shard_map/ppermute | solution.py:359
  22.2 9.3 %collective-permute-start.7 = (bf16[8,2,16,512]{3,2,1,0:T(8,128)(2,1)S(1)}, bf16[8,2,16,512]{3,2,1,0:T(8,128)(2,1)S(1)}, u32[]{:S(2)}, u32[]{:S(2)}) collective-permute-start(bf16[8,2,16,512]{3,2,1,0:T(8,128)(2,1)S(1)} %pad_maximum_fusion.2.refs_4_), channel_id=1, source_target_pairs={{0,2},{1,3},{2,0},{3,1},{4,6},{5,7},{6,4},{7,5},{8,10},{9,11},{10,... | collective-permute-start | bytes 786440 | tf_op jit(solution)/shard_map/ppermute | solution.py:359
  25.2 6.3 %collective-permute-start.8 = (bf16[8,2,16,512]{3,2,1,0:T(8,128)(2,1)S(1)}, bf16[8,2,16,512]{3,2,1,0:T(8,128)(2,1)S(1)}, u32[]{:S(2)}, u32[]{:S(2)}) collective-permute-start(bf16[8,2,16,512]{3,2,1,0:T(8,128)(2,1)S(1)} %pad_maximum_fusion.2.refs_4_), channel_id=1, source_target_pairs={{0,1},{1,0},{2,3},{3,2},{4,5},{5,4},{6,7},{7,6},{8,9},{9,8},{10,11... | collective-permute-start | bytes 786440 | tf_op jit(solution)/shard_map/ppermute | solution.py:359
  25.3 6.3 %copy-start.2 = (s32[2,16]{1,0:T(2,128)S(1)}, s32[2,16]{1,0:T(2,128)}, u32[]{:S(2)}) copy-start(s32[2,16]{1,0:T(2,128)} %param.13) | copy-start | bytes 388
  31.5 1.5 %collective-permute-start.9 = (bf16[8,2,16,512]{3,2,1,0:T(8,128)(2,1)S(1)}, bf16[8,2,16,512]{3,2,1,0:T(8,128)(2,1)S(1)}, u32[]{:S(2)}, u32[]{:S(2)}) collective-permute-start(bf16[8,2,16,512]{3,2,1,0:T(8,128)(2,1)S(1)} %collective-permute-done.7.refs_5_), channel_id=1, source_target_pairs={{0,1},{1,0},{2,3},{3,2},{4,5},{5,4},{6,7},{7,6},{8,9},{9,8},{10,11... | collective-permute-start | bytes 786440 | tf_op jit(solution)/shard_map/ppermute | solution.py:359
  37.1 1.6 %collective-permute-start.10 = (bf16[8,2,16,512]{3,2,1,0:T(8,128)(2,1)S(1)}, bf16[8,2,16,512]{3,2,1,0:T(8,128)(2,1)S(1)}, u32[]{:S(2)}, u32[]{:S(2)}) collective-permute-start(bf16[8,2,16,512]{3,2,1,0:T(8,128)(2,1)S(1)} %get-tuple-element.70), channel_id=1, source_target_pairs={{0,1},{1,0},{2,3},{3,2},{4,5},{5,4},{6,7},{7,6},{8,9},{9,8},{10,11... | collective-permute-start | bytes 786440 | tf_op jit(solution)/shard_map/ppermute | solution.py:359
  37.3 7.2 %collective-permute-start.11 = (bf16[8,2,16,512]{3,2,1,0:T(8,128)(2,1)S(1)}, bf16[8,2,16,512]{3,2,1,0:T(8,128)(2,1)S(1)}, u32[]{:S(2)}, u32[]{:S(2)}) collective-permute-start(bf16[8,2,16,512]{3,2,1,0:T(8,128)(2,1)S(1)} %get-tuple-element.77), channel_id=1, source_target_pairs={{0,1},{1,0},{2,3},{3,2},{4,5},{5,4},{6,7},{7,6},{8,9},{9,8},{10,11... | collective-permute-start | bytes 786440 | tf_op jit(solution)/shard_map/ppermute | solution.py:359
  38.7 8.4 %collective-permute-start.12 = (bf16[8,2,16,512]{3,2,1,0:T(8,128)(2,1)S(1)}, bf16[8,2,16,512]{3,2,1,0:T(8,128)(2,1)S(1)}, u32[]{:S(2)}, u32[]{:S(2)}) collective-permute-start(bf16[8,2,16,512]{3,2,1,0:T(8,128)(2,1)S(1)} %add_convert_fusion), channel_id=1, source_target_pairs={{0,4},{1,5},{2,6},{3,7},{4,0},{5,1},{6,2},{7,3},{8,12},{9,13},{10,... | collective-permute-start | bytes 786440 | tf_op jit(solution)/shard_map/ppermute | solution.py:359
  47.3 5.0 %collective-permute-start.14 = (bf16[4,2,16,512]{3,2,1,0:T(8,128)(2,1)S(1)}, bf16[4,2,16,512]{3,2,1,0:T(8,128)(2,1)S(1)}, u32[]{:S(2)}, u32[]{:S(2)}) collective-permute-start(bf16[4,2,16,512]{3,2,1,0:T(8,128)(2,1)S(1)} %slice.132), channel_id=1, source_target_pairs={{0,2},{1,3},{2,0},{3,1},{4,6},{5,7},{6,4},{7,5},{8,10},{9,11},{10,... | collective-permute-start | bytes 393224 | tf_op jit(solution)/shard_map/ppermute | solution.py:359
  49.1 6.1 %collective-permute-start.15 = (bf16[256,512]{1,0:T(8,128)(2,1)S(1)}, bf16[256,512]{1,0:T(8,128)(2,1)S(1)}, u32[]{:S(2)}, u32[]{:S(2)}) collective-permute-start(bf16[256,512]{1,0:T(8,128)(2,1)S(1)} %get-tuple-element.82), channel_id=1, source_target_pairs={{1,2},{3,4},{5,6},{7,8},{9,10},{11,12},{13,14},{15,16},{17,18},{19... | collective-permute-start | bytes 786440 | tf_op jit(solution)/shard_map/ppermute | solution.py:364
  52.4 7.2 %collective-permute-start.16 = (bf16[2,2,16,512]{3,2,1,0:T(8,128)(2,1)S(1)}, bf16[2,2,16,512]{3,2,1,0:T(8,128)(2,1)S(1)}, u32[]{:S(2)}, u32[]{:S(2)}) collective-permute-start(bf16[2,2,16,512]{3,2,1,0:T(8,128)(2,1)S(1)} %slice.133), channel_id=1, source_target_pairs={{0,16},{1,17},{2,18},{3,19},{4,20},{5,21},{6,22},{7,23},{8,24},{9,... | collective-permute-start | bytes 196616 | tf_op jit(solution)/shard_map/ppermute | solution.py:359
  54.5 9.3 %collective-permute-start.13 = (bf16[2,256,512]{2,1,0:T(8,128)(2,1)S(1)}, bf16[2,256,512]{2,1,0:T(8,128)(2,1)S(1)}, u32[]{:S(2)}, u32[]{:S(2)}) collective-permute-start(bf16[2,256,512]{2,1,0:T(8,128)(2,1)S(1)} %get-tuple-element.80), channel_id=1, source_target_pairs={{0,1},{1,0},{2,3},{3,2},{4,5},{5,4},{6,7},{7,6},{8,9},{9,8},{10,11... | collective-permute-start | bytes 1572872 | tf_op jit(solution)/shard_map/ppermute | solution.py:359
  54.5 5.2 %collective-permute-start.17 = (bf16[256,512]{1,0:T(8,128)(2,1)S(1)}, bf16[256,512]{1,0:T(8,128)(2,1)S(1)}, u32[]{:S(2)}, u32[]{:S(2)}) collective-permute-start(bf16[256,512]{1,0:T(8,128)(2,1)S(1)} %get-tuple-element.84), channel_id=1, source_target_pairs={{1,2},{3,4},{5,6},{7,8},{9,10},{11,12},{13,14},{15,16},{17,18},{19... | collective-permute-start | bytes 786440 | tf_op jit(solution)/shard_map/ppermute | solution.py:364
  59.6 4.2 %collective-permute-start.18 = (bf16[1,2,16,512]{3,2,1,0:T(8,128)(2,1)S(1)}, bf16[1,2,16,512]{3,2,1,0:T(8,128)(2,1)S(1)}, u32[]{:S(2)}, u32[]{:S(2)}) collective-permute-start(bf16[1,2,16,512]{3,2,1,0:T(8,128)(2,1)S(1)} %slice.134), channel_id=1, source_target_pairs={{0,8},{1,9},{2,10},{3,11},{4,12},{5,13},{6,14},{7,15},{8,0},{9,1},... | collective-permute-start | bytes 98312 | tf_op jit(solution)/shard_map/ppermute | solution.py:359
  64.1 0.8 %copy-start = (f32[256,512]{1,0:T(8,128)}, f32[256,512]{1,0:T(8,128)S(1)}, u32[]{:S(2)}) copy-start(f32[256,512]{1,0:T(8,128)S(1)} %get-tuple-element.91) | copy-start | bytes 1572868
  64.1 1.0 %copy-start.1 = (f32[256,512]{1,0:T(8,128)}, f32[256,512]{1,0:T(8,128)S(1)}, u32[]{:S(2)}) copy-start(f32[256,512]{1,0:T(8,128)S(1)} %get-tuple-element.92) | copy-start | bytes 1572868

commit v6 on v5

--- a/solution.py
+++ b/solution.py
@@ -113,21 +113,18 @@
 def stripe_products(
     flags, slots, pair, stats, table_a, table_b, table_c, table_d,
     coefs, far_query, keep_a, keep_b, send_a, send_b,
-    far_k, far_v, q_two, g_two, far_s, far_d, far_probs, far_scores, table_sum,
+    far_k, far_v, q_two, g_two, far_s, far_d, far_probs, far_scores, table_sum, table,
 ):
     flip = flags[0]
     part = table_a.shape[0]
+    for at, piece in enumerate((table_a, table_b, table_c, table_d)):
+        table[at * part : (at + 1) * part] = piece[...]
     for i in range(2):
         for j in range(NCOL):
             slot = slots[0, i ^ flip, j]
-            place = slot & (part - 1)
             rows = slice(j * STRIPE, (j + 1) * STRIPE)
             for which, far in ((0, far_k), (1, far_v)):
-                far[i, rows] = jnp.where(
-                    slot < 2 * part,
-                    jnp.where(slot < part, table_a[place, which], table_b[place, which]),
-                    jnp.where(slot < 3 * part, table_c[place, which], table_d[place, which]),
-                )
+                far[i, rows] = table[slot, which]
     split_blocks(pair, 0, flip, q_two)
     split_blocks(pair, 1, flip, g_two)
     for far, two, out in ((far_k, q_two, far_s), (far_v, g_two, far_d)):
@@ -140,7 +137,7 @@
 def stripe_probs(
     flags, slots, pair, stats, table_a, table_b, table_c, table_d,
     coefs, far_query, keep_a, keep_b, send_a, send_b,
-    far_k, far_v, q_two, g_two, far_s, far_d, far_probs, far_scores, table_sum,
+    far_k, far_v, q_two, g_two, far_s, far_d, far_probs, far_scores, table_sum, table,
 ):
     s, d = far_s[...], far_d[...]
     near_top = stats[0, 0:1]
@@ -160,7 +157,7 @@
 def stripe_gradients(
     flags, slots, pair, stats, table_a, table_b, table_c, table_d,
     coefs, far_query, keep_a, keep_b, send_a, send_b,
-    far_k, far_v, q_two, g_two, far_s, far_d, far_probs, far_scores, table_sum,
+    far_k, far_v, q_two, g_two, far_s, far_d, far_probs, far_scores, table_sum, table,
 ):
     flip = flags[0]
     part = table_a.shape[0]
@@ -321,6 +318,7 @@
             pltpu.VMEM((FAR, 4 * BLOCK), BF16),
             pltpu.VMEM((FAR, 4 * BLOCK), BF16),
             pltpu.VMEM((4 * part, 2, STRIPE, LANES), F32),
+            pltpu.VMEM((4 * part, 2, STRIPE, LANES), BF16),
         ],
         1 << 30,
         4 << 20,

time: 65.7 us -> 65.2 us (level)
  no operation moved by 1% of the time
where the time goes in v6:
time: 65.2 us; the launch traced here: 64.5 us
  waiting for transfers between devices  26.5 us (41%)
  starting transfers between devices  21.3 us (33%)
  Pallas kernels  10.4 us (16%)
  other arithmetic  4.33 us (7%)
  local copies, waits for them, and re-layouts  1.01 us (2%)
  between operations  0.89 us (1%)
    ppermute x15, waiting for transfers between devices, swapped(): return lax.ppermute(x, 'ctx', [(i, i ^ bit) for i in range(count)])  26.5 us
    ppermute x15, starting transfers between devices, swapped(): return lax.ppermute(x, 'ctx', [(i, i ^ bit) for i in range(count)])  18.7 us
    pallas_call x3, Pallas kernels, call(): pl.pallas_call(whole, in_specs=[SMEM_SPEC if kind == FULL else VMEM_SPEC...  10.4 us
    ppermute x4, starting transfers between devices, crossed(): return lax.ppermute(x, 'ctx', up + [(j, i) for i, j in up])  2.67 us
    another operation x2, other arithmetic, body(): pair = jnp.stack([query_rows * BF16(SCALE), grad_out])  1.98 us
  transfers between devices with their start and end apart: 19, of which 9 were waited for; matrix products, arithmetic and copies ran while one was open for 5% of the time, Pallas kernels for 11%

profile of v6, /device:TPU:0, one launch (start us, length us, event | category | flops | bytes accessed | tf_op | source)
XLA Modules:
  0.0 64.5 jit_solution(3093286214731593472)
XLA Ops:
  0.6 0.7 %fusion.7 = bf16[1,2,16,512]{3,2,1,0:T(8,128)(2,1)S(1)} fusion(bf16[1,256,512]{2,1,0:T(8,128)(2,1)} %bitcast.37, bf16[1,256,512]{2,1,0:T(8,128)(2,1)} %bitcast.35), kind=kLoop, calls=%fused_computation.29 | loop fusion | flops 16384 | bytes 557056 | tf_op jit(solution)/shard_map/broadcast_in_dim | solution.py:385
  1.4 3.0 %collective-permute-start.1 = (bf16[1,2,16,512]{3,2,1,0:T(8,128)(2,1)S(1)}, bf16[1,2,16,512]{3,2,1,0:T(8,128)(2,1)S(1)}, u32[]{:S(2)}, u32[]{:S(2)}) collective-permute-start(bf16[1,2,16,512]{3,2,1,0:T(8,128)(2,1)S(1)} %fusion.7), channel_id=1, source_target_pairs={{0,8},{1,9},{2,10},{3,11},{4,12},{5,13},{6,14},{7,15},{8,0},{9,1},... | collective-permute-start | bytes 98312 | tf_op jit(solution)/shard_map/ppermute | solution.py:357
  5.1 2.9 %collective-permute-start = (bf16[256,512]{1,0:T(8,128)(2,1)}, bf16[256,512]{1,0:T(8,128)(2,1)S(1)}, u32[]{:S(2)}, u32[]{:S(2)}) collective-permute-start(bf16[256,512]{1,0:T(8,128)(2,1)} %param.10), channel_id=1, source_target_pairs={{0,1},{1,0},{2,3},{3,2},{4,5},{5,4},{6,7},{7,6},{8,9},{9,8},{10,11... | collective-permute-start | bytes 786440 | tf_op jit(solution)/shard_map/ppermute | solution.py:357
  8.1 2.7 %collective-permute-start.2 = (bf16[2,2,16,512]{3,2,1,0:T(8,128)(2,1)S(1)}, bf16[2,2,16,512]{3,2,1,0:T(8,128)(2,1)S(1)}, u32[]{:S(2)}, u32[]{:S(2)}) collective-permute-start(bf16[2,2,16,512]{3,2,1,0:T(8,128)(2,1)S(1)} %pad_maximum_fusion.4), channel_id=1, source_target_pairs={{0,16},{1,17},{2,18},{3,19},{4,20},{5,21},{6,22},{7,23},{8,24},{9,... | collective-permute-start | bytes 196616 | tf_op jit(solution)/shard_map/ppermute | solution.py:357
  10.7 1.0 %multiply_bitcast_fusion = bf16[1,256,512]{2,1,0:T(8,128)(2,1)S(1)} fusion(bf16[256,512]{1,0:T(8,128)(2,1)} %param.9), kind=kLoop, calls=%fused_computation.15 | loop fusion | flops 131072 | bytes 524288 | tf_op jit(solution)/shard_map/stack | solution.py:381
  12.4 3.6 %collective-permute-done.2 = bf16[2,2,16,512]{3,2,1,0:T(8,128)(2,1)S(1)} collective-permute-done((bf16[2,2,16,512]{3,2,1,0:T(8,128)(2,1)S(1)}, bf16[2,2,16,512]{3,2,1,0:T(8,128)(2,1)S(1)}, u32[]{:S(2)}, u32[]{:S(2)}) %collective-permute-start.2) | collective-permute-done | bytes 65568 | tf_op jit(solution)/shard_map/ppermute | solution.py:357
  16.6 1.1 %pad_maximum_fusion.refs_3_.refs_2_ = bf16[2,256,512]{2,1,0:T(8,128)(2,1)S(1)} fusion(bf16[1,256,512]{2,1,0:T(8,128)(2,1)} %bitcast.38, bf16[1,256,512]{2,1,0:T(8,128)(2,1)} %bitcast.36), kind=kLoop, calls=%fused_computation.1 | loop fusion | flops 262144 | bytes 1048576 | tf_op jit(solution)/shard_map/stack | solution.py:382
  17.7 1.0 %pad_maximum_fusion.1.refs_2_.refs_1_ = bf16[2,256,512]{2,1,0:T(8,128)(2,1)S(1)} fusion(bf16[1,256,512]{2,1,0:T(8,128)(2,1)} %bitcast.39, bf16[1,256,512]{2,1,0:T(8,128)(2,1)S(1)} %multiply_bitcast_fusion), kind=kLoop, calls=%fused_computation.3 | loop fusion | flops 262144 | bytes 1048576 | tf_op jit(solution)/shard_map/stack | solution.py:381
  18.7 3.5 %collective-permute-done.5 = bf16[4,2,16,512]{3,2,1,0:T(8,128)(2,1)S(1)} collective-permute-done((bf16[4,2,16,512]{3,2,1,0:T(8,128)(2,1)S(1)}, bf16[4,2,16,512]{3,2,1,0:T(8,128)(2,1)S(1)}, u32[]{:S(2)}, u32[]{:S(2)}) %collective-permute-start.5) | collective-permute-done | bytes 131104 | tf_op jit(solution)/shard_map/ppermute | solution.py:357
  22.2 3.0 %collective-permute-start.7 = (bf16[8,2,16,512]{3,2,1,0:T(8,128)(2,1)S(1)}, bf16[8,2,16,512]{3,2,1,0:T(8,128)(2,1)S(1)}, u32[]{:S(2)}, u32[]{:S(2)}) collective-permute-start(bf16[8,2,16,512]{3,2,1,0:T(8,128)(2,1)S(1)} %pad_maximum_fusion.2.refs_4_), channel_id=1, source_target_pairs={{0,2},{1,3},{2,0},{3,1},{4,6},{5,7},{6,4},{7,5},{8,10},{9,11},{10,... | collective-permute-start | bytes 786440 | tf_op jit(solution)/shard_map/ppermute | solution.py:357
  25.3 3.1 %shard_map.76 = (f32[4,768,512]{2,1,0:T(8,128)S(1)}, f32[4,768,512]{2,1,0:T(8,128)S(1)}, f32[4,8,512]{2,1,0:T(8,128)S(1)}) custom-call(s32[1]{0:T(128)} %bitcast.refs_0_, f32[1]{0:T(128)} %bitcast.6.refs_1_, bf16[2,256,512]{2,1,0:T(8,128)(2,1)S(1)} %pad_maximum_fusion.1.refs_2_.refs_1_, bf16[2,256,512]{2,1,0:T(8,128)(2,1)S(1)} %pad_maximum_fusion.refs_3_.refs_2_, ...), custom_call_target="tpu_custom_call" | custom-call | flops 17179869184 | bytes 12582912 | tf_op jit(solution)/shard_map/pallas_call | solution.py:272
  28.3 3.2 %collective-permute-done.7.refs_5_ = bf16[8,2,16,512]{3,2,1,0:T(8,128)(2,1)S(1)} collective-permute-done((bf16[8,2,16,512]{3,2,1,0:T(8,128)(2,1)S(1)}, bf16[8,2,16,512]{3,2,1,0:T(8,128)(2,1)S(1)}, u32[]{:S(2)}, u32[]{:S(2)}) %collective-permute-start.7) | collective-permute-done | bytes 262176 | tf_op jit(solution)/shard_map/ppermute | solution.py:357
  31.6 1.5 %collective-permute-done.9.refs_7_ = bf16[8,2,16,512]{3,2,1,0:T(8,128)(2,1)S(1)} collective-permute-done((bf16[8,2,16,512]{3,2,1,0:T(8,128)(2,1)S(1)}, bf16[8,2,16,512]{3,2,1,0:T(8,128)(2,1)S(1)}, u32[]{:S(2)}, u32[]{:S(2)}) %collective-permute-start.9) | collective-permute-done | bytes 262176 | tf_op jit(solution)/shard_map/ppermute | solution.py:357
  33.1 3.4 %shard_map.77 = (f32[4,8,512]{2,1,0:T(8,128)S(1)}, f32[4,128,256]{2,1,0:T(8,128)S(1)}, f32[8,2,16,512]{3,2,1,0:T(8,128)S(1)}, f32[8,2,16,512]{3,2,1,0:T(8,128)S(...) custom-call(s32[1]{0:T(128)} %bitcast.refs_0_, s32[2,2,16]{2,1,0:T(2,128)S(1)} %pad_add_fusion.refs_1_, ...), custom_call_target="tpu_custom_call" | custom-call | flops 1073741824 | bytes 4194304 | tf_op jit(solution)/shard_map/pallas_call | solution.py:272
  37.1 1.0 %collective-permute-done.10 = bf16[8,2,16,512]{3,2,1,0:T(8,128)(2,1)S(1)} collective-permute-done((bf16[8,2,16,512]{3,2,1,0:T(8,128)(2,1)S(1)}, bf16[8,2,16,512]{3,2,1,0:T(8,128)(2,1)S(1)}, u32[]{:S(2)}, u32[]{:S(2)}) %collective-permute-start.10) | collective-permute-done | bytes 262176 | tf_op jit(solution)/shard_map/ppermute | solution.py:357
  38.2 1.8 %collective-permute-start.12 = (bf16[8,2,16,512]{3,2,1,0:T(8,128)(2,1)S(1)}, bf16[8,2,16,512]{3,2,1,0:T(8,128)(2,1)S(1)}, u32[]{:S(2)}, u32[]{:S(2)}) collective-permute-start(bf16[8,2,16,512]{3,2,1,0:T(8,128)(2,1)S(1)} %add_convert_fusion), channel_id=1, source_target_pairs={{0,4},{1,5},{2,6},{3,7},{4,0},{5,1},{6,2},{7,3},{8,12},{9,13},{10,... | collective-permute-start | bytes 786440 | tf_op jit(solution)/shard_map/ppermute | solution.py:357
  39.9 4.0 %shard_map.78 = (f32[256,512]{1,0:T(8,128)}, f32[256,512]{1,0:T(8,128)S(1)}, f32[256,512]{1,0:T(8,128)S(1)}, bf16[2,256,512]{2,1,0:T(8,128)(2,1)S(1)}, bf16[256,...) custom-call(s32[1]{0:T(128)} %bitcast.refs_0_, bf16[2,256,512]{2,1,0:T(8,128)(2,1)S(1)} %pad_maximum_fusion.1.refs_2_.refs_1_, ...), custom_call_target="tpu_custom_call" | custom-call | flops 1073741824 | bytes 1048576 | tf_op jit(solution)/shard_map/pallas_call | solution.py:272
  43.9 2.7 %collective-permute-done.12 = bf16[8,2,16,512]{3,2,1,0:T(8,128)(2,1)S(1)} collective-permute-done((bf16[8,2,16,512]{3,2,1,0:T(8,128)(2,1)S(1)}, bf16[8,2,16,512]{3,2,1,0:T(8,128)(2,1)S(1)}, u32[]{:S(2)}, u32[]{:S(2)}) %collective-permute-start.12) | collective-permute-done | bytes 262176 | tf_op jit(solution)/shard_map/ppermute | solution.py:357
  46.7 1.8 %collective-permute-start.14 = (bf16[4,2,16,512]{3,2,1,0:T(8,128)(2,1)S(1)}, bf16[4,2,16,512]{3,2,1,0:T(8,128)(2,1)S(1)}, u32[]{:S(2)}, u32[]{:S(2)}) collective-permute-start(bf16[4,2,16,512]{3,2,1,0:T(8,128)(2,1)S(1)} %slice.132), channel_id=1, source_target_pairs={{0,2},{1,3},{2,0},{3,1},{4,6},{5,7},{6,4},{7,5},{8,10},{9,11},{10,... | collective-permute-start | bytes 393224 | tf_op jit(solution)/shard_map/ppermute | solution.py:357
  49.2 2.5 %collective-permute-done.14 = bf16[4,2,16,512]{3,2,1,0:T(8,128)(2,1)S(1)} collective-permute-done((bf16[4,2,16,512]{3,2,1,0:T(8,128)(2,1)S(1)}, bf16[4,2,16,512]{3,2,1,0:T(8,128)(2,1)S(1)}, u32[]{:S(2)}, u32[]{:S(2)}) %collective-permute-start.14) | collective-permute-done | bytes 131104 | tf_op jit(solution)/shard_map/ppermute | solution.py:357
  51.8 2.1 %collective-permute-start.16 = (bf16[2,2,16,512]{3,2,1,0:T(8,128)(2,1)S(1)}, bf16[2,2,16,512]{3,2,1,0:T(8,128)(2,1)S(1)}, u32[]{:S(2)}, u32[]{:S(2)}) collective-permute-start(bf16[2,2,16,512]{3,2,1,0:T(8,128)(2,1)S(1)} %slice.133), channel_id=1, source_target_pairs={{0,16},{1,17},{2,18},{3,19},{4,20},{5,21},{6,22},{7,23},{8,24},{9,... | collective-permute-start | bytes 196616 | tf_op jit(solution)/shard_map/ppermute | solution.py:357
  54.6 4.3 %collective-permute-done.16 = bf16[2,2,16,512]{3,2,1,0:T(8,128)(2,1)S(1)} collective-permute-done((bf16[2,2,16,512]{3,2,1,0:T(8,128)(2,1)S(1)}, bf16[2,2,16,512]{3,2,1,0:T(8,128)(2,1)S(1)}, u32[]{:S(2)}, u32[]{:S(2)}) %collective-permute-start.16) | collective-permute-done | bytes 65568 | tf_op jit(solution)/shard_map/ppermute | solution.py:357
  59.1 4.1 %collective-permute-done.18 = bf16[1,2,16,512]{3,2,1,0:T(8,128)(2,1)S(1)} collective-permute-done((bf16[1,2,16,512]{3,2,1,0:T(8,128)(2,1)S(1)}, bf16[1,2,16,512]{3,2,1,0:T(8,128)(2,1)S(1)}, u32[]{:S(2)}, u32[]{:S(2)}) %collective-permute-start.18) | collective-permute-done | bytes 32800 | tf_op jit(solution)/shard_map/ppermute | solution.py:357
  63.5 0.8 %copy-done = f32[256,512]{1,0:T(8,128)} copy-done((f32[256,512]{1,0:T(8,128)}, f32[256,512]{1,0:T(8,128)S(1)}, u32[]{:S(2)}) %copy-start) | copy-done | bytes 524312
  (44 shorter events, 4.9 us)
Async XLA Ops:
  1.4 6.7 %collective-permute-start.1 = (bf16[1,2,16,512]{3,2,1,0:T(8,128)(2,1)S(1)}, bf16[1,2,16,512]{3,2,1,0:T(8,128)(2,1)S(1)}, u32[]{:S(2)}, u32[]{:S(2)}) collective-permute-start(bf16[1,2,16,512]{3,2,1,0:T(8,128)(2,1)S(1)} %fusion.7), channel_id=1, source_target_pairs={{0,8},{1,9},{2,10},{3,11},{4,12},{5,13},{6,14},{7,15},{8,0},{9,1},... | collective-permute-start | bytes 98312 | tf_op jit(solution)/shard_map/ppermute | solution.py:357
  4.4 11.6 %collective-permute-start.3 = (bf16[256,512]{1,0:T(8,128)(2,1)}, bf16[256,512]{1,0:T(8,128)(2,1)S(1)}, u32[]{:S(2)}, u32[]{:S(2)}) collective-permute-start(bf16[256,512]{1,0:T(8,128)(2,1)} %param.10), channel_id=1, source_target_pairs={{1,2},{3,4},{5,6},{7,8},{9,10},{11,12},{13,14},{15,16},{17,18},{19... | collective-permute-start | bytes 786440 | tf_op jit(solution)/shard_map/ppermute | solution.py:362
  5.1 20.2 %collective-permute-start = (bf16[256,512]{1,0:T(8,128)(2,1)}, bf16[256,512]{1,0:T(8,128)(2,1)S(1)}, u32[]{:S(2)}, u32[]{:S(2)}) collective-permute-start(bf16[256,512]{1,0:T(8,128)(2,1)} %param.10), channel_id=1, source_target_pairs={{0,1},{1,0},{2,3},{3,2},{4,5},{5,4},{6,7},{7,6},{8,9},{9,8},{10,11... | collective-permute-start | bytes 786440 | tf_op jit(solution)/shard_map/ppermute | solution.py:357
  8.0 17.3 %collective-permute-start.4 = (bf16[256,512]{1,0:T(8,128)(2,1)}, bf16[256,512]{1,0:T(8,128)(2,1)S(1)}, u32[]{:S(2)}, u32[]{:S(2)}) collective-permute-start(bf16[256,512]{1,0:T(8,128)(2,1)} %param.11), channel_id=1, source_target_pairs={{0,1},{1,0},{2,3},{3,2},{4,5},{5,4},{6,7},{7,6},{8,9},{9,8},{10,11... | collective-permute-start | bytes 786440 | tf_op jit(solution)/shard_map/ppermute | solution.py:357
  8.1 7.9 %collective-permute-start.2 = (bf16[2,2,16,512]{3,2,1,0:T(8,128)(2,1)S(1)}, bf16[2,2,16,512]{3,2,1,0:T(8,128)(2,1)S(1)}, u32[]{:S(2)}, u32[]{:S(2)}) collective-permute-start(bf16[2,2,16,512]{3,2,1,0:T(8,128)(2,1)S(1)} %pad_maximum_fusion.4), channel_id=1, source_target_pairs={{0,16},{1,17},{2,18},{3,19},{4,20},{5,21},{6,22},{7,23},{8,24},{9,... | collective-permute-start | bytes 196616 | tf_op jit(solution)/shard_map/ppermute | solution.py:357
  11.7 10.5 %collective-permute-start.6 = (bf16[256,512]{1,0:T(8,128)(2,1)}, bf16[256,512]{1,0:T(8,128)(2,1)S(1)}, u32[]{:S(2)}, u32[]{:S(2)}) collective-permute-start(bf16[256,512]{1,0:T(8,128)(2,1)} %param.11), channel_id=1, source_target_pairs={{1,2},{3,4},{5,6},{7,8},{9,10},{11,12},{13,14},{15,16},{17,18},{19... | collective-permute-start | bytes 786440 | tf_op jit(solution)/shard_map/ppermute | solution.py:362
  16.0 6.2 %collective-permute-start.5 = (bf16[4,2,16,512]{3,2,1,0:T(8,128)(2,1)S(1)}, bf16[4,2,16,512]{3,2,1,0:T(8,128)(2,1)S(1)}, u32[]{:S(2)}, u32[]{:S(2)}) collective-permute-start(bf16[4,2,16,512]{3,2,1,0:T(8,128)(2,1)S(1)} %pad_maximum_fusion.3), channel_id=1, source_target_pairs={{0,4},{1,5},{2,6},{3,7},{4,0},{5,1},{6,2},{7,3},{8,12},{9,13},{10,... | collective-permute-start | bytes 393224 | tf_op jit(solution)/shard_map/ppermute | solution.py:357
  22.2 9.3 %collective-permute-start.7 = (bf16[8,2,16,512]{3,2,1,0:T(8,128)(2,1)S(1)}, bf16[8,2,16,512]{3,2,1,0:T(8,128)(2,1)S(1)}, u32[]{:S(2)}, u32[]{:S(2)}) collective-permute-start(bf16[8,2,16,512]{3,2,1,0:T(8,128)(2,1)S(1)} %pad_maximum_fusion.2.refs_4_), channel_id=1, source_target_pairs={{0,2},{1,3},{2,0},{3,1},{4,6},{5,7},{6,4},{7,5},{8,10},{9,11},{10,... | collective-permute-start | bytes 786440 | tf_op jit(solution)/shard_map/ppermute | solution.py:357
  25.2 6.3 %collective-permute-start.8 = (bf16[8,2,16,512]{3,2,1,0:T(8,128)(2,1)S(1)}, bf16[8,2,16,512]{3,2,1,0:T(8,128)(2,1)S(1)}, u32[]{:S(2)}, u32[]{:S(2)}) collective-permute-start(bf16[8,2,16,512]{3,2,1,0:T(8,128)(2,1)S(1)} %pad_maximum_fusion.2.refs_4_), channel_id=1, source_target_pairs={{0,1},{1,0},{2,3},{3,2},{4,5},{5,4},{6,7},{7,6},{8,9},{9,8},{10,11... | collective-permute-start | bytes 786440 | tf_op jit(solution)/shard_map/ppermute | solution.py:357
  25.3 6.3 %copy-start.2 = (s32[2,16]{1,0:T(2,128)S(1)}, s32[2,16]{1,0:T(2,128)}, u32[]{:S(2)}) copy-start(s32[2,16]{1,0:T(2,128)} %param.13) | copy-start | bytes 388
  31.5 1.5 %collective-permute-start.9 = (bf16[8,2,16,512]{3,2,1,0:T(8,128)(2,1)S(1)}, bf16[8,2,16,512]{3,2,1,0:T(8,128)(2,1)S(1)}, u32[]{:S(2)}, u32[]{:S(2)}) collective-permute-start(bf16[8,2,16,512]{3,2,1,0:T(8,128)(2,1)S(1)} %collective-permute-done.7.refs_5_), channel_id=1, source_target_pairs={{0,1},{1,0},{2,3},{3,2},{4,5},{5,4},{6,7},{7,6},{8,9},{9,8},{10,11... | collective-permute-start | bytes 786440 | tf_op jit(solution)/shard_map/ppermute | solution.py:357
  36.5 1.6 %collective-permute-start.10 = (bf16[8,2,16,512]{3,2,1,0:T(8,128)(2,1)S(1)}, bf16[8,2,16,512]{3,2,1,0:T(8,128)(2,1)S(1)}, u32[]{:S(2)}, u32[]{:S(2)}) collective-permute-start(bf16[8,2,16,512]{3,2,1,0:T(8,128)(2,1)S(1)} %get-tuple-element.70), channel_id=1, source_target_pairs={{0,1},{1,0},{2,3},{3,2},{4,5},{5,4},{6,7},{7,6},{8,9},{9,8},{10,11... | collective-permute-start | bytes 786440 | tf_op jit(solution)/shard_map/ppermute | solution.py:357
  36.7 7.2 %collective-permute-start.11 = (bf16[8,2,16,512]{3,2,1,0:T(8,128)(2,1)S(1)}, bf16[8,2,16,512]{3,2,1,0:T(8,128)(2,1)S(1)}, u32[]{:S(2)}, u32[]{:S(2)}) collective-permute-start(bf16[8,2,16,512]{3,2,1,0:T(8,128)(2,1)S(1)} %get-tuple-element.77), channel_id=1, source_target_pairs={{0,1},{1,0},{2,3},{3,2},{4,5},{5,4},{6,7},{7,6},{8,9},{9,8},{10,11... | collective-permute-start | bytes 786440 | tf_op jit(solution)/shard_map/ppermute | solution.py:357
  38.2 8.4 %collective-permute-start.12 = (bf16[8,2,16,512]{3,2,1,0:T(8,128)(2,1)S(1)}, bf16[8,2,16,512]{3,2,1,0:T(8,128)(2,1)S(1)}, u32[]{:S(2)}, u32[]{:S(2)}) collective-permute-start(bf16[8,2,16,512]{3,2,1,0:T(8,128)(2,1)S(1)} %add_convert_fusion), channel_id=1, source_target_pairs={{0,4},{1,5},{2,6},{3,7},{4,0},{5,1},{6,2},{7,3},{8,12},{9,13},{10,... | collective-permute-start | bytes 786440 | tf_op jit(solution)/shard_map/ppermute | solution.py:357
  46.7 5.0 %collective-permute-start.14 = (bf16[4,2,16,512]{3,2,1,0:T(8,128)(2,1)S(1)}, bf16[4,2,16,512]{3,2,1,0:T(8,128)(2,1)S(1)}, u32[]{:S(2)}, u32[]{:S(2)}) collective-permute-start(bf16[4,2,16,512]{3,2,1,0:T(8,128)(2,1)S(1)} %slice.132), channel_id=1, source_target_pairs={{0,2},{1,3},{2,0},{3,1},{4,6},{5,7},{6,4},{7,5},{8,10},{9,11},{10,... | collective-permute-start | bytes 393224 | tf_op jit(solution)/shard_map/ppermute | solution.py:357
  48.5 6.1 %collective-permute-start.15 = (bf16[256,512]{1,0:T(8,128)(2,1)S(1)}, bf16[256,512]{1,0:T(8,128)(2,1)S(1)}, u32[]{:S(2)}, u32[]{:S(2)}) collective-permute-start(bf16[256,512]{1,0:T(8,128)(2,1)S(1)} %get-tuple-element.82), channel_id=1, source_target_pairs={{1,2},{3,4},{5,6},{7,8},{9,10},{11,12},{13,14},{15,16},{17,18},{19... | collective-permute-start | bytes 786440 | tf_op jit(solution)/shard_map/ppermute | solution.py:362
  51.8 7.2 %collective-permute-start.16 = (bf16[2,2,16,512]{3,2,1,0:T(8,128)(2,1)S(1)}, bf16[2,2,16,512]{3,2,1,0:T(8,128)(2,1)S(1)}, u32[]{:S(2)}, u32[]{:S(2)}) collective-permute-start(bf16[2,2,16,512]{3,2,1,0:T(8,128)(2,1)S(1)} %slice.133), channel_id=1, source_target_pairs={{0,16},{1,17},{2,18},{3,19},{4,20},{5,21},{6,22},{7,23},{8,24},{9,... | collective-permute-start | bytes 196616 | tf_op jit(solution)/shard_map/ppermute | solution.py:357
  53.9 9.3 %collective-permute-start.13 = (bf16[2,256,512]{2,1,0:T(8,128)(2,1)S(1)}, bf16[2,256,512]{2,1,0:T(8,128)(2,1)S(1)}, u32[]{:S(2)}, u32[]{:S(2)}) collective-permute-start(bf16[2,256,512]{2,1,0:T(8,128)(2,1)S(1)} %get-tuple-element.80), channel_id=1, source_target_pairs={{0,1},{1,0},{2,3},{3,2},{4,5},{5,4},{6,7},{7,6},{8,9},{9,8},{10,11... | collective-permute-start | bytes 1572872 | tf_op jit(solution)/shard_map/ppermute | solution.py:357
  53.9 5.2 %collective-permute-start.17 = (bf16[256,512]{1,0:T(8,128)(2,1)S(1)}, bf16[256,512]{1,0:T(8,128)(2,1)S(1)}, u32[]{:S(2)}, u32[]{:S(2)}) collective-permute-start(bf16[256,512]{1,0:T(8,128)(2,1)S(1)} %get-tuple-element.84), channel_id=1, source_target_pairs={{1,2},{3,4},{5,6},{7,8},{9,10},{11,12},{13,14},{15,16},{17,18},{19... | collective-permute-start | bytes 786440 | tf_op jit(solution)/shard_map/ppermute | solution.py:362
  59.0 4.2 %collective-permute-start.18 = (bf16[1,2,16,512]{3,2,1,0:T(8,128)(2,1)S(1)}, bf16[1,2,16,512]{3,2,1,0:T(8,128)(2,1)S(1)}, u32[]{:S(2)}, u32[]{:S(2)}) collective-permute-start(bf16[1,2,16,512]{3,2,1,0:T(8,128)(2,1)S(1)} %slice.134), channel_id=1, source_target_pairs={{0,8},{1,9},{2,10},{3,11},{4,12},{5,13},{6,14},{7,15},{8,0},{9,1},... | collective-permute-start | bytes 98312 | tf_op jit(solution)/shard_map/ppermute | solution.py:357
  63.5 0.8 %copy-start = (f32[256,512]{1,0:T(8,128)}, f32[256,512]{1,0:T(8,128)S(1)}, u32[]{:S(2)}) copy-start(f32[256,512]{1,0:T(8,128)S(1)} %get-tuple-element.91) | copy-start | bytes 1572868
  63.5 1.0 %copy-start.1 = (f32[256,512]{1,0:T(8,128)}, f32[256,512]{1,0:T(8,128)S(1)}, u32[]{:S(2)}) copy-start(f32[256,512]{1,0:T(8,128)S(1)} %get-tuple-element.92) | copy-start | bytes 1572868

commit v7 on v6

--- a/solution.py
+++ b/solution.py
@@ -112,8 +112,8 @@
 
 def stripe_products(
     flags, slots, pair, stats, table_a, table_b, table_c, table_d,
-    coefs, far_query, keep_a, keep_b, send_a, send_b,
-    far_k, far_v, q_two, g_two, far_s, far_d, far_probs, far_scores, table_sum, table,
+    coefs, far_k, far_scores, keep_a, keep_b, send_a, send_b,
+    far_v, q_two, g_two, far_s, far_d, far_probs, table_sum, table,
 ):
     flip = flags[0]
     part = table_a.shape[0]
@@ -123,11 +123,11 @@
         for j in range(NCOL):
             slot = slots[0, i ^ flip, j]
             rows = slice(j * STRIPE, (j + 1) * STRIPE)
-            for which, far in ((0, far_k), (1, far_v)):
+            for which, far in ((0, far_k.at[0]), (1, far_v)):
                 far[i, rows] = table[slot, which]
     split_blocks(pair, 0, flip, q_two)
     split_blocks(pair, 1, flip, g_two)
-    for far, two, out in ((far_k, q_two, far_s), (far_v, g_two, far_d)):
+    for far, two, out in ((far_k.at[0], q_two, far_s), (far_v, g_two, far_d)):
         for i in range(2):
             out[:, both(i)] = lax.dot_general(
                 far[i], two[both(i)], NT, preferred_element_type=F32
@@ -136,8 +136,8 @@
 
 def stripe_probs(
     flags, slots, pair, stats, table_a, table_b, table_c, table_d,
-    coefs, far_query, keep_a, keep_b, send_a, send_b,
-    far_k, far_v, q_two, g_two, far_s, far_d, far_probs, far_scores, table_sum, table,
+    coefs, far_k, far_scores, keep_a, keep_b, send_a, send_b,
+    far_v, q_two, g_two, far_s, far_d, far_probs, table_sum, table,
 ):
     s, d = far_s[...], far_d[...]
     near_top = stats[0, 0:1]
@@ -151,18 +151,18 @@
     coefs[0, 1:2] = dot
     p = u * inv
     far_probs[...] = p.astype(BF16)
-    far_scores[...] = (p * (d - dot)).astype(BF16)
+    far_scores[0] = (p * (d - dot)).astype(BF16)
 
 
 def stripe_gradients(
     flags, slots, pair, stats, table_a, table_b, table_c, table_d,
-    coefs, far_query, keep_a, keep_b, send_a, send_b,
-    far_k, far_v, q_two, g_two, far_s, far_d, far_probs, far_scores, table_sum, table,
+    coefs, far_k, far_scores, keep_a, keep_b, send_a, send_b,
+    far_v, q_two, g_two, far_s, far_d, far_probs, table_sum, table,
 ):
     flip = flags[0]
     part = table_a.shape[0]
     table_sum[...] = jnp.zeros_like(table_sum)
-    for which, left, right in ((0, far_scores, q_two), (1, far_probs, g_two)):
+    for which, left, right in ((0, far_scores.at[0], q_two), (1, far_probs, g_two)):
         for i in range(2):
             far = jnp.dot(left[:, both(i)], right[both(i)], preferred_element_type=F32)
             parts = [far[j * STRIPE : (j + 1) * STRIPE] for j in range(NCOL)]
@@ -175,17 +175,10 @@
     keep_b[...] = table_sum[part : 2 * part]
     send_a[...] = table_sum[2 * part : 3 * part].astype(send_a.dtype)
     send_b[...] = table_sum[3 * part :].astype(send_b.dtype)
-    for i in range(2):
-        out = jnp.dot(
-            jnp.transpose(far_k[i]), far_scores[:, both(i)], preferred_element_type=F32
-        )
-        rows = slice(i * BLOCK, (i + 1) * BLOCK)
-        far_query[0, :HEAD_DIM, rows] = out[:HEAD_DIM, :BLOCK]
-        far_query[0, HEAD_DIM:, rows] = out[HEAD_DIM:, BLOCK:]
 
 
 def window_probs(
-    flags, pair, own, mate_k, across_k, near_s, near_d, coefs, far_query,
+    flags, pair, own, mate_k, across_k, near_s, near_d, coefs, far_k, far_scores,
     grad_query, grad_key, grad_value, grad_mate, across_k_out, across_v_out,
     ext_k, q_two, g_two, probs, scores,
 ):
@@ -210,7 +203,7 @@
 
 
 def window_gradients(
-    flags, pair, own, mate_k, across_k, near_s, near_d, coefs, far_query,
+    flags, pair, own, mate_k, across_k, near_s, near_d, coefs, far_k, far_scores,
     grad_query, grad_key, grad_value, grad_mate, across_k_out, across_v_out,
     ext_k, q_two, g_two, probs, scores,
 ):
@@ -234,7 +227,14 @@
         )
         for h in range(2)
     ]
-    out = jnp.transpose(jnp.concatenate(near, axis=0) + far_query[0]) * SCALE
+    far = [
+        jnp.dot(jnp.transpose(far_k[0, i]), far_scores[0, :, both(i)], preferred_element_type=F32)
+        for i in range(2)
+    ]
+    far = [
+        jnp.concatenate([x[:HEAD_DIM, :BLOCK], x[HEAD_DIM:, BLOCK:]], axis=0) for x in far
+    ]
+    out = jnp.transpose(jnp.concatenate(near, axis=0) + jnp.concatenate(far, axis=1)) * SCALE
     for i in range(2):
         grad_query[block_rows(i, flip)] = out[i * BLOCK : (i + 1) * BLOCK]
 
@@ -304,18 +304,20 @@
         (stripe_products, stripe_probs, stripe_gradients),
         steps,
         [FULL, FULL, PAIR, STEP] + [TABLE] * 4,
-        [STEP, STEP] + [TABLE] * 4,
-        [((steps, 8, 2 * ROWS), F32), ((steps, LANES, ROWS), F32)]
+        [STEP, STEP, STEP] + [TABLE] * 4,
+        [
+            ((steps, 8, 2 * ROWS), F32),
+            ((steps, 2, FAR, LANES), BF16),
+            ((steps, FAR, 4 * BLOCK), BF16),
+        ]
         + [((part, 2, STRIPE, width), F32)] * 2
         + [((part, 2, STRIPE, width), BF16)] * 2,
         [
-            pltpu.VMEM((2, FAR, LANES), BF16),
             pltpu.VMEM((2, FAR, LANES), BF16),
             TWO,
             TWO,
             pltpu.VMEM((FAR, 4 * BLOCK), F32),
             pltpu.VMEM((FAR, 4 * BLOCK), F32),
-            pltpu.VMEM((FAR, 4 * BLOCK), BF16),
             pltpu.VMEM((FAR, 4 * BLOCK), BF16),
             pltpu.VMEM((4 * part, 2, STRIPE, LANES), F32),
             pltpu.VMEM((4 * part, 2, STRIPE, LANES), BF16),
@@ -326,13 +328,13 @@
     )
 
 
-def gradient_part(flags, pair, own, mate_k, across_k, near_s, near_d, coefs, far_query):
+def gradient_part(flags, pair, own, mate_k, across_k, near_s, near_d, coefs, far_k, far_scores):
     width = pair.shape[2]
     steps = width // LANES
     return call(
         (window_probs, window_gradients),
         steps,
-        [FULL, PAIR, PAIR, ROW, ROW, STEP, STEP, STEP, STEP],
+        [FULL, PAIR, PAIR, ROW, ROW, STEP, STEP, STEP, STEP, STEP],
         [ROW, ROW, ROW, PAIR, ROW, ROW],
         [((ROWS, width), F32)] * 3 + [((2, ROWS, width), BF16)] + [((ROWS, width), BF16)] * 2,
         [
@@ -344,7 +346,7 @@
         ],
         1 << 30,
         1 << 20,
-        (flags, pair, own, mate_k, across_k, near_s, near_d, coefs, far_query),
+        (flags, pair, own, mate_k, across_k, near_s, near_d, coefs, far_k, far_scores),
     )
 
 
@@ -398,14 +400,14 @@
     beside = swapped(gathered, count, x_bit)
     beside, stats = lax.optimization_barrier((beside, stats))
     tables = [gathered, beside] + [swapped(x, count, core_bit) for x in (gathered, beside)]
-    coefs, far_query, keep_a, keep_b, send_a, send_b = stripe_part(
+    coefs, far_k, far_scores, keep_a, keep_b, send_a, send_b = stripe_part(
         flags, slots, pair, stats, *tables
     )
     send = keep_b + swapped(send_b, count, core_bit).astype(F32)
     keep = keep_a + swapped(send_a, count, core_bit).astype(F32)
     send, coefs = lax.optimization_barrier((send.astype(BF16), coefs))
     grad_query, grad_key, grad_value, grad_mate, out_k, out_v = gradient_part(
-        flags, pair, own, mate_k, across_k, near_s, near_d, coefs, far_query
+        flags, pair, own, mate_k, across_k, near_s, near_d, coefs, far_k, far_scores
     )
     from_v, from_k = crossed(out_v, count), crossed(out_k, count)
     total = keep + swapped(send, count, y_bit).astype(F32)

time: 65.2 us -> 65.1 us (level)
  no operation moved by 1% of the time
where the time goes in v7:
time: 65.1 us; the launch traced here: 64.5 us
  waiting for transfers between devices  26.3 us (40%)
  starting transfers between devices  21.3 us (33%)
  Pallas kernels  10.6 us (16%)
  other arithmetic  4.36 us (7%)
  local copies, waits for them, and re-layouts  1.01 us (2%)
  between operations  0.89 us (1%)
    ppermute x15, waiting for transfers between devices, swapped(): return lax.ppermute(x, 'ctx', [(i, i ^ bit) for i in range(count)])  26.3 us
    ppermute x15, starting transfers between devices, swapped(): return lax.ppermute(x, 'ctx', [(i, i ^ bit) for i in range(count)])  18.7 us
    pallas_call x3, Pallas kernels, call(): pl.pallas_call(whole, in_specs=[SMEM_SPEC if kind == FULL else VMEM_SPEC...  10.6 us
    ppermute x4, starting transfers between devices, crossed(): return lax.ppermute(x, 'ctx', up + [(j, i) for i, j in up])  2.67 us
    another operation x2, other arithmetic, body(): pair = jnp.stack([query_rows * BF16(SCALE), grad_out])  1.98 us
  transfers between devices with their start and end apart: 19, of which 9 were waited for; matrix products, arithmetic and copies ran while one was open for 5% of the time, Pallas kernels for 11%

profile of v7, /device:TPU:0, one launch (start us, length us, event | category | flops | bytes accessed | tf_op | source)
XLA Modules:
  0.0 64.5 jit_solution(13034057963360316004)
XLA Ops:
  0.6 0.7 %fusion.7 = bf16[1,2,16,512]{3,2,1,0:T(8,128)(2,1)S(1)} fusion(bf16[1,256,512]{2,1,0:T(8,128)(2,1)} %bitcast.37, bf16[1,256,512]{2,1,0:T(8,128)(2,1)} %bitcast.35), kind=kLoop, calls=%fused_computation.29 | loop fusion | flops 16384 | bytes 557056 | tf_op jit(solution)/shard_map/broadcast_in_dim | solution.py:387
  1.4 3.0 %collective-permute-start.1 = (bf16[1,2,16,512]{3,2,1,0:T(8,128)(2,1)S(1)}, bf16[1,2,16,512]{3,2,1,0:T(8,128)(2,1)S(1)}, u32[]{:S(2)}, u32[]{:S(2)}) collective-permute-start(bf16[1,2,16,512]{3,2,1,0:T(8,128)(2,1)S(1)} %fusion.7), channel_id=1, source_target_pairs={{0,8},{1,9},{2,10},{3,11},{4,12},{5,13},{6,14},{7,15},{8,0},{9,1},... | collective-permute-start | bytes 98312 | tf_op jit(solution)/shard_map/ppermute | solution.py:359
  5.1 2.9 %collective-permute-start = (bf16[256,512]{1,0:T(8,128)(2,1)}, bf16[256,512]{1,0:T(8,128)(2,1)S(1)}, u32[]{:S(2)}, u32[]{:S(2)}) collective-permute-start(bf16[256,512]{1,0:T(8,128)(2,1)} %param.10), channel_id=1, source_target_pairs={{0,1},{1,0},{2,3},{3,2},{4,5},{5,4},{6,7},{7,6},{8,9},{9,8},{10,11... | collective-permute-start | bytes 786440 | tf_op jit(solution)/shard_map/ppermute | solution.py:359
  8.1 2.7 %collective-permute-start.2 = (bf16[2,2,16,512]{3,2,1,0:T(8,128)(2,1)S(1)}, bf16[2,2,16,512]{3,2,1,0:T(8,128)(2,1)S(1)}, u32[]{:S(2)}, u32[]{:S(2)}) collective-permute-start(bf16[2,2,16,512]{3,2,1,0:T(8,128)(2,1)S(1)} %pad_maximum_fusion.4), channel_id=1, source_target_pairs={{0,16},{1,17},{2,18},{3,19},{4,20},{5,21},{6,22},{7,23},{8,24},{9,... | collective-permute-start | bytes 196616 | tf_op jit(solution)/shard_map/ppermute | solution.py:359
  10.7 1.0 %multiply_bitcast_fusion = bf16[1,256,512]{2,1,0:T(8,128)(2,1)S(1)} fusion(bf16[256,512]{1,0:T(8,128)(2,1)} %param.9), kind=kLoop, calls=%fused_computation.15 | loop fusion | flops 131072 | bytes 524288 | tf_op jit(solution)/shard_map/stack | solution.py:383
  12.4 3.6 %collective-permute-done.2 = bf16[2,2,16,512]{3,2,1,0:T(8,128)(2,1)S(1)} collective-permute-done((bf16[2,2,16,512]{3,2,1,0:T(8,128)(2,1)S(1)}, bf16[2,2,16,512]{3,2,1,0:T(8,128)(2,1)S(1)}, u32[]{:S(2)}, u32[]{:S(2)}) %collective-permute-start.2) | collective-permute-done | bytes 65568 | tf_op jit(solution)/shard_map/ppermute | solution.py:359
  16.6 1.1 %pad_maximum_fusion.refs_3_.refs_2_ = bf16[2,256,512]{2,1,0:T(8,128)(2,1)S(1)} fusion(bf16[1,256,512]{2,1,0:T(8,128)(2,1)} %bitcast.38, bf16[1,256,512]{2,1,0:T(8,128)(2,1)} %bitcast.36), kind=kLoop, calls=%fused_computation.1 | loop fusion | flops 262144 | bytes 1048576 | tf_op jit(solution)/shard_map/stack | solution.py:384
  17.7 1.0 %pad_maximum_fusion.1.refs_2_.refs_1_ = bf16[2,256,512]{2,1,0:T(8,128)(2,1)S(1)} fusion(bf16[1,256,512]{2,1,0:T(8,128)(2,1)} %bitcast.39, bf16[1,256,512]{2,1,0:T(8,128)(2,1)S(1)} %multiply_bitcast_fusion), kind=kLoop, calls=%fused_computation.3 | loop fusion | flops 262144 | bytes 1048576 | tf_op jit(solution)/shard_map/stack | solution.py:383
  18.7 3.5 %collective-permute-done.5 = bf16[4,2,16,512]{3,2,1,0:T(8,128)(2,1)S(1)} collective-permute-done((bf16[4,2,16,512]{3,2,1,0:T(8,128)(2,1)S(1)}, bf16[4,2,16,512]{3,2,1,0:T(8,128)(2,1)S(1)}, u32[]{:S(2)}, u32[]{:S(2)}) %collective-permute-start.5) | collective-permute-done | bytes 131104 | tf_op jit(solution)/shard_map/ppermute | solution.py:359
  22.2 3.0 %collective-permute-start.7 = (bf16[8,2,16,512]{3,2,1,0:T(8,128)(2,1)S(1)}, bf16[8,2,16,512]{3,2,1,0:T(8,128)(2,1)S(1)}, u32[]{:S(2)}, u32[]{:S(2)}) collective-permute-start(bf16[8,2,16,512]{3,2,1,0:T(8,128)(2,1)S(1)} %pad_maximum_fusion.2.refs_4_), channel_id=1, source_target_pairs={{0,2},{1,3},{2,0},{3,1},{4,6},{5,7},{6,4},{7,5},{8,10},{9,11},{10,... | collective-permute-start | bytes 786440 | tf_op jit(solution)/shard_map/ppermute | solution.py:359
  25.3 3.1 %shard_map.76 = (f32[4,768,512]{2,1,0:T(8,128)S(1)}, f32[4,768,512]{2,1,0:T(8,128)S(1)}, f32[4,8,512]{2,1,0:T(8,128)S(1)}) custom-call(s32[1]{0:T(128)} %bitcast.refs_0_, f32[1]{0:T(128)} %bitcast.6.refs_1_, bf16[2,256,512]{2,1,0:T(8,128)(2,1)S(1)} %pad_maximum_fusion.1.refs_2_.refs_1_, bf16[2,256,512]{2,1,0:T(8,128)(2,1)S(1)} %pad_maximum_fusion.refs_3_.refs_2_, ...), custom_call_target="tpu_custom_call" | custom-call | flops 17179869184 | bytes 12582912 | tf_op jit(solution)/shard_map/pallas_call | solution.py:272
  28.3 3.2 %collective-permute-done.7.refs_5_ = bf16[8,2,16,512]{3,2,1,0:T(8,128)(2,1)S(1)} collective-permute-done((bf16[8,2,16,512]{3,2,1,0:T(8,128)(2,1)S(1)}, bf16[8,2,16,512]{3,2,1,0:T(8,128)(2,1)S(1)}, u32[]{:S(2)}, u32[]{:S(2)}) %collective-permute-start.7) | collective-permute-done | bytes 262176 | tf_op jit(solution)/shard_map/ppermute | solution.py:359
  31.6 1.5 %collective-permute-done.9.refs_7_ = bf16[8,2,16,512]{3,2,1,0:T(8,128)(2,1)S(1)} collective-permute-done((bf16[8,2,16,512]{3,2,1,0:T(8,128)(2,1)S(1)}, bf16[8,2,16,512]{3,2,1,0:T(8,128)(2,1)S(1)}, u32[]{:S(2)}, u32[]{:S(2)}) %collective-permute-start.9) | collective-permute-done | bytes 262176 | tf_op jit(solution)/shard_map/ppermute | solution.py:359
  33.1 3.4 %shard_map.77 = (f32[4,8,512]{2,1,0:T(8,128)S(1)}, bf16[4,2,256,128]{3,2,1,0:T(8,128)(2,1)S(1)}, bf16[4,256,512]{2,1,0:T(8,128)(2,1)S(1)}, f32[8,2,16,512]{3,2,1...) custom-call(s32[1]{0:T(128)} %bitcast.refs_0_, ...), custom_call_target="tpu_custom_call" | custom-call | flops 1073741824 | bytes 4194304 | tf_op jit(solution)/shard_map/pallas_call | solution.py:272
  37.0 1.0 %collective-permute-done.10 = bf16[8,2,16,512]{3,2,1,0:T(8,128)(2,1)S(1)} collective-permute-done((bf16[8,2,16,512]{3,2,1,0:T(8,128)(2,1)S(1)}, bf16[8,2,16,512]{3,2,1,0:T(8,128)(2,1)S(1)}, u32[]{:S(2)}, u32[]{:S(2)}) %collective-permute-start.10) | collective-permute-done | bytes 262176 | tf_op jit(solution)/shard_map/ppermute | solution.py:359
  38.1 1.8 %collective-permute-start.12 = (bf16[8,2,16,512]{3,2,1,0:T(8,128)(2,1)S(1)}, bf16[8,2,16,512]{3,2,1,0:T(8,128)(2,1)S(1)}, u32[]{:S(2)}, u32[]{:S(2)}) collective-permute-start(bf16[8,2,16,512]{3,2,1,0:T(8,128)(2,1)S(1)} %add_convert_fusion), channel_id=1, source_target_pairs={{0,4},{1,5},{2,6},{3,7},{4,0},{5,1},{6,2},{7,3},{8,12},{9,13},{10,... | collective-permute-start | bytes 786440 | tf_op jit(solution)/shard_map/ppermute | solution.py:359
  39.9 4.1 %shard_map.78 = (f32[256,512]{1,0:T(8,128)}, f32[256,512]{1,0:T(8,128)S(1)}, f32[256,512]{1,0:T(8,128)S(1)}, bf16[2,256,512]{2,1,0:T(8,128)(2,1)S(1)}, bf16[256,...) custom-call(s32[1]{0:T(128)} %bitcast.refs_0_, bf16[2,256,512]{2,1,0:T(8,128)(2,1)S(1)} %pad_maximum_fusion.1.refs_2_.refs_1_, ...), custom_call_target="tpu_custom_call" | custom-call | flops 1073741824 | bytes 1048576 | tf_op jit(solution)/shard_map/pallas_call | solution.py:272
  44.0 2.5 %collective-permute-done.12 = bf16[8,2,16,512]{3,2,1,0:T(8,128)(2,1)S(1)} collective-permute-done((bf16[8,2,16,512]{3,2,1,0:T(8,128)(2,1)S(1)}, bf16[8,2,16,512]{3,2,1,0:T(8,128)(2,1)S(1)}, u32[]{:S(2)}, u32[]{:S(2)}) %collective-permute-start.12) | collective-permute-done | bytes 262176 | tf_op jit(solution)/shard_map/ppermute | solution.py:359
  46.7 1.8 %collective-permute-start.14 = (bf16[4,2,16,512]{3,2,1,0:T(8,128)(2,1)S(1)}, bf16[4,2,16,512]{3,2,1,0:T(8,128)(2,1)S(1)}, u32[]{:S(2)}, u32[]{:S(2)}) collective-permute-start(bf16[4,2,16,512]{3,2,1,0:T(8,128)(2,1)S(1)} %slice.132), channel_id=1, source_target_pairs={{0,2},{1,3},{2,0},{3,1},{4,6},{5,7},{6,4},{7,5},{8,10},{9,11},{10,... | collective-permute-start | bytes 393224 | tf_op jit(solution)/shard_map/ppermute | solution.py:359
  49.1 2.6 %collective-permute-done.14 = bf16[4,2,16,512]{3,2,1,0:T(8,128)(2,1)S(1)} collective-permute-done((bf16[4,2,16,512]{3,2,1,0:T(8,128)(2,1)S(1)}, bf16[4,2,16,512]{3,2,1,0:T(8,128)(2,1)S(1)}, u32[]{:S(2)}, u32[]{:S(2)}) %collective-permute-start.14) | collective-permute-done | bytes 131104 | tf_op jit(solution)/shard_map/ppermute | solution.py:359
  51.8 2.1 %collective-permute-start.16 = (bf16[2,2,16,512]{3,2,1,0:T(8,128)(2,1)S(1)}, bf16[2,2,16,512]{3,2,1,0:T(8,128)(2,1)S(1)}, u32[]{:S(2)}, u32[]{:S(2)}) collective-permute-start(bf16[2,2,16,512]{3,2,1,0:T(8,128)(2,1)S(1)} %slice.133), channel_id=1, source_target_pairs={{0,16},{1,17},{2,18},{3,19},{4,20},{5,21},{6,22},{7,23},{8,24},{9,... | collective-permute-start | bytes 196616 | tf_op jit(solution)/shard_map/ppermute | solution.py:359
  54.6 4.3 %collective-permute-done.16 = bf16[2,2,16,512]{3,2,1,0:T(8,128)(2,1)S(1)} collective-permute-done((bf16[2,2,16,512]{3,2,1,0:T(8,128)(2,1)S(1)}, bf16[2,2,16,512]{3,2,1,0:T(8,128)(2,1)S(1)}, u32[]{:S(2)}, u32[]{:S(2)}) %collective-permute-start.16) | collective-permute-done | bytes 65568 | tf_op jit(solution)/shard_map/ppermute | solution.py:359
  59.0 4.1 %collective-permute-done.18 = bf16[1,2,16,512]{3,2,1,0:T(8,128)(2,1)S(1)} collective-permute-done((bf16[1,2,16,512]{3,2,1,0:T(8,128)(2,1)S(1)}, bf16[1,2,16,512]{3,2,1,0:T(8,128)(2,1)S(1)}, u32[]{:S(2)}, u32[]{:S(2)}) %collective-permute-start.18) | collective-permute-done | bytes 32800 | tf_op jit(solution)/shard_map/ppermute | solution.py:359
  63.5 0.8 %copy-done = f32[256,512]{1,0:T(8,128)} copy-done((f32[256,512]{1,0:T(8,128)}, f32[256,512]{1,0:T(8,128)S(1)}, u32[]{:S(2)}) %copy-start) | copy-done | bytes 524312
  (44 shorter events, 4.9 us)
Async XLA Ops:
  1.4 6.7 %collective-permute-start.1 = (bf16[1,2,16,512]{3,2,1,0:T(8,128)(2,1)S(1)}, bf16[1,2,16,512]{3,2,1,0:T(8,128)(2,1)S(1)}, u32[]{:S(2)}, u32[]{:S(2)}) collective-permute-start(bf16[1,2,16,512]{3,2,1,0:T(8,128)(2,1)S(1)} %fusion.7), channel_id=1, source_target_pairs={{0,8},{1,9},{2,10},{3,11},{4,12},{5,13},{6,14},{7,15},{8,0},{9,1},... | collective-permute-start | bytes 98312 | tf_op jit(solution)/shard_map/ppermute | solution.py:359
  4.4 11.6 %collective-permute-start.3 = (bf16[256,512]{1,0:T(8,128)(2,1)}, bf16[256,512]{1,0:T(8,128)(2,1)S(1)}, u32[]{:S(2)}, u32[]{:S(2)}) collective-permute-start(bf16[256,512]{1,0:T(8,128)(2,1)} %param.10), channel_id=1, source_target_pairs={{1,2},{3,4},{5,6},{7,8},{9,10},{11,12},{13,14},{15,16},{17,18},{19... | collective-permute-start | bytes 786440 | tf_op jit(solution)/shard_map/ppermute | solution.py:364
  5.1 20.2 %collective-permute-start = (bf16[256,512]{1,0:T(8,128)(2,1)}, bf16[256,512]{1,0:T(8,128)(2,1)S(1)}, u32[]{:S(2)}, u32[]{:S(2)}) collective-permute-start(bf16[256,512]{1,0:T(8,128)(2,1)} %param.10), channel_id=1, source_target_pairs={{0,1},{1,0},{2,3},{3,2},{4,5},{5,4},{6,7},{7,6},{8,9},{9,8},{10,11... | collective-permute-start | bytes 786440 | tf_op jit(solution)/shard_map/ppermute | solution.py:359
  8.0 17.3 %collective-permute-start.4 = (bf16[256,512]{1,0:T(8,128)(2,1)}, bf16[256,512]{1,0:T(8,128)(2,1)S(1)}, u32[]{:S(2)}, u32[]{:S(2)}) collective-permute-start(bf16[256,512]{1,0:T(8,128)(2,1)} %param.11), channel_id=1, source_target_pairs={{0,1},{1,0},{2,3},{3,2},{4,5},{5,4},{6,7},{7,6},{8,9},{9,8},{10,11... | collective-permute-start | bytes 786440 | tf_op jit(solution)/shard_map/ppermute | solution.py:359
  8.1 7.9 %collective-permute-start.2 = (bf16[2,2,16,512]{3,2,1,0:T(8,128)(2,1)S(1)}, bf16[2,2,16,512]{3,2,1,0:T(8,128)(2,1)S(1)}, u32[]{:S(2)}, u32[]{:S(2)}) collective-permute-start(bf16[2,2,16,512]{3,2,1,0:T(8,128)(2,1)S(1)} %pad_maximum_fusion.4), channel_id=1, source_target_pairs={{0,16},{1,17},{2,18},{3,19},{4,20},{5,21},{6,22},{7,23},{8,24},{9,... | collective-permute-start | bytes 196616 | tf_op jit(solution)/shard_map/ppermute | solution.py:359
  11.7 10.5 %collective-permute-start.6 = (bf16[256,512]{1,0:T(8,128)(2,1)}, bf16[256,512]{1,0:T(8,128)(2,1)S(1)}, u32[]{:S(2)}, u32[]{:S(2)}) collective-permute-start(bf16[256,512]{1,0:T(8,128)(2,1)} %param.11), channel_id=1, source_target_pairs={{1,2},{3,4},{5,6},{7,8},{9,10},{11,12},{13,14},{15,16},{17,18},{19... | collective-permute-start | bytes 786440 | tf_op jit(solution)/shard_map/ppermute | solution.py:364
  16.0 6.2 %collective-permute-start.5 = (bf16[4,2,16,512]{3,2,1,0:T(8,128)(2,1)S(1)}, bf16[4,2,16,512]{3,2,1,0:T(8,128)(2,1)S(1)}, u32[]{:S(2)}, u32[]{:S(2)}) collective-permute-start(bf16[4,2,16,512]{3,2,1,0:T(8,128)(2,1)S(1)} %pad_maximum_fusion.3), channel_id=1, source_target_pairs={{0,4},{1,5},{2,6},{3,7},{4,0},{5,1},{6,2},{7,3},{8,12},{9,13},{10,... | collective-permute-start | bytes 393224 | tf_op jit(solution)/shard_map/ppermute | solution.py:359
  22.2 9.3 %collective-permute-start.7 = (bf16[8,2,16,512]{3,2,1,0:T(8,128)(2,1)S(1)}, bf16[8,2,16,512]{3,2,1,0:T(8,128)(2,1)S(1)}, u32[]{:S(2)}, u32[]{:S(2)}) collective-permute-start(bf16[8,2,16,512]{3,2,1,0:T(8,128)(2,1)S(1)} %pad_maximum_fusion.2.refs_4_), channel_id=1, source_target_pairs={{0,2},{1,3},{2,0},{3,1},{4,6},{5,7},{6,4},{7,5},{8,10},{9,11},{10,... | collective-permute-start | bytes 786440 | tf_op jit(solution)/shard_map/ppermute | solution.py:359
  25.2 6.3 %collective-permute-start.8 = (bf16[8,2,16,512]{3,2,1,0:T(8,128)(2,1)S(1)}, bf16[8,2,16,512]{3,2,1,0:T(8,128)(2,1)S(1)}, u32[]{:S(2)}, u32[]{:S(2)}) collective-permute-start(bf16[8,2,16,512]{3,2,1,0:T(8,128)(2,1)S(1)} %pad_maximum_fusion.2.refs_4_), channel_id=1, source_target_pairs={{0,1},{1,0},{2,3},{3,2},{4,5},{5,4},{6,7},{7,6},{8,9},{9,8},{10,11... | collective-permute-start | bytes 786440 | tf_op jit(solution)/shard_map/ppermute | solution.py:359
  25.3 6.3 %copy-start.2 = (s32[2,16]{1,0:T(2,128)S(1)}, s32[2,16]{1,0:T(2,128)}, u32[]{:S(2)}) copy-start(s32[2,16]{1,0:T(2,128)} %param.13) | copy-start | bytes 388
  31.5 1.5 %collective-permute-start.9 = (bf16[8,2,16,512]{3,2,1,0:T(8,128)(2,1)S(1)}, bf16[8,2,16,512]{3,2,1,0:T(8,128)(2,1)S(1)}, u32[]{:S(2)}, u32[]{:S(2)}) collective-permute-start(bf16[8,2,16,512]{3,2,1,0:T(8,128)(2,1)S(1)} %collective-permute-done.7.refs_5_), channel_id=1, source_target_pairs={{0,1},{1,0},{2,3},{3,2},{4,5},{5,4},{6,7},{7,6},{8,9},{9,8},{10,11... | collective-permute-start | bytes 786440 | tf_op jit(solution)/shard_map/ppermute | solution.py:359
  36.4 1.6 %collective-permute-start.10 = (bf16[8,2,16,512]{3,2,1,0:T(8,128)(2,1)S(1)}, bf16[8,2,16,512]{3,2,1,0:T(8,128)(2,1)S(1)}, u32[]{:S(2)}, u32[]{:S(2)}) collective-permute-start(bf16[8,2,16,512]{3,2,1,0:T(8,128)(2,1)S(1)} %get-tuple-element.71), channel_id=1, source_target_pairs={{0,1},{1,0},{2,3},{3,2},{4,5},{5,4},{6,7},{7,6},{8,9},{9,8},{10,11... | collective-permute-start | bytes 786440 | tf_op jit(solution)/shard_map/ppermute | solution.py:359
  36.6 7.4 %collective-permute-start.11 = (bf16[8,2,16,512]{3,2,1,0:T(8,128)(2,1)S(1)}, bf16[8,2,16,512]{3,2,1,0:T(8,128)(2,1)S(1)}, u32[]{:S(2)}, u32[]{:S(2)}) collective-permute-start(bf16[8,2,16,512]{3,2,1,0:T(8,128)(2,1)S(1)} %get-tuple-element.79), channel_id=1, source_target_pairs={{0,1},{1,0},{2,3},{3,2},{4,5},{5,4},{6,7},{7,6},{8,9},{9,8},{10,11... | collective-permute-start | bytes 786440 | tf_op jit(solution)/shard_map/ppermute | solution.py:359
  38.1 8.4 %collective-permute-start.12 = (bf16[8,2,16,512]{3,2,1,0:T(8,128)(2,1)S(1)}, bf16[8,2,16,512]{3,2,1,0:T(8,128)(2,1)S(1)}, u32[]{:S(2)}, u32[]{:S(2)}) collective-permute-start(bf16[8,2,16,512]{3,2,1,0:T(8,128)(2,1)S(1)} %add_convert_fusion), channel_id=1, source_target_pairs={{0,4},{1,5},{2,6},{3,7},{4,0},{5,1},{6,2},{7,3},{8,12},{9,13},{10,... | collective-permute-start | bytes 786440 | tf_op jit(solution)/shard_map/ppermute | solution.py:359
  46.7 5.0 %collective-permute-start.14 = (bf16[4,2,16,512]{3,2,1,0:T(8,128)(2,1)S(1)}, bf16[4,2,16,512]{3,2,1,0:T(8,128)(2,1)S(1)}, u32[]{:S(2)}, u32[]{:S(2)}) collective-permute-start(bf16[4,2,16,512]{3,2,1,0:T(8,128)(2,1)S(1)} %slice.132), channel_id=1, source_target_pairs={{0,2},{1,3},{2,0},{3,1},{4,6},{5,7},{6,4},{7,5},{8,10},{9,11},{10,... | collective-permute-start | bytes 393224 | tf_op jit(solution)/shard_map/ppermute | solution.py:359
  48.5 6.1 %collective-permute-start.15 = (bf16[256,512]{1,0:T(8,128)(2,1)S(1)}, bf16[256,512]{1,0:T(8,128)(2,1)S(1)}, u32[]{:S(2)}, u32[]{:S(2)}) collective-permute-start(bf16[256,512]{1,0:T(8,128)(2,1)S(1)} %get-tuple-element.84), channel_id=1, source_target_pairs={{1,2},{3,4},{5,6},{7,8},{9,10},{11,12},{13,14},{15,16},{17,18},{19... | collective-permute-start | bytes 786440 | tf_op jit(solution)/shard_map/ppermute | solution.py:364
  51.8 7.2 %collective-permute-start.16 = (bf16[2,2,16,512]{3,2,1,0:T(8,128)(2,1)S(1)}, bf16[2,2,16,512]{3,2,1,0:T(8,128)(2,1)S(1)}, u32[]{:S(2)}, u32[]{:S(2)}) collective-permute-start(bf16[2,2,16,512]{3,2,1,0:T(8,128)(2,1)S(1)} %slice.133), channel_id=1, source_target_pairs={{0,16},{1,17},{2,18},{3,19},{4,20},{5,21},{6,22},{7,23},{8,24},{9,... | collective-permute-start | bytes 196616 | tf_op jit(solution)/shard_map/ppermute | solution.py:359
  53.9 9.3 %collective-permute-start.13 = (bf16[2,256,512]{2,1,0:T(8,128)(2,1)S(1)}, bf16[2,256,512]{2,1,0:T(8,128)(2,1)S(1)}, u32[]{:S(2)}, u32[]{:S(2)}) collective-permute-start(bf16[2,256,512]{2,1,0:T(8,128)(2,1)S(1)} %get-tuple-element.82), channel_id=1, source_target_pairs={{0,1},{1,0},{2,3},{3,2},{4,5},{5,4},{6,7},{7,6},{8,9},{9,8},{10,11... | collective-permute-start | bytes 1572872 | tf_op jit(solution)/shard_map/ppermute | solution.py:359
  53.9 5.1 %collective-permute-start.17 = (bf16[256,512]{1,0:T(8,128)(2,1)S(1)}, bf16[256,512]{1,0:T(8,128)(2,1)S(1)}, u32[]{:S(2)}, u32[]{:S(2)}) collective-permute-start(bf16[256,512]{1,0:T(8,128)(2,1)S(1)} %get-tuple-element.86), channel_id=1, source_target_pairs={{1,2},{3,4},{5,6},{7,8},{9,10},{11,12},{13,14},{15,16},{17,18},{19... | collective-permute-start | bytes 786440 | tf_op jit(solution)/shard_map/ppermute | solution.py:364
  58.9 4.2 %collective-permute-start.18 = (bf16[1,2,16,512]{3,2,1,0:T(8,128)(2,1)S(1)}, bf16[1,2,16,512]{3,2,1,0:T(8,128)(2,1)S(1)}, u32[]{:S(2)}, u32[]{:S(2)}) collective-permute-start(bf16[1,2,16,512]{3,2,1,0:T(8,128)(2,1)S(1)} %slice.134), channel_id=1, source_target_pairs={{0,8},{1,9},{2,10},{3,11},{4,12},{5,13},{6,14},{7,15},{8,0},{9,1},... | collective-permute-start | bytes 98312 | tf_op jit(solution)/shard_map/ppermute | solution.py:359
  63.5 0.8 %copy-start = (f32[256,512]{1,0:T(8,128)}, f32[256,512]{1,0:T(8,128)S(1)}, u32[]{:S(2)}) copy-start(f32[256,512]{1,0:T(8,128)S(1)} %get-tuple-element.93) | copy-start | bytes 1572868
  63.5 1.0 %copy-start.1 = (f32[256,512]{1,0:T(8,128)}, f32[256,512]{1,0:T(8,128)S(1)}, u32[]{:S(2)}) copy-start(f32[256,512]{1,0:T(8,128)S(1)} %get-tuple-element.94) | copy-start | bytes 1572868

commit v8 on v6

--- a/solution.py
+++ b/solution.py
@@ -385,9 +385,10 @@
     gathered = own[None, :, ROWS - STRIPE :]
     across_k = crossed(key_rows, count)
     for stage, bit in enumerate((*z_bits, y_bit)):
+        got = swapped(gathered, count, bit)
         if bit == y_bit:
-            gathered, across_k = lax.optimization_barrier((gathered, across_k))
-        gathered = jnp.concatenate([gathered, swapped(gathered, count, bit)], axis=0)
+            got, across_k = lax.optimization_barrier((got, across_k))
+        gathered = jnp.concatenate([gathered, got], axis=0)
         if stage == 0:
             gathered, late = lax.optimization_barrier((gathered, value_rows))
             across_v = crossed(late, count)

time: 65.2 us -> 64.9 us (level)
  waiting for transfers between devices: 26.5 us -> 29 us
  starting transfers between devices: 21.3 us -> 18.9 us
    ppermute x15, waiting for transfers between devices: 26.5 us -> 28.9 us  [swapped(): return lax.ppermute(x, 'ctx', [(i, i ^ bit) for i in range(count)])]
    ppermute x15, starting transfers between devices: 18.7 us -> 16.2 us  [swapped(): return lax.ppermute(x, 'ctx', [(i, i ^ bit) for i in range(count)])]
where the time goes in v8:
time: 64.9 us; the launch traced here: 64.5 us
  waiting for transfers between devices  29 us (45%)
  starting transfers between devices  18.9 us (29%)
  Pallas kernels  10.4 us (16%)
  other arithmetic  4.34 us (7%)
  local copies, waits for them, and re-layouts  1.01 us (2%)
  between operations  0.88 us (1%)
    ppermute x15, waiting for transfers between devices, swapped(): return lax.ppermute(x, 'ctx', [(i, i ^ bit) for i in range(count)])  28.9 us
    ppermute x15, starting transfers between devices, swapped(): return lax.ppermute(x, 'ctx', [(i, i ^ bit) for i in range(count)])  16.2 us
    pallas_call x3, Pallas kernels, call(): pl.pallas_call(whole, in_specs=[SMEM_SPEC if kind == FULL else VMEM_SPEC...  10.4 us
    ppermute x4, starting transfers between devices, crossed(): return lax.ppermute(x, 'ctx', up + [(j, i) for i, j in up])  2.67 us
    another operation x2, other arithmetic, body(): pair = jnp.stack([query_rows * BF16(SCALE), grad_out])  1.98 us
  transfers between devices with their start and end apart: 19, of which 9 were waited for; matrix products, arithmetic and copies ran while one was open for 5% of the time, Pallas kernels for 11%

profile of v8, /device:TPU:0, one launch (start us, length us, event | category | flops | bytes accessed | tf_op | source)
XLA Modules:
  0.0 64.5 jit_solution(7650100076308455144)
XLA Ops:
  0.6 0.7 %fusion.7 = bf16[1,2,16,512]{3,2,1,0:T(8,128)(2,1)S(1)} fusion(bf16[1,256,512]{2,1,0:T(8,128)(2,1)} %bitcast.37, bf16[1,256,512]{2,1,0:T(8,128)(2,1)} %bitcast.35), kind=kLoop, calls=%fused_computation.29 | loop fusion | flops 16384 | bytes 557056 | tf_op jit(solution)/shard_map/broadcast_in_dim | solution.py:385
  1.4 3.0 %collective-permute-start.1 = (bf16[1,2,16,512]{3,2,1,0:T(8,128)(2,1)S(1)}, bf16[1,2,16,512]{3,2,1,0:T(8,128)(2,1)S(1)}, u32[]{:S(2)}, u32[]{:S(2)}) collective-permute-start(bf16[1,2,16,512]{3,2,1,0:T(8,128)(2,1)S(1)} %fusion.7), channel_id=1, source_target_pairs={{0,8},{1,9},{2,10},{3,11},{4,12},{5,13},{6,14},{7,15},{8,0},{9,1},... | collective-permute-start | bytes 98312 | tf_op jit(solution)/shard_map/ppermute | solution.py:357
  5.1 2.9 %collective-permute-start = (bf16[256,512]{1,0:T(8,128)(2,1)}, bf16[256,512]{1,0:T(8,128)(2,1)S(1)}, u32[]{:S(2)}, u32[]{:S(2)}) collective-permute-start(bf16[256,512]{1,0:T(8,128)(2,1)} %param.10), channel_id=1, source_target_pairs={{0,1},{1,0},{2,3},{3,2},{4,5},{5,4},{6,7},{7,6},{8,9},{9,8},{10,11... | collective-permute-start | bytes 786440 | tf_op jit(solution)/shard_map/ppermute | solution.py:357
  8.1 2.7 %collective-permute-start.2 = (bf16[2,2,16,512]{3,2,1,0:T(8,128)(2,1)S(1)}, bf16[2,2,16,512]{3,2,1,0:T(8,128)(2,1)S(1)}, u32[]{:S(2)}, u32[]{:S(2)}) collective-permute-start(bf16[2,2,16,512]{3,2,1,0:T(8,128)(2,1)S(1)} %pad_maximum_fusion.4), channel_id=1, source_target_pairs={{0,16},{1,17},{2,18},{3,19},{4,20},{5,21},{6,22},{7,23},{8,24},{9,... | collective-permute-start | bytes 196616 | tf_op jit(solution)/shard_map/ppermute | solution.py:357
  10.7 1.0 %multiply_bitcast_fusion = bf16[1,256,512]{2,1,0:T(8,128)(2,1)S(1)} fusion(bf16[256,512]{1,0:T(8,128)(2,1)} %param.9), kind=kLoop, calls=%fused_computation.15 | loop fusion | flops 131072 | bytes 524288 | tf_op jit(solution)/shard_map/stack | solution.py:381
  11.7 0.7 %collective-permute-start.6 = (bf16[256,512]{1,0:T(8,128)(2,1)}, bf16[256,512]{1,0:T(8,128)(2,1)S(1)}, u32[]{:S(2)}, u32[]{:S(2)}) collective-permute-start(bf16[256,512]{1,0:T(8,128)(2,1)} %param.11), channel_id=1, source_target_pairs={{1,2},{3,4},{5,6},{7,8},{9,10},{11,12},{13,14},{15,16},{17,18},{19... | collective-permute-start | bytes 786440 | tf_op jit(solution)/shard_map/ppermute | solution.py:362
  12.4 3.6 %collective-permute-done.2 = bf16[2,2,16,512]{3,2,1,0:T(8,128)(2,1)S(1)} collective-permute-done((bf16[2,2,16,512]{3,2,1,0:T(8,128)(2,1)S(1)}, bf16[2,2,16,512]{3,2,1,0:T(8,128)(2,1)S(1)}, u32[]{:S(2)}, u32[]{:S(2)}) %collective-permute-start.2) | collective-permute-done | bytes 65568 | tf_op jit(solution)/shard_map/ppermute | solution.py:357
  16.4 1.1 %pad_maximum_fusion.refs_3_.refs_2_ = bf16[2,256,512]{2,1,0:T(8,128)(2,1)S(1)} fusion(bf16[1,256,512]{2,1,0:T(8,128)(2,1)} %bitcast.38, bf16[1,256,512]{2,1,0:T(8,128)(2,1)} %bitcast.36), kind=kLoop, calls=%fused_computation.1 | loop fusion | flops 262144 | bytes 1048576 | tf_op jit(solution)/shard_map/stack | solution.py:382
  17.5 1.0 %pad_maximum_fusion.1.refs_2_.refs_1_ = bf16[2,256,512]{2,1,0:T(8,128)(2,1)S(1)} fusion(bf16[1,256,512]{2,1,0:T(8,128)(2,1)} %bitcast.39, bf16[1,256,512]{2,1,0:T(8,128)(2,1)S(1)} %multiply_bitcast_fusion), kind=kLoop, calls=%fused_computation.3 | loop fusion | flops 262144 | bytes 1048576 | tf_op jit(solution)/shard_map/stack | solution.py:381
  18.5 3.7 %collective-permute-done.3 = bf16[4,2,16,512]{3,2,1,0:T(8,128)(2,1)S(1)} collective-permute-done((bf16[4,2,16,512]{3,2,1,0:T(8,128)(2,1)S(1)}, bf16[4,2,16,512]{3,2,1,0:T(8,128)(2,1)S(1)}, u32[]{:S(2)}, u32[]{:S(2)}) %collective-permute-start.3) | collective-permute-done | bytes 131104 | tf_op jit(solution)/shard_map/ppermute | solution.py:357
  22.2 3.0 %collective-permute-start.7 = (bf16[8,2,16,512]{3,2,1,0:T(8,128)(2,1)S(1)}, bf16[8,2,16,512]{3,2,1,0:T(8,128)(2,1)S(1)}, u32[]{:S(2)}, u32[]{:S(2)}) collective-permute-start(bf16[8,2,16,512]{3,2,1,0:T(8,128)(2,1)S(1)} %pad_maximum_fusion.2.refs_4_), channel_id=1, source_target_pairs={{0,2},{1,3},{2,0},{3,1},{4,6},{5,7},{6,4},{7,5},{8,10},{9,11},{10,... | collective-permute-start | bytes 786440 | tf_op jit(solution)/shard_map/ppermute | solution.py:357
  25.3 3.1 %shard_map.76 = (f32[4,768,512]{2,1,0:T(8,128)S(1)}, f32[4,768,512]{2,1,0:T(8,128)S(1)}, f32[4,8,512]{2,1,0:T(8,128)S(1)}) custom-call(s32[1]{0:T(128)} %bitcast.refs_0_, f32[1]{0:T(128)} %bitcast.6.refs_1_, bf16[2,256,512]{2,1,0:T(8,128)(2,1)S(1)} %pad_maximum_fusion.1.refs_2_.refs_1_, bf16[2,256,512]{2,1,0:T(8,128)(2,1)S(1)} %pad_maximum_fusion.refs_3_.refs_2_, ...), custom_call_target="tpu_custom_call" | custom-call | flops 17179869184 | bytes 12582912 | tf_op jit(solution)/shard_map/pallas_call | solution.py:272
  28.3 3.3 %collective-permute-done.7.refs_5_ = bf16[8,2,16,512]{3,2,1,0:T(8,128)(2,1)S(1)} collective-permute-done((bf16[8,2,16,512]{3,2,1,0:T(8,128)(2,1)S(1)}, bf16[8,2,16,512]{3,2,1,0:T(8,128)(2,1)S(1)}, u32[]{:S(2)}, u32[]{:S(2)}) %collective-permute-start.7) | collective-permute-done | bytes 262176 | tf_op jit(solution)/shard_map/ppermute | solution.py:357
  31.6 1.5 %collective-permute-done.9.refs_7_ = bf16[8,2,16,512]{3,2,1,0:T(8,128)(2,1)S(1)} collective-permute-done((bf16[8,2,16,512]{3,2,1,0:T(8,128)(2,1)S(1)}, bf16[8,2,16,512]{3,2,1,0:T(8,128)(2,1)S(1)}, u32[]{:S(2)}, u32[]{:S(2)}) %collective-permute-start.9) | collective-permute-done | bytes 262176 | tf_op jit(solution)/shard_map/ppermute | solution.py:357
  33.1 3.4 %shard_map.77 = (f32[4,8,512]{2,1,0:T(8,128)S(1)}, f32[4,128,256]{2,1,0:T(8,128)S(1)}, f32[8,2,16,512]{3,2,1,0:T(8,128)S(1)}, f32[8,2,16,512]{3,2,1,0:T(8,128)S(...) custom-call(s32[1]{0:T(128)} %bitcast.refs_0_, s32[2,2,16]{2,1,0:T(2,128)S(1)} %pad_add_fusion.refs_1_, ...), custom_call_target="tpu_custom_call" | custom-call | flops 1073741824 | bytes 4194304 | tf_op jit(solution)/shard_map/pallas_call | solution.py:272
  37.1 1.0 %collective-permute-done.10 = bf16[8,2,16,512]{3,2,1,0:T(8,128)(2,1)S(1)} collective-permute-done((bf16[8,2,16,512]{3,2,1,0:T(8,128)(2,1)S(1)}, bf16[8,2,16,512]{3,2,1,0:T(8,128)(2,1)S(1)}, u32[]{:S(2)}, u32[]{:S(2)}) %collective-permute-start.10) | collective-permute-done | bytes 262176 | tf_op jit(solution)/shard_map/ppermute | solution.py:357
  38.2 1.1 %collective-permute-start.12 = (bf16[8,2,16,512]{3,2,1,0:T(8,128)(2,1)S(1)}, bf16[8,2,16,512]{3,2,1,0:T(8,128)(2,1)S(1)}, u32[]{:S(2)}, u32[]{:S(2)}) collective-permute-start(bf16[8,2,16,512]{3,2,1,0:T(8,128)(2,1)S(1)} %add_convert_fusion), channel_id=1, source_target_pairs={{0,4},{1,5},{2,6},{3,7},{4,0},{5,1},{6,2},{7,3},{8,12},{9,13},{10,... | collective-permute-start | bytes 786440 | tf_op jit(solution)/shard_map/ppermute | solution.py:357
  39.3 4.0 %shard_map.78 = (f32[256,512]{1,0:T(8,128)}, f32[256,512]{1,0:T(8,128)S(1)}, f32[256,512]{1,0:T(8,128)S(1)}, bf16[2,256,512]{2,1,0:T(8,128)(2,1)S(1)}, bf16[256,...) custom-call(s32[1]{0:T(128)} %bitcast.refs_0_, bf16[2,256,512]{2,1,0:T(8,128)(2,1)S(1)} %pad_maximum_fusion.1.refs_2_.refs_1_, ...), custom_call_target="tpu_custom_call" | custom-call | flops 1073741824 | bytes 1048576 | tf_op jit(solution)/shard_map/pallas_call | solution.py:272
  43.3 3.4 %collective-permute-done.12 = bf16[8,2,16,512]{3,2,1,0:T(8,128)(2,1)S(1)} collective-permute-done((bf16[8,2,16,512]{3,2,1,0:T(8,128)(2,1)S(1)}, bf16[8,2,16,512]{3,2,1,0:T(8,128)(2,1)S(1)}, u32[]{:S(2)}, u32[]{:S(2)}) %collective-permute-start.12) | collective-permute-done | bytes 262176 | tf_op jit(solution)/shard_map/ppermute | solution.py:357
  46.8 1.8 %collective-permute-start.14 = (bf16[4,2,16,512]{3,2,1,0:T(8,128)(2,1)S(1)}, bf16[4,2,16,512]{3,2,1,0:T(8,128)(2,1)S(1)}, u32[]{:S(2)}, u32[]{:S(2)}) collective-permute-start(bf16[4,2,16,512]{3,2,1,0:T(8,128)(2,1)S(1)} %slice.132), channel_id=1, source_target_pairs={{0,2},{1,3},{2,0},{3,1},{4,6},{5,7},{6,4},{7,5},{8,10},{9,11},{10,... | collective-permute-start | bytes 393224 | tf_op jit(solution)/shard_map/ppermute | solution.py:357
  49.3 2.6 %collective-permute-done.14 = bf16[4,2,16,512]{3,2,1,0:T(8,128)(2,1)S(1)} collective-permute-done((bf16[4,2,16,512]{3,2,1,0:T(8,128)(2,1)S(1)}, bf16[4,2,16,512]{3,2,1,0:T(8,128)(2,1)S(1)}, u32[]{:S(2)}, u32[]{:S(2)}) %collective-permute-start.14) | collective-permute-done | bytes 131104 | tf_op jit(solution)/shard_map/ppermute | solution.py:357
  53.1 5.9 %collective-permute-done.16 = bf16[2,2,16,512]{3,2,1,0:T(8,128)(2,1)S(1)} collective-permute-done((bf16[2,2,16,512]{3,2,1,0:T(8,128)(2,1)S(1)}, bf16[2,2,16,512]{3,2,1,0:T(8,128)(2,1)S(1)}, u32[]{:S(2)}, u32[]{:S(2)}) %collective-permute-start.16) | collective-permute-done | bytes 65568 | tf_op jit(solution)/shard_map/ppermute | solution.py:357
  59.1 4.1 %collective-permute-done.18 = bf16[1,2,16,512]{3,2,1,0:T(8,128)(2,1)S(1)} collective-permute-done((bf16[1,2,16,512]{3,2,1,0:T(8,128)(2,1)S(1)}, bf16[1,2,16,512]{3,2,1,0:T(8,128)(2,1)S(1)}, u32[]{:S(2)}, u32[]{:S(2)}) %collective-permute-start.18) | collective-permute-done | bytes 32800 | tf_op jit(solution)/shard_map/ppermute | solution.py:357
  63.5 0.8 %copy-done = f32[256,512]{1,0:T(8,128)} copy-done((f32[256,512]{1,0:T(8,128)}, f32[256,512]{1,0:T(8,128)S(1)}, u32[]{:S(2)}) %copy-start) | copy-done | bytes 524312
  (44 shorter events, 4.5 us)
Async XLA Ops:
  1.4 6.7 %collective-permute-start.1 = (bf16[1,2,16,512]{3,2,1,0:T(8,128)(2,1)S(1)}, bf16[1,2,16,512]{3,2,1,0:T(8,128)(2,1)S(1)}, u32[]{:S(2)}, u32[]{:S(2)}) collective-permute-start(bf16[1,2,16,512]{3,2,1,0:T(8,128)(2,1)S(1)} %fusion.7), channel_id=1, source_target_pairs={{0,8},{1,9},{2,10},{3,11},{4,12},{5,13},{6,14},{7,15},{8,0},{9,1},... | collective-permute-start | bytes 98312 | tf_op jit(solution)/shard_map/ppermute | solution.py:357
  4.4 17.8 %collective-permute-start.4 = (bf16[256,512]{1,0:T(8,128)(2,1)}, bf16[256,512]{1,0:T(8,128)(2,1)S(1)}, u32[]{:S(2)}, u32[]{:S(2)}) collective-permute-start(bf16[256,512]{1,0:T(8,128)(2,1)} %param.10), channel_id=1, source_target_pairs={{1,2},{3,4},{5,6},{7,8},{9,10},{11,12},{13,14},{15,16},{17,18},{19... | collective-permute-start | bytes 786440 | tf_op jit(solution)/shard_map/ppermute | solution.py:362
  5.1 20.2 %collective-permute-start = (bf16[256,512]{1,0:T(8,128)(2,1)}, bf16[256,512]{1,0:T(8,128)(2,1)S(1)}, u32[]{:S(2)}, u32[]{:S(2)}) collective-permute-start(bf16[256,512]{1,0:T(8,128)(2,1)} %param.10), channel_id=1, source_target_pairs={{0,1},{1,0},{2,3},{3,2},{4,5},{5,4},{6,7},{7,6},{8,9},{9,8},{10,11... | collective-permute-start | bytes 786440 | tf_op jit(solution)/shard_map/ppermute | solution.py:357
  8.0 17.3 %collective-permute-start.5 = (bf16[256,512]{1,0:T(8,128)(2,1)}, bf16[256,512]{1,0:T(8,128)(2,1)S(1)}, u32[]{:S(2)}, u32[]{:S(2)}) collective-permute-start(bf16[256,512]{1,0:T(8,128)(2,1)} %param.11), channel_id=1, source_target_pairs={{0,1},{1,0},{2,3},{3,2},{4,5},{5,4},{6,7},{7,6},{8,9},{9,8},{10,11... | collective-permute-start | bytes 786440 | tf_op jit(solution)/shard_map/ppermute | solution.py:357
  8.1 7.9 %collective-permute-start.2 = (bf16[2,2,16,512]{3,2,1,0:T(8,128)(2,1)S(1)}, bf16[2,2,16,512]{3,2,1,0:T(8,128)(2,1)S(1)}, u32[]{:S(2)}, u32[]{:S(2)}) collective-permute-start(bf16[2,2,16,512]{3,2,1,0:T(8,128)(2,1)S(1)} %pad_maximum_fusion.4), channel_id=1, source_target_pairs={{0,16},{1,17},{2,18},{3,19},{4,20},{5,21},{6,22},{7,23},{8,24},{9,... | collective-permute-start | bytes 196616 | tf_op jit(solution)/shard_map/ppermute | solution.py:357
  11.7 10.5 %collective-permute-start.6 = (bf16[256,512]{1,0:T(8,128)(2,1)}, bf16[256,512]{1,0:T(8,128)(2,1)S(1)}, u32[]{:S(2)}, u32[]{:S(2)}) collective-permute-start(bf16[256,512]{1,0:T(8,128)(2,1)} %param.11), channel_id=1, source_target_pairs={{1,2},{3,4},{5,6},{7,8},{9,10},{11,12},{13,14},{15,16},{17,18},{19... | collective-permute-start | bytes 786440 | tf_op jit(solution)/shard_map/ppermute | solution.py:362
  16.0 6.2 %collective-permute-start.3 = (bf16[4,2,16,512]{3,2,1,0:T(8,128)(2,1)S(1)}, bf16[4,2,16,512]{3,2,1,0:T(8,128)(2,1)S(1)}, u32[]{:S(2)}, u32[]{:S(2)}) collective-permute-start(bf16[4,2,16,512]{3,2,1,0:T(8,128)(2,1)S(1)} %pad_maximum_fusion.3), channel_id=1, source_target_pairs={{0,4},{1,5},{2,6},{3,7},{4,0},{5,1},{6,2},{7,3},{8,12},{9,13},{10,... | collective-permute-start | bytes 393224 | tf_op jit(solution)/shard_map/ppermute | solution.py:357
  22.2 9.3 %collective-permute-start.7 = (bf16[8,2,16,512]{3,2,1,0:T(8,128)(2,1)S(1)}, bf16[8,2,16,512]{3,2,1,0:T(8,128)(2,1)S(1)}, u32[]{:S(2)}, u32[]{:S(2)}) collective-permute-start(bf16[8,2,16,512]{3,2,1,0:T(8,128)(2,1)S(1)} %pad_maximum_fusion.2.refs_4_), channel_id=1, source_target_pairs={{0,2},{1,3},{2,0},{3,1},{4,6},{5,7},{6,4},{7,5},{8,10},{9,11},{10,... | collective-permute-start | bytes 786440 | tf_op jit(solution)/shard_map/ppermute | solution.py:357
  25.2 6.4 %collective-permute-start.8 = (bf16[8,2,16,512]{3,2,1,0:T(8,128)(2,1)S(1)}, bf16[8,2,16,512]{3,2,1,0:T(8,128)(2,1)S(1)}, u32[]{:S(2)}, u32[]{:S(2)}) collective-permute-start(bf16[8,2,16,512]{3,2,1,0:T(8,128)(2,1)S(1)} %pad_maximum_fusion.2.refs_4_), channel_id=1, source_target_pairs={{0,1},{1,0},{2,3},{3,2},{4,5},{5,4},{6,7},{7,6},{8,9},{9,8},{10,11... | collective-permute-start | bytes 786440 | tf_op jit(solution)/shard_map/ppermute | solution.py:357
  25.2 6.3 %copy-start.2 = (s32[2,16]{1,0:T(2,128)S(1)}, s32[2,16]{1,0:T(2,128)}, u32[]{:S(2)}) copy-start(s32[2,16]{1,0:T(2,128)} %param.13) | copy-start | bytes 388
  31.6 1.5 %collective-permute-start.9 = (bf16[8,2,16,512]{3,2,1,0:T(8,128)(2,1)S(1)}, bf16[8,2,16,512]{3,2,1,0:T(8,128)(2,1)S(1)}, u32[]{:S(2)}, u32[]{:S(2)}) collective-permute-start(bf16[8,2,16,512]{3,2,1,0:T(8,128)(2,1)S(1)} %collective-permute-done.7.refs_5_), channel_id=1, source_target_pairs={{0,1},{1,0},{2,3},{3,2},{4,5},{5,4},{6,7},{7,6},{8,9},{9,8},{10,11... | collective-permute-start | bytes 786440 | tf_op jit(solution)/shard_map/ppermute | solution.py:357
  36.5 1.6 %collective-permute-start.10 = (bf16[8,2,16,512]{3,2,1,0:T(8,128)(2,1)S(1)}, bf16[8,2,16,512]{3,2,1,0:T(8,128)(2,1)S(1)}, u32[]{:S(2)}, u32[]{:S(2)}) collective-permute-start(bf16[8,2,16,512]{3,2,1,0:T(8,128)(2,1)S(1)} %get-tuple-element.70), channel_id=1, source_target_pairs={{0,1},{1,0},{2,3},{3,2},{4,5},{5,4},{6,7},{7,6},{8,9},{9,8},{10,11... | collective-permute-start | bytes 786440 | tf_op jit(solution)/shard_map/ppermute | solution.py:357
  36.7 6.5 %collective-permute-start.11 = (bf16[8,2,16,512]{3,2,1,0:T(8,128)(2,1)S(1)}, bf16[8,2,16,512]{3,2,1,0:T(8,128)(2,1)S(1)}, u32[]{:S(2)}, u32[]{:S(2)}) collective-permute-start(bf16[8,2,16,512]{3,2,1,0:T(8,128)(2,1)S(1)} %get-tuple-element.77), channel_id=1, source_target_pairs={{0,1},{1,0},{2,3},{3,2},{4,5},{5,4},{6,7},{7,6},{8,9},{9,8},{10,11... | collective-permute-start | bytes 786440 | tf_op jit(solution)/shard_map/ppermute | solution.py:357
  38.2 8.4 %collective-permute-start.12 = (bf16[8,2,16,512]{3,2,1,0:T(8,128)(2,1)S(1)}, bf16[8,2,16,512]{3,2,1,0:T(8,128)(2,1)S(1)}, u32[]{:S(2)}, u32[]{:S(2)}) collective-permute-start(bf16[8,2,16,512]{3,2,1,0:T(8,128)(2,1)S(1)} %add_convert_fusion), channel_id=1, source_target_pairs={{0,4},{1,5},{2,6},{3,7},{4,0},{5,1},{6,2},{7,3},{8,12},{9,13},{10,... | collective-permute-start | bytes 786440 | tf_op jit(solution)/shard_map/ppermute | solution.py:357
  46.8 5.0 %collective-permute-start.14 = (bf16[4,2,16,512]{3,2,1,0:T(8,128)(2,1)S(1)}, bf16[4,2,16,512]{3,2,1,0:T(8,128)(2,1)S(1)}, u32[]{:S(2)}, u32[]{:S(2)}) collective-permute-start(bf16[4,2,16,512]{3,2,1,0:T(8,128)(2,1)S(1)} %slice.132), channel_id=1, source_target_pairs={{0,2},{1,3},{2,0},{3,1},{4,6},{5,7},{6,4},{7,5},{8,10},{9,11},{10,... | collective-permute-start | bytes 393224 | tf_op jit(solution)/shard_map/ppermute | solution.py:357
  48.6 4.5 %collective-permute-start.15 = (bf16[256,512]{1,0:T(8,128)(2,1)S(1)}, bf16[256,512]{1,0:T(8,128)(2,1)S(1)}, u32[]{:S(2)}, u32[]{:S(2)}) collective-permute-start(bf16[256,512]{1,0:T(8,128)(2,1)S(1)} %get-tuple-element.82), channel_id=1, source_target_pairs={{1,2},{3,4},{5,6},{7,8},{9,10},{11,12},{13,14},{15,16},{17,18},{19... | collective-permute-start | bytes 786440 | tf_op jit(solution)/shard_map/ppermute | solution.py:362
  51.9 7.1 %collective-permute-start.16 = (bf16[2,2,16,512]{3,2,1,0:T(8,128)(2,1)S(1)}, bf16[2,2,16,512]{3,2,1,0:T(8,128)(2,1)S(1)}, u32[]{:S(2)}, u32[]{:S(2)}) collective-permute-start(bf16[2,2,16,512]{3,2,1,0:T(8,128)(2,1)S(1)} %slice.133), channel_id=1, source_target_pairs={{0,16},{1,17},{2,18},{3,19},{4,20},{5,21},{6,22},{7,23},{8,24},{9,... | collective-permute-start | bytes 196616 | tf_op jit(solution)/shard_map/ppermute | solution.py:357
  52.4 10.9 %collective-permute-start.13 = (bf16[2,256,512]{2,1,0:T(8,128)(2,1)S(1)}, bf16[2,256,512]{2,1,0:T(8,128)(2,1)S(1)}, u32[]{:S(2)}, u32[]{:S(2)}) collective-permute-start(bf16[2,256,512]{2,1,0:T(8,128)(2,1)S(1)} %get-tuple-element.80), channel_id=1, source_target_pairs={{0,1},{1,0},{2,3},{3,2},{4,5},{5,4},{6,7},{7,6},{8,9},{9,8},{10,11... | collective-permute-start | bytes 1572872 | tf_op jit(solution)/shard_map/ppermute | solution.py:357
  52.4 6.8 %collective-permute-start.17 = (bf16[256,512]{1,0:T(8,128)(2,1)S(1)}, bf16[256,512]{1,0:T(8,128)(2,1)S(1)}, u32[]{:S(2)}, u32[]{:S(2)}) collective-permute-start(bf16[256,512]{1,0:T(8,128)(2,1)S(1)} %get-tuple-element.84), channel_id=1, source_target_pairs={{1,2},{3,4},{5,6},{7,8},{9,10},{11,12},{13,14},{15,16},{17,18},{19... | collective-permute-start | bytes 786440 | tf_op jit(solution)/shard_map/ppermute | solution.py:362
  59.0 4.2 %collective-permute-start.18 = (bf16[1,2,16,512]{3,2,1,0:T(8,128)(2,1)S(1)}, bf16[1,2,16,512]{3,2,1,0:T(8,128)(2,1)S(1)}, u32[]{:S(2)}, u32[]{:S(2)}) collective-permute-start(bf16[1,2,16,512]{3,2,1,0:T(8,128)(2,1)S(1)} %slice.134), channel_id=1, source_target_pairs={{0,8},{1,9},{2,10},{3,11},{4,12},{5,13},{6,14},{7,15},{8,0},{9,1},... | collective-permute-start | bytes 98312 | tf_op jit(solution)/shard_map/ppermute | solution.py:357
  63.5 0.8 %copy-start = (f32[256,512]{1,0:T(8,128)}, f32[256,512]{1,0:T(8,128)S(1)}, u32[]{:S(2)}) copy-start(f32[256,512]{1,0:T(8,128)S(1)} %get-tuple-element.91) | copy-start | bytes 1572868
  63.5 1.0 %copy-start.1 = (f32[256,512]{1,0:T(8,128)}, f32[256,512]{1,0:T(8,128)S(1)}, u32[]{:S(2)}) copy-start(f32[256,512]{1,0:T(8,128)S(1)} %get-tuple-element.92) | copy-start | bytes 1572868
